TPU v7x, 128 devices: a whole 4x4x4 slice. The times are simulated.
128 devices in a mesh: chan: 64 (over x, z_hi, y, core), tm: 2 (over z_lo).
Axes of the slice: x: 4, y: 4, z: 4 (z_hi: 2, z_lo: 2; z = z_hi * 2 + z_lo), core: 2. Of those that a mesh axis runs over, the one named last changes fastest.
Arguments:
- spectra: bfloat16 [2, 64, 10240, 2, 384], P('tm', 'chan'), as said below
- mask: int32 [2, 64, 10240], P('tm', 'chan'), may hold values from 0 to 1, as said below
Outputs:
- correlations: float32 [8, 10240, 3001], P('tm', 'chan')
Inputs may be any that keep to these rules, and one draw needn't show every extreme that they name: `spectra`: spectra of the windows, of scales that vary over bins and over channels. `mask`: in every window, among the 160 channels of one block (channels b * 160 to (b + 1) * 160 - 1) at most 120 flags are 1.
All inputs are finite; a program needn't handle non-finite values.
Results may differ from a plain program's by a relative error of at most 0.004.
Values may be sent and summed in bfloat16 or wider, within the bound.
No kernel may reach another device: no remote copies, remote signals or barrier semaphores. Data moves between devices by JAX's collectives and lax.ppermute only.
A program may use at most 192 MiB of HBM per device.

v0:
```python
import math

import jax
import jax.numpy as jnp
from jax import lax
from jax.sharding import PartitionSpec as P

CH = 10240
F = 384
F0 = 12
NFFT = 6000
MAXLAG = 1500
SB = 4
STEPS = 2
LAGS = 3001


def spread(x, axis, root):
    mine = lax.axis_index(axis) == root
    return lax.psum(jnp.where(mine, x, jnp.zeros_like(x)), axis)


def lag_table():
    bin_index = F0 + jnp.arange(F, dtype=jnp.int32)
    lag_index = jnp.arange(LAGS, dtype=jnp.int32) - MAXLAG
    phase_steps = jnp.mod(bin_index[:, None] * lag_index[None, :], NFFT)
    angles = phase_steps.astype(jnp.float32) * jnp.float32(2.0 * math.pi / NFFT)
    return jnp.concatenate([jnp.cos(angles), -jnp.sin(angles)], axis=0)


def whiten(window_spec, kept_mask):
    values = window_spec.astype(jnp.float32)
    energy = jnp.sum(values * values, axis=(-2, -1)) / F
    factor = lax.rsqrt(energy + 1e-06) * kept_mask.astype(jnp.float32)
    return (values * factor[..., None, None]).astype(jnp.bfloat16)


def to_lags(cross_sum, block_width, lag_matrix):
    sources = cross_sum.shape[0]
    flat_cross = cross_sum.reshape(sources * block_width, 2 * F)
    lagged = jnp.dot(
        flat_cross, lag_matrix, precision=lax.Precision.HIGHEST, preferred_element_type=jnp.float32
    )
    return lagged.reshape(sources, block_width, LAGS)


def local(spectra, mask):
    blocks = lax.axis_size("chan")
    block_width = CH // blocks
    win_local = spectra.shape[1]
    whitened = whiten(spectra[0], mask[0])
    by_owner = whitened.reshape(win_local, blocks, block_width, 2, F)
    owner_mask = mask[0].reshape(win_local, blocks, block_width)
    got_rows, got_flags = (
        lax.all_to_all(by_owner, "chan", split_axis=1, concat_axis=0, tiled=True),
        lax.all_to_all(owner_mask, "chan", split_axis=1, concat_axis=0, tiled=True),
    )
    received = got_rows[:, 0]
    receiver_keep = got_flags[:, 0].astype(jnp.float32)
    stride = blocks // STEPS
    row_pieces = []
    keep_pieces = []
    for block in range(STEPS):
        got_block, got_keep = (
            spread(received[:, :SB], "chan", block * stride),
            spread(receiver_keep[:, :SB].astype(jnp.bfloat16), "chan", block * stride),
        )
        row_pieces.append(got_block)
        keep_pieces.append(got_keep)
    source_rows = jnp.concatenate(row_pieces, axis=1)
    source_keep = jnp.concatenate(keep_pieces, axis=1)
    products = jnp.einsum(
        "wqaj,wcbj->qcabj", source_rows, received, preferred_element_type=jnp.float32
    )
    real_part = products[:, :, 0, 0] + products[:, :, 1, 1]
    imag_part = products[:, :, 1, 0] - products[:, :, 0, 1]
    cross_sum = jnp.stack([real_part, imag_part], axis=2)
    pair_count = jnp.einsum("wq,wc->qc", source_keep.astype(jnp.float32), receiver_keep)
    lag_matrix = lag_table()
    lagged_all = to_lags(cross_sum, block_width, lag_matrix)
    lagged, count_part = (
        lax.psum_scatter(lagged_all, "tm", scatter_dimension=0, tiled=True),
        lax.psum_scatter(pair_count, "tm", scatter_dimension=0, tiled=True),
    )
    return lagged / jnp.maximum(count_part, 1.0)[:, :, None]


def solution(mesh):
    placed = (P("tm", "chan", None, None, None), P("tm", "chan", None))
    return jax.shard_map(
        local, mesh=mesh, in_specs=placed, out_specs=P("tm", "chan", None), check_vma=False
    )
```

profile of v0, /device:TPU:0, one launch (start us, length us, event | category | flops | bytes accessed | tf_op | source)
XLA Modules:
  0.0 1561.5 jit_solution(18425485674048573974)
XLA Ops:
  6.5 0.0 copy-start
  6.5 18.4 %copy_convert_fusion = f32[1,1,10240,2,384]{4,2,3,1,0:T(8,128)} fusion(bf16[1,1,10240,2,384]{4,3,2,1,0:T(2,128)(2,1)} %param.2), kind=kLoop, calls=%fused_computation.2 | loop fusion | flops 7864320 | bytes 47185920 | tf_op jit(solution)/shard_map/convert_element_type | solution.py:32
  25.0 3.1 copy-done
  28.1 0.0 copy-start.1
  28.1 3.8 multiply_reduce_fusion
  31.9 0.1 rsqrt.13
  32.0 0.0 copy-done.1
  32.0 0.1 convert_reduce_fusion
  32.1 0.1 convert_element_type.67
  32.2 11.8 multiply_convert_fusion
  44.0 7.0 copy.16
  51.0 11.6 all-to-all-start
  62.6 0.0 all-reduce.5.cloned.1.call-start
  62.7 204.4 %all-to-all-done = bf16[1,64,160,2,384]{4,2,3,0,1:T(8,128)(2,1)} async-done(((bf16[1,64,160,2,384]{4,2,3,0,1:T(8,128)(2,1)}), bf16[1,64,160,2,384]{4,2,3,0,1:T(8,128)(2,1)}, u32[]{:S(2)}, u32[]{:S(2)}) %all-to-all-start) | async-done | bytes 15728672 | tf_op jit(solution)/shard_map/all_to_all | solution.py:55
  267.1 53.1 %copy.17 = bf16[1,64,160,2,384]{1,2,3,4,0:T(8,128)(2,1)} copy(bf16[1,64,160,2,384]{4,2,3,0,1:T(8,128)(2,1)} %all-to-all-done) | data formatting | bytes 31457280 | tf_op jit(solution)/shard_map/all_to_all | solution.py:55
  320.1 3.1 broadcast_select_fusion.1
  323.3 0.0 all-reduce.5.cloned.1.call-update
  323.3 0.2 reduce-scatter.2.cloned.1.call-start
  323.5 20.7 %fusion.8 = (f32[384,3001]{0,1:T(8,128)}, f32[384,3001]{0,1:T(8,128)}) fusion(s32[3001]{0:T(1024)S(1)} %iota_add_fusion, s32[384]{0:T(512)S(1)} %iota_add_fusion.1), kind=kLoop, calls=%fused_computation.16 | loop fusion | flops 11523840 | bytes 9232612 | tf_op jit(solution)/shard_map/cos | solution.py:28
  344.2 53.1 %copy.24 = bf16[64,160,2,384,1]{0,1,4,2,3:T(8,128)(2,1)} copy(bf16[64,160,2,384,1]{3,1,2,0,4:T(8,128)(2,1)} %bitcast.3) | data formatting | bytes 31457280 | tf_op jit(solution)/shard_map/squeeze | solution.py:58
  397.3 584.3 %all-reduce.5.cloned.1.call-done = (bf16[64,4,2,384]{0,1,2,3:T(4,128)(2,1)}, bf16[64,4,2,384]{0,1,2,3:T(4,128)(2,1)}) async-done(((bf16[64,4,2,384]{0,1,2,3:T(4,128)(2,1)}, bf16[64,4,2,384]{0,1,2,3:T(4,128)(2,1)}), (bf16[64,4,2,384]{0,1,2,3:T(4,128)(2,1)}, bf16[64,4,2,384]{0,1,2,3:T(4,128)(2,1)})) %all-reduce.5.cloned.1.call-update) | async-done | bytes 786448 | tf_op jit(solution)/shard_map/psum | solution.py:20
  981.5 22.7 %convolution_bitcast_fusion = f32[8,160,2,2,384]{1,0,2,3,4:T(8,128)} fusion(bf16[64,160,2,384,1]{0,1,4,2,3:T(8,128)(2,1)} %copy.24, bf16[64,4,2,384]{0,1,2,3:T(4,128)(2,1)} %get-tuple-element.7, bf16[64,4,2,384]{0,1,2,3:T(4,128)(2,1)} %get-tuple-element.8), kind=kOutput, calls=%fused_computation.18 | convolution fusion | flops 253231104 | bytes 24379392 | tf_op jit(solution)/shard_map/wqaj,wcbj->qcabj/dot_general | solution.py:72
  1004.2 3.3 fusion.10
  1007.5 0.0 slice-start
  1007.5 0.0 slice-start.2
  1007.5 3.4 fusion.12
  1011.0 0.0 slice-start.1
  1011.0 0.0 slice-start.3
  1011.0 0.4 pad_maximum_fusion
  1011.4 0.2 slice-done
  1011.6 1.3 slice-done.2
  1012.9 0.2 slice-done.1
  1013.1 0.1 slice-done.3
  1013.2 179.1 %fusion = f32[8,160,3001]{2,1,0:T(8,128)} fusion(f32[384,3001]{0,1:T(8,128)S(1)} %bitcast.42, f32[384,3001]{0,1:T(8,128)S(1)} %bitcast.40, f32[8,160,768]{1,0,2:T(8,128)S(1)} %bitcast.38), kind=kOutput, calls=%fused_computation.4 | convolution fusion | flops 35403542528 | bytes 28516352 | tf_op jit(solution)/shard_map/dot_general | solution.py:41
  1192.3 0.0 copy-start.2
  1192.3 0.0 reduce-scatter.2.cloned.1.call-update
  1192.3 0.5 broadcast.61
  1192.8 0.7 reduce.9
  1193.6 0.8 reshape_squeeze.3
  1194.3 9.7 all-to-all-start.1
  1204.0 0.0 copy-done.2
  1204.0 0.6 dynamic-slice
  1205.3 8.2 all-to-all-done.1
  1213.6 327.7 %all-reduce.1 = (bf16[64,4]{1,0:T(8,128)(2,1)S(1)}, bf16[64,4]{1,0:T(8,128)(2,1)S(1)}) all-reduce(bf16[64,4]{1,0:T(8,128)(2,1)S(1)} %get-tuple-element.12, bf16[64,4]{1,0:T(8,128)(2,1)S(1)} %get-tuple-element.11), channel_id=1, replica_groups=mesh['chan'=64,'tm'=2] {'chan'}, use_global_device_ids=true, to_apply=%region_5.6 | all-reduce | flops 512 | bytes 2048 | tf_op jit(solution)/shard_map/psum | solution.py:20
  1541.3 0.1 copy.22
  1541.4 0.1 copy.23
  1541.5 0.1 fusion.15
  1541.6 5.0 all-reduce
  1546.6 0.0 reduce-scatter.2.cloned.1.call-done
  1546.6 7.7 broadcast_divide_fusion
  (10 shorter events, 0.1 us)
Async XLA Ops:
  6.5 21.6 %copy-start = (bf16[1,1,10240,2,384]{4,3,2,1,0:T(2,128)(2,1)S(1)}, bf16[1,1,10240,2,384]{4,3,2,1,0:T(2,128)(2,1)}, u32[]{:S(2)}) copy-start(bf16[1,1,10240,2,384]{4,3,2,1,0:T(2,128)(2,1)} %param.2) | copy-start | bytes 47185924
  28.1 3.9 copy-start.1
  51.0 216.1 %all-to-all-start = ((bf16[1,64,160,2,384]{4,2,3,0,1:T(8,128)(2,1)}), bf16[1,64,160,2,384]{4,2,3,0,1:T(8,128)(2,1)}, u32[]{:S(2)}, u32[]{:S(2)}) async-start(bf16[1,64,160,2,384]{4,2,3,0,1:T(8,128)(2,1)} %copy.16), calls=%async_computation | async-start | bytes 31457280 | tf_op jit(solution)/shard_map/all_to_all | solution.py:55
  62.6 919.0 %all-reduce.5.cloned.1.call-start = ((), (), s32[]{:S(2)}) async-start(), calls=%async_computation.4 | async-start | bytes 3145728 | tf_op jit(solution)/shard_map/psum | solution.py:20
  323.3 1223.3 %reduce-scatter.2.cloned.1.call-start = ((), (), s32[]{:S(2)}) async-start(), calls=%async_computation.3 | async-start | bytes 23592960 | tf_op jit(solution)/shard_map/reduce_scatter | solution.py:82
  1007.5 4.1 slice-start
  1007.5 5.3 slice-start.2
  1011.0 2.1 slice-start.1
  1011.0 2.2 slice-start.3
  1192.3 11.8 copy-start.2
  1194.3 19.2 %all-to-all-start.1 = ((s32[1,64,160]{2,0,1:T(1,128)}), s32[1,64,160]{2,0,1:T(1,128)S(1)}, u32[]{:S(2)}, u32[]{:S(2)}) async-start(s32[1,64,160]{2,0,1:T(1,128)} %reshape_squeeze.3), calls=%async_computation.2 | async-start | bytes 131072 | tf_op jit(solution)/shard_map/all_to_all | solution.py:56
Sparse Core Ops, SparseCore 0:
  323.4 658.0 all-reduce.4
  1192.4 183.9 reduce-scatter.1
where the time goes:
time: 1570 us; the launch traced here: 1560 us
  waiting for transfers between devices  797 us (51%)
  blocking collectives  333 us (21%)
  matrix products  202 us (13%)
  local copies, waits for them, and re-layouts  120 us (8%)
  other arithmetic  73.6 us (5%)
  starting transfers between devices  21.5 us (1%)
    psum x1, waiting for transfers between devices, spread(): return lax.psum(jnp.where(mine, x, jnp.zeros_like(x)), axis)  584 us
    psum x1, blocking collectives, spread(): return lax.psum(jnp.where(mine, x, jnp.zeros_like(x)), axis)  328 us
    all_to_all x1, waiting for transfers between devices, local(): lax.all_to_all(by_owner, 'chan', split_axis=1, concat_axis=0, tiled=True)  204 us
    dot_general x1, matrix products, to_lags(): jnp.dot(flat_cross, lag_matrix, precision=lax.Precision.HIGHEST, preferre...  179 us
    all_to_all x1, local copies, waits for them, and re-layouts, local(): lax.all_to_all(by_owner, 'chan', split_axis=1, concat_axis=0, tiled=True)  53.1 us
    squeeze x1, local copies, waits for them, and re-layouts, local(): received = got_rows[:, 0]  53.1 us
  transfers between devices with their start and end apart: 4, of which 3 were waited for; matrix products, arithmetic and copies ran while one was open for 5% of the time, Pallas kernels for 0%

commit v1 on v0

v1 whole, which is shorter than its diff:
```python
import functools
import math

import jax
import jax.numpy as jnp
from jax import lax
from jax.experimental import pallas as pl
from jax.experimental.pallas import tpu as pltpu
from jax.sharding import PartitionSpec as P

CH = 10240
F = 384
F0 = 12
NFFT = 6000
MAXLAG = 1500
SB = 4
SRC = 8
LAGS = 3001
BLOCKS = 64
WIDE = 160
WINS = 64
SLOTS = 128
ROWS = 2 * SLOTS
BINS_A = 256
BINS_B = 128
STEP = 8
LAG_TILE = 512


def iota(shape, dim):
    return lax.broadcasted_iota(jnp.int32, shape, dim)


def one_hot(where):
    return jnp.where(where, 1.0, 0.0).astype(jnp.bfloat16)


def dot(a, b):
    return jnp.dot(a, b, preferred_element_type=jnp.float32)


def pack_kernel(tm_ref, mask_ref, x0, x1, x2, a0, a1, a2, b0, b1, b2, send_a, send_b, slot_ref, key_ref, src_ref, srcflag_ref):
    block = pl.program_id(0)

    @pl.when(block == 0)
    def _():
        flags = mask_ref[...].astype(jnp.float32).astype(jnp.bfloat16)
        lane = iota((WIDE, 2 * WIDE), 1)
        row = iota((WIDE, 2 * WIDE), 0)
        before = dot(flags, one_hot(row < lane // 2)).astype(jnp.int32)
        kept = dot(flags, one_hot(row == lane // 2))
        part = iota((BLOCKS, 2 * WIDE), 1) % 2
        slot_ref[...] = jnp.where(kept > 0.5, before + part * SLOTS, -1)
        lane = iota((WIDE, BINS_A), 1)
        row = iota((WIDE, BINS_A), 0)
        before = dot(flags, one_hot(row < lane))
        key_ref[...] = jnp.where(dot(flags, one_hot(row == lane)) > 0.5, before, -1.0)
        shift = SB * (1 - tm_ref[0])
        source = (lane + shift) % SRC
        first = dot(flags, one_hot((row == source % SB) & (source < SB) & (lane < SRC)))
        second = dot(flags, one_hot((row == source % SB) & (source >= SB) & (lane < SRC)))
        middle = BLOCKS // 2
        srcflag_ref[...] = first[0:1] + second[middle : middle + 1]
        take = iota((2 * SRC, 16), 0)
        lane = iota((2 * SRC, 16), 1)
        source = (take % SRC + shift) % SRC
        hit = lane == 2 * (source % SB) + take // SRC
        pick_a = one_hot(hit & (source < SB) & (kept[0:1, :16] > 0.5))
        pick_b = one_hot(hit & (source >= SB) & (kept[middle : middle + 1, :16] > 0.5))
        rows = [
            dot(pick_a, ra.reshape(16, 128)[...]) + dot(pick_b, rb.reshape(16, 128)[...])
            for ra, rb in ((a0, b0), (a1, b1), (a2, b2))
        ]
        squares = sum(r * r for r in rows)
        energy = jnp.sum(squares[:SRC] + squares[SRC:], axis=1, keepdims=True) / F
        factor = lax.rsqrt(energy + 1e-06)
        for k, r in enumerate(rows):
            src_ref[:SRC, k * 128 : (k + 1) * 128] = r[:SRC] * factor
            src_ref[SRC:, k * 128 : (k + 1) * 128] = r[SRC:] * factor

    slot = slot_ref[pl.ds(block, 1), :]
    pick = one_hot(iota((ROWS, 2 * WIDE), 0) == slot)
    band = jnp.concatenate([r.reshape(2 * WIDE, 128)[...] for r in (x0, x1, x2)], axis=1)
    rows = dot(pick, band)
    real, imag = rows[:SLOTS], rows[SLOTS:]
    energy = jnp.sum(real * real + imag * imag, axis=1, keepdims=True) / F
    factor = lax.rsqrt(energy + 1e-06)
    real = (real * factor).astype(jnp.bfloat16)
    imag = (imag * factor).astype(jnp.bfloat16)
    src = src_ref[...].astype(jnp.bfloat16)
    for out, lo, hi in ((send_a, 0, BINS_A), (send_b, BINS_A, F)):
        out[0, :SLOTS] = real[:, lo:hi]
        out[0, SLOTS:ROWS] = imag[:, lo:hi]
        out[0, SLOTS - SRC : SLOTS] = src[:SRC, lo:hi]
        out[0, ROWS - SRC : ROWS] = src[SRC:, lo:hi]
    line = iota((8, BINS_A), 0)
    notes = jnp.where(line == 0, key_ref[pl.ds(block, 1), :], jnp.where(line == 1, srcflag_ref[...], 0.0))
    send_a[0, ROWS : ROWS + 8] = notes.astype(jnp.bfloat16)


def pack(tm_index, mask, spectra):
    whole = lambda k: pl.BlockSpec((WIDE, 2, 128), lambda b: (b, 0, k))
    head = lambda k, at: pl.BlockSpec((8, 2, 128), lambda b: (at, 0, k))
    middle = BLOCKS // 2 * WIDE // 8
    return pl.pallas_call(
        pack_kernel,
        grid=(BLOCKS,),
        in_specs=[
            pl.BlockSpec(memory_space=pltpu.SMEM),
            pl.BlockSpec((BLOCKS, WIDE), lambda b: (0, 0)),
            *[whole(k) for k in range(3)],
            *[head(k, 0) for k in range(3)],
            *[head(k, middle) for k in range(3)],
        ],
        out_specs=[
            pl.BlockSpec((1, ROWS + 8, BINS_A), lambda b: (b, 0, 0)),
            pl.BlockSpec((1, ROWS, BINS_B), lambda b: (b, 0, 0)),
        ],
        out_shape=[
            jax.ShapeDtypeStruct((BLOCKS, ROWS + 8, BINS_A), jnp.bfloat16),
            jax.ShapeDtypeStruct((BLOCKS, ROWS, BINS_B), jnp.bfloat16),
        ],
        scratch_shapes=[
            pltpu.VMEM((BLOCKS, 2 * WIDE), jnp.int32),
            pltpu.VMEM((BLOCKS, BINS_A), jnp.float32),
            pltpu.VMEM((2 * SRC, F), jnp.float32),
            pltpu.VMEM((1, BINS_A), jnp.float32),
        ],
        cost_estimate=pl.CostEstimate(flops=2 * BLOCKS * ROWS * 2 * WIDE * F, bytes_accessed=30_000_000, transcendentals=0),
        compiler_params=pltpu.CompilerParams(vmem_limit_bytes=32 << 20),
        name="whiten_pack",
    )(tm_index, mask, *[spectra] * 9)


def spread_slots(got, pick, held, src, win, bins):
    held[win, :, :bins] = dot(pick, got[win, :SLOTS, :])
    held[win, :, bins:] = dot(pick, got[win, SLOTS:ROWS, :])
    src[win, :SRC] = got[win, SLOTS - SRC : SLOTS, :].astype(jnp.float32)
    src[win, SRC:] = got[win, ROWS - SRC : ROWS, :].astype(jnp.float32)


def correlate(held, src, outs, bins):
    def group(i, _):
        rows = pl.ds(pl.multiple_of(i * 8, 8), 8)
        for t in range(0, bins, 128):
            re_at, im_at = slice(t, t + 128), slice(bins + t, bins + t + 128)
            sums = [[ref[q, rows, re_at], ref[q, rows, im_at]] for ref, _ in outs for q in range(SB)]
            for win in range(STEP):
                b0, b1 = held[win, rows, re_at], held[win, rows, im_at]
                for n, q in enumerate([first + k for _, first in outs for k in range(SB)]):
                    a0 = jnp.broadcast_to(src[win, q : q + 1, re_at], (8, 128))
                    a1 = jnp.broadcast_to(src[win, SRC + q : SRC + q + 1, re_at], (8, 128))
                    sums[n][0] += a0 * b0 + a1 * b1
                    sums[n][1] += a1 * b0 - a0 * b1
            n = 0
            for ref, _ in outs:
                for q in range(SB):
                    ref[q, rows, re_at], ref[q, rows, im_at] = sums[n]
                    n += 1
        return 0

    lax.fori_loop(0, WIDE // 8, group, 0)


def first_kernel(got, theirs, mine, picks, count, held, src):
    @pl.when(pl.program_id(0) == 0)
    def _():
        theirs[...] = jnp.zeros_like(theirs)
        mine[...] = jnp.zeros_like(mine)
        count[...] = jnp.zeros_like(count)

    for win in range(STEP):
        notes = got[win, ROWS : ROWS + 8, :].astype(jnp.float32)
        key = jnp.transpose(notes)[:WIDE, 0:1]
        pick = one_hot(iota((WIDE, SLOTS), 1) == key.astype(jnp.int32))
        picks[win] = pick
        count[...] += jnp.where(key > -0.5, 1.0, 0.0) * notes[1:2, :128]
        spread_slots(got, pick, held, src, win, BINS_A)
    correlate(held, src, ((theirs, 0), (mine, SB)), BINS_A)


def first_sums(got):
    sums = jax.ShapeDtypeStruct((SB, WIDE, 2 * BINS_A), jnp.float32)
    sums_spec = pl.BlockSpec(sums.shape, lambda g: (0, 0, 0))
    return pl.pallas_call(
        first_kernel,
        grid=(WINS // STEP,),
        in_specs=[pl.BlockSpec((STEP, ROWS + 8, BINS_A), lambda g: (g, 0, 0))],
        out_specs=[
            sums_spec,
            sums_spec,
            pl.BlockSpec((STEP, WIDE, SLOTS), lambda g: (g, 0, 0)),
            pl.BlockSpec((WIDE, 128), lambda g: (0, 0)),
        ],
        out_shape=[
            sums,
            sums,
            jax.ShapeDtypeStruct((WINS, WIDE, SLOTS), jnp.bfloat16),
            jax.ShapeDtypeStruct((WIDE, 128), jnp.float32),
        ],
        scratch_shapes=[
            pltpu.VMEM((STEP, WIDE, 2 * BINS_A), jnp.float32),
            pltpu.VMEM((STEP, 2 * SRC, BINS_A), jnp.float32),
        ],
        cost_estimate=pl.CostEstimate(flops=30_000_000_000, bytes_accessed=20_000_000, transcendentals=0),
        compiler_params=pltpu.CompilerParams(vmem_limit_bytes=32 << 20),
        name="cross_sums_first",
    )(got)


def second_kernel(first, got, picks, out, held, src):
    @pl.when(pl.program_id(0) == 0)
    def _():
        out[...] = jnp.zeros_like(out)

    for win in range(STEP):
        spread_slots(got, picks[win], held, src, win, BINS_B)
    correlate(held, src, ((out, first),), BINS_B)


def second_sums(got, picks, first):
    sums = jax.ShapeDtypeStruct((SB, WIDE, 2 * BINS_B), jnp.float32)
    return pl.pallas_call(
        functools.partial(second_kernel, first),
        grid=(WINS // STEP,),
        in_specs=[
            pl.BlockSpec((STEP, ROWS, BINS_B), lambda g: (g, 0, 0)),
            pl.BlockSpec((STEP, WIDE, SLOTS), lambda g: (g, 0, 0)),
        ],
        out_specs=pl.BlockSpec(sums.shape, lambda g: (0, 0, 0)),
        out_shape=sums,
        scratch_shapes=[
            pltpu.VMEM((STEP, WIDE, 2 * BINS_B), jnp.float32),
            pltpu.VMEM((STEP, 2 * SRC, BINS_B), jnp.float32),
        ],
        cost_estimate=pl.CostEstimate(flops=8_000_000_000, bytes_accessed=8_000_000, transcendentals=0),
        compiler_params=pltpu.CompilerParams(vmem_limit_bytes=32 << 20),
        name="cross_sums_second",
    )(got, picks)


def split(x):
    high = x.astype(jnp.bfloat16)
    return high, (x - high.astype(jnp.float32)).astype(jnp.bfloat16)


def three_dots(high, low, table_high, table_low):
    t = table_high[...]
    return dot(high[...], t) + (dot(low[...], t) + dot(high[...], table_low[...]))


def load_sums(mine, theirs, high, low):
    total = mine[...] + theirs[...]
    h, rest = split(total)
    high[...] = h
    low[...] = rest


def lags_first_kernel(mine, theirs, table_high, table_low, out, high, low):
    @pl.when(pl.program_id(0) == 0)
    def _():
        load_sums(mine, theirs, high, low)

    out[...] = three_dots(high, low, table_high, table_low)


def lags_last_kernel(mine, theirs, table_high, table_low, before, count, count_theirs, out, high, low, scale):
    @pl.when(pl.program_id(0) == 0)
    def _():
        load_sums(mine, theirs, high, low)
        for q in range(SB):
            pairs = count[:, SB + q : SB + q + 1] + count_theirs[:, q : q + 1]
            scale[q * WIDE : (q + 1) * WIDE] = jnp.broadcast_to(1.0 / jnp.maximum(pairs, 1.0), (WIDE, 128))

    out[...] = (before[...] + three_dots(high, low, table_high, table_low)) * scale[:, 0:1]


def to_lags(mine, theirs, tables, before=None, counts=()):
    rows, depth = SB * WIDE, tables[0].shape[0]
    tile = pl.BlockSpec((rows, LAG_TILE), lambda n: (0, n))
    full = lambda shape: pl.BlockSpec(shape, lambda n: (0, 0))
    table = pl.BlockSpec((depth, LAG_TILE), lambda n: (0, n))
    last = before is not None
    return pl.pallas_call(
        lags_last_kernel if last else lags_first_kernel,
        grid=(pl.cdiv(LAGS, LAG_TILE),),
        in_specs=[full((rows, depth)), full((rows, depth)), table, table]
        + ([tile, full((WIDE, 128)), full((WIDE, 128))] if last else []),
        out_specs=tile,
        out_shape=jax.ShapeDtypeStruct((rows, LAGS), jnp.float32),
        scratch_shapes=[pltpu.VMEM((rows, depth), jnp.bfloat16)] * 2
        + ([pltpu.VMEM((rows, 128), jnp.float32)] if last else []),
        cost_estimate=pl.CostEstimate(flops=6 * rows * depth * LAGS, bytes_accessed=4 * rows * LAGS * (2 if last else 1), transcendentals=0),
        compiler_params=pltpu.CompilerParams(vmem_limit_bytes=32 << 20),
        name="to_lags_last" if last else "to_lags_first",
    )(
        mine.reshape(rows, depth),
        theirs.reshape(rows, depth),
        *tables,
        *((before, *counts) if last else ()),
    )


def lag_table(first_bin, bins, zero):
    bin_index = F0 + first_bin + zero + jnp.arange(bins, dtype=jnp.int32)
    lag_index = jnp.arange(LAGS, dtype=jnp.int32) - MAXLAG
    phase_steps = jnp.mod(bin_index[:, None] * lag_index[None, :], NFFT)
    angles = phase_steps.astype(jnp.float32) * jnp.float32(2.0 * math.pi / NFFT)
    table = jnp.concatenate([jnp.cos(angles), -jnp.sin(angles)], axis=0)
    high = lax.reduce_precision(table, 8, 7)
    return high.astype(jnp.bfloat16), (table - high).astype(jnp.bfloat16)


def swap(x):
    return lax.ppermute(x, "tm", [(0, 1), (1, 0)])


def local(spectra, mask):
    tm_index = lax.axis_index("tm").astype(jnp.int32)[None]
    send_a, send_b = pack(tm_index, mask.reshape(BLOCKS, WIDE), spectra.reshape(CH, 2, F))
    send_a, send_b, zero = lax.optimization_barrier((send_a, send_b, jnp.int32(0)))
    exchange = lambda x: lax.all_to_all(x, "chan", split_axis=0, concat_axis=0, tiled=True)
    got_a = exchange(send_a)
    got_b = exchange(send_b)
    tables_a = lag_table(0, BINS_A, zero)
    tables_b = lag_table(BINS_A, BINS_B, zero)
    theirs_a, mine_a, picks, count = first_sums(got_a)
    from_a = swap(theirs_a)
    count_from = swap(count)
    theirs_b = second_sums(got_b, picks, 0)
    from_b = swap(theirs_b)
    mine_b = second_sums(got_b, picks, SB)
    lagged = to_lags(mine_a, from_a, tables_a)
    lagged = to_lags(mine_b, from_b, tables_b, lagged, (count, count_from))
    return lagged.reshape(SB, WIDE, LAGS)


def solution(mesh):
    placed = (P("tm", "chan", None, None, None), P("tm", "chan", None))
    return jax.shard_map(
        local, mesh=mesh, in_specs=placed, out_specs=P("tm", "chan", None), check_vma=False
    )
```

time: 1570 us -> 291 us (0.19)
  waiting for transfers between devices: 797 us -> 111 us
  blocking collectives: 333 us -> 0 us
  matrix products: 202 us -> 0 us
  Pallas kernels: 0 us -> 118 us
  local copies, waits for them, and re-layouts: 120 us -> 10.3 us
  other arithmetic: 73.6 us -> 25.3 us
    psum x1 -> x0, waiting for transfers between devices: 584 us -> none  [spread(): return lax.psum(jnp.where(mine, x, jnp.zeros_like(x)), axis)]
    psum x1 -> x0, blocking collectives: 328 us -> none  [spread(): return lax.psum(jnp.where(mine, x, jnp.zeros_like(x)), axis)]
    dot_general x3 -> x0, matrix products: 202 us -> none  [the longest x1 179 us: to_lags(): jnp.dot(flat_cross, lag_matrix, precision=lax.Precision.HIGHEST, preferre...]
    pallas_call x0 -> x6, Pallas kernels: none -> 118 us  [the longest x1 47.2 us: pack(): pl.pallas_call(pack_kernel, grid=(BLOCKS,), in_specs=[pl.BlockSpec(memory...]
    all_to_all x2, waiting for transfers between devices: 213 us -> 102 us  [local(): lax.all_to_all(x, 'chan', split_axis=0, concat_axis=0, tiled=True)]
    all_to_all x1 -> x0, local copies, waits for them, and re-layouts: 53.1 us -> none  [local(): lax.all_to_all(by_owner, 'chan', split_axis=1, concat_axis=0, tiled=True)]
    squeeze x1 -> x0, local copies, waits for them, and re-layouts: 53.1 us -> none  [local(): received = got_rows[:, 0]]
    convert_element_type x4 -> x2, other arithmetic: 30.4 us -> 4.51 us  [lag_table(): return (high.astype(jnp.bfloat16), (table - high).astype(jnp.bfloat16))]
  transfers between devices with their start and end apart: 4 -> 5, of which waited for: 3 -> 4; matrix products, arithmetic and copies ran while one was open for 5% -> 8% of each run, Pallas kernels for 0% -> 22%
where the time goes in v1:
time: 291 us; the launch traced here: 289 us
  Pallas kernels  118 us (41%)
  waiting for transfers between devices  111 us (38%)
  other arithmetic  25.3 us (9%)
  starting transfers between devices  24.6 us (8%)
  local copies, waits for them, and re-layouts  10.3 us (4%)
    all_to_all x2, waiting for transfers between devices, local(): lax.all_to_all(x, 'chan', split_axis=0, concat_axis=0, tiled=True)  102 us
    pallas_call x1, Pallas kernels, pack(): pl.pallas_call(pack_kernel, grid=(BLOCKS,), in_specs=[pl.BlockSpec(memory...  47.2 us
    pallas_call x1, Pallas kernels, first_sums(): pl.pallas_call(first_kernel, grid=(WINS // STEP,), in_specs=[pl.BlockSpec...  32.1 us
    pallas_call x2, Pallas kernels, second_sums(): pl.pallas_call(functools.partial(second_kernel, first), grid=(WINS // STE...  22 us
    all_to_all x2, starting transfers between devices, local(): lax.all_to_all(x, 'chan', split_axis=0, concat_axis=0, tiled=True)  21.4 us
    cos x2, other arithmetic, lag_table(): table = jnp.concatenate([jnp.cos(angles), -jnp.sin(angles)], axis=0)  19.3 us
    pallas_call x2, Pallas kernels, to_lags(): pl.pallas_call(lags_last_kernel if last else lags_first_kernel, grid=(pl....  16.5 us
    unnamed x17, local copies, waits for them, and re-layouts  10.2 us
  transfers between devices with their start and end apart: 5, of which 4 were waited for; matrix products, arithmetic and copies ran while one was open for 8% of the time, Pallas kernels for 22%

profile of v1, /device:TPU:0, one launch (start us, length us, event | category | flops | bytes accessed | tf_op | source)
XLA Modules:
  0.0 288.8 jit_solution(15951319073772810301)
XLA Ops:
  0.0 0.6 broadcast.25
  0.6 1.6 reduce.3
  2.2 0.1 reshape.33.mask_ref
  2.2 47.2 %whiten_pack.1 = (bf16[64,264,256]{2,1,0:T(8,128)(2,1)S(1)}, bf16[64,256,128]{2,1,0:T(8,128)(2,1)S(1)}) custom-call(s32[1]{0:T(128)} %bitcast.tm_ref, s32[64,160]{1,0:T(8,128)S(1)} %reshape.33.mask_ref, bf16[10240,2,384]{2,1,0:T(2,128)(2,1)} %bitcast.10, bf16[10240,2,384]{2,1,0:T(2,128)(2,1)} %bitcast.11, bf16[10240,2,384]{2,1,0:T(2,128)(2,1)} %bitcast.12, ...), custom_call_target="tpu_custom_call" | custom-call | flops 4026531840 | bytes 30000000 | tf_op jit(solution)/shard_map/whiten_pack/pallas_call | solution.py:105
  49.5 0.0 copy-start
  49.5 3.3 %copy-done = bf16[64,264,256]{2,1,0:T(8,128)(2,1)} copy-done((bf16[64,264,256]{2,1,0:T(8,128)(2,1)}, bf16[64,264,256]{2,1,0:T(8,128)(2,1)S(1)}, u32[]{:S(2)}) %copy-start) | copy-done | bytes 8650776
  52.8 0.0 copy-start.1
  52.8 2.0 copy-done.1
  54.8 11.6 %all-to-all-start.1 = ((bf16[64,264,256]{2,1,0:T(8,128)(2,1)}), bf16[64,264,256]{2,1,0:T(8,128)(2,1)}, u32[]{:S(2)}, u32[]{:S(2)}) async-start(bf16[64,264,256]{2,1,0:T(8,128)(2,1)} %copy-done), calls=%async_computation.1 | async-start | bytes 17301504 | tf_op jit(solution)/shard_map/all_to_all | solution.py:322
  66.4 6.4 %fusion.12 = (f32[128,3001]{1,0:T(8,128)S(1)}, f32[128,3001]{1,0:T(8,128)S(1)}) fusion(s32[3001]{0:T(1024)S(1)} %iota_add_fusion, s32[128]{0:T(128)S(1)} %iota_add_fusion.2), kind=kLoop, calls=%fused_computation.24 | loop fusion | flops 3841280 | bytes 3085540 | tf_op jit(solution)/shard_map/cos | solution.py:309
  72.8 0.6 fusion.1
  73.4 100.5 %all-to-all-done.1.got = bf16[64,264,256]{2,1,0:T(8,128)(2,1)} async-done(((bf16[64,264,256]{2,1,0:T(8,128)(2,1)}), bf16[64,264,256]{2,1,0:T(8,128)(2,1)}, u32[]{:S(2)}, u32[]{:S(2)}) %all-to-all-start.1) | async-done | bytes 8650784 | tf_op jit(solution)/shard_map/all_to_all | solution.py:322
  173.9 9.9 %all-to-all-start = ((bf16[64,256,128]{2,1,0:T(8,128)(2,1)}), bf16[64,256,128]{2,1,0:T(8,128)(2,1)}, u32[]{:S(2)}, u32[]{:S(2)}) async-start(bf16[64,256,128]{2,1,0:T(8,128)(2,1)} %copy-done.1), calls=%async_computation | async-start | bytes 8388608 | tf_op jit(solution)/shard_map/all_to_all | solution.py:322
  183.8 12.9 %fusion.6 = (f32[256,3001]{1,0:T(8,128)S(1)}, f32[256,3001]{1,0:T(8,128)S(1)}) fusion(s32[3001]{0:T(1024)S(1)} %iota_add_fusion, s32[256]{0:T(256)S(1)} %iota_add_fusion.1), kind=kLoop, calls=%fused_computation.15 | loop fusion | flops 7682560 | bytes 6159076 | tf_op jit(solution)/shard_map/cos | solution.py:309
  196.7 3.9 %fusion = (bf16[512,3001]{1,0:T(8,128)(2,1)}, bf16[512,3001]{1,0:T(8,128)(2,1)}) fusion(f32[256,3001]{1,0:T(8,128)S(1)} %get-tuple-element.28, f32[256,3001]{1,0:T(8,128)S(1)} %get-tuple-element.27), kind=kLoop, calls=%fused_computation.2 | loop fusion | flops 7682560 | bytes 12292096 | tf_op jit(solution)/shard_map/convert_element_type | solution.py:311
  200.6 32.1 %cross_sums_first.1 = (f32[4,160,512]{2,1,0:T(8,128)}, f32[4,160,512]{2,1,0:T(8,128)S(1)}, bf16[64,160,128]{2,1,0:T(8,128)(2,1)S(1)}, f32[160,128]{1,0:T(8,128)S(1)}) custom-call(bf16[64,264,256]{2,1,0:T(8,128)(2,1)} %all-to-all-done.1.got), custom_call_target="tpu_custom_call" | custom-call | flops 30000001024 | bytes 20000000 | tf_op jit(solution)/shard_map/cross_sums_first/pallas_call | solution.py:185
  232.7 0.0 copy-start.4
  232.7 1.1 copy-done.4
  233.8 0.0 copy-start.6
  233.8 1.5 copy-done.6
  235.3 1.0 collective-permute-start.1
  236.3 1.4 all-to-all-done.got
  237.7 0.0 copy-start.7
  237.7 1.7 copy-done.7
  239.5 10.8 %cross_sums_second.3 = f32[4,160,256]{2,1,0:T(8,128)S(1)} custom-call(bf16[64,256,128]{2,1,0:T(8,128)(2,1)} %all-to-all-done.got, bf16[64,160,128]{2,1,0:T(8,128)(2,1)S(1)} %copy-done.7), custom_call_target="tpu_custom_call" | custom-call | flops 8000000000 | bytes 8000000 | tf_op jit(solution)/shard_map/cross_sums_second/pallas_call | solution.py:223
  250.3 1.1 collective-permute-start
  251.4 0.0 copy-start.2
  251.4 0.0 copy-start.3
  251.4 0.0 copy-start.5
  251.4 1.0 collective-permute-start.2
  252.4 11.3 %cross_sums_second.2 = f32[4,160,256]{2,1,0:T(8,128)S(1)} custom-call(bf16[64,256,128]{2,1,0:T(8,128)(2,1)} %all-to-all-done.got, bf16[64,160,128]{2,1,0:T(8,128)(2,1)S(1)} %copy-done.7), custom_call_target="tpu_custom_call" | custom-call | flops 8000000000 | bytes 8000000 | tf_op jit(solution)/shard_map/cross_sums_second/pallas_call | solution.py:223
  263.7 3.6 %collective-permute-done.1 = f32[4,160,512]{2,1,0:T(8,128)} collective-permute-done((f32[4,160,512]{2,1,0:T(8,128)}, f32[4,160,512]{2,1,0:T(8,128)}, u32[]{:S(2)}, u32[]{:S(2)}) %collective-permute-start.1) | collective-permute-done | bytes 1310752 | tf_op jit(solution)/shard_map/ppermute | solution.py:315
  267.3 0.0 copy-done.2
  267.3 0.0 copy-done.3
  267.3 0.0 copy-done.5
  267.3 9.5 %to_lags_first.1.before = f32[640,3001]{1,0:T(8,128)S(1)} custom-call(f32[640,512]{1,0:T(8,128)S(1)} %bitcast.9, f32[640,512]{1,0:T(8,128)} %bitcast.5.theirs, bf16[512,3001]{1,0:T(8,128)(2,1)S(1)} %copy-done.3, bf16[512,3001]{1,0:T(8,128)(2,1)S(1)} %copy-done.2), custom_call_target="tpu_custom_call" | custom-call | flops 5900206080 | bytes 7682560 | tf_op jit(solution)/shard_map/to_lags_first/pallas_call | solution.py:284
  276.9 5.0 %collective-permute-done.2.count_theirs = f32[160,128]{1,0:T(8,128)S(1)} collective-permute-done((f32[160,128]{1,0:T(8,128)S(1)}, f32[160,128]{1,0:T(8,128)S(1)}, u32[]{:S(2)}, u32[]{:S(2)}) %collective-permute-start.2) | collective-permute-done | bytes 81952 | tf_op jit(solution)/shard_map/ppermute | solution.py:315
  281.9 0.0 collective-permute-done
  281.9 6.9 %to_lags_last.1 = f32[640,3001]{1,0:T(8,128)} custom-call(f32[640,256]{1,0:T(8,128)S(1)} %bitcast.8, f32[640,256]{1,0:T(8,128)S(1)} %bitcast.7, bf16[256,3001]{1,0:T(8,128)(2,1)S(1)} %get-tuple-element.26.table_high, bf16[256,3001]{1,0:T(8,128)(2,1)S(1)} %get-tuple-element.25.table_low, f32[640,3001]{1,0:T(8,128)S(1)} %to_lags_first.1.before, ...), custom_call_target="tpu_custom_call" | custom-call | flops 2950103040 | bytes 15365120 | tf_op jit(solution)/shard_map/to_lags_last/pallas_call | solution.py:284
  (3 shorter events, 0.0 us)
Async XLA Ops:
  49.5 3.3 %copy-start = (bf16[64,264,256]{2,1,0:T(8,128)(2,1)}, bf16[64,264,256]{2,1,0:T(8,128)(2,1)S(1)}, u32[]{:S(2)}) copy-start(bf16[64,264,256]{2,1,0:T(8,128)(2,1)S(1)} %get-tuple-element.17) | copy-start | bytes 25952260
  52.8 2.0 copy-start.1
  54.8 119.1 %all-to-all-start.1 = ((bf16[64,264,256]{2,1,0:T(8,128)(2,1)}), bf16[64,264,256]{2,1,0:T(8,128)(2,1)}, u32[]{:S(2)}, u32[]{:S(2)}) async-start(bf16[64,264,256]{2,1,0:T(8,128)(2,1)} %copy-done), calls=%async_computation.1 | async-start | bytes 17301504 | tf_op jit(solution)/shard_map/all_to_all | solution.py:322
  173.9 63.8 %all-to-all-start = ((bf16[64,256,128]{2,1,0:T(8,128)(2,1)}), bf16[64,256,128]{2,1,0:T(8,128)(2,1)}, u32[]{:S(2)}, u32[]{:S(2)}) async-start(bf16[64,256,128]{2,1,0:T(8,128)(2,1)} %copy-done.1), calls=%async_computation | async-start | bytes 8388608 | tf_op jit(solution)/shard_map/all_to_all | solution.py:322
  232.7 1.1 copy-start.4
  233.8 1.5 copy-start.6
  235.3 32.0 %collective-permute-start.1 = (f32[4,160,512]{2,1,0:T(8,128)}, f32[4,160,512]{2,1,0:T(8,128)}, u32[]{:S(2)}, u32[]{:S(2)}) collective-permute-start(f32[4,160,512]{2,1,0:T(8,128)} %get-tuple-element.21), channel_id=1, source_target_pairs={{0,1},{1,0},{2,3},{3,2},{4,5},{5,4},{6,7},{7,6},{8,9},{9,8},{10,11... | collective-permute-start | bytes 3932168 | tf_op jit(solution)/shard_map/ppermute | solution.py:315
  237.7 1.7 copy-start.7
  250.3 31.6 %collective-permute-start = (f32[4,160,256]{2,1,0:T(8,128)S(1)}, f32[4,160,256]{2,1,0:T(8,128)S(1)}, u32[]{:S(2)}, u32[]{:S(2)}) collective-permute-start(f32[4,160,256]{2,1,0:T(8,128)S(1)} %cross_sums_second.3), channel_id=1, source_target_pairs={{0,1},{1,0},{2,3},{3,2},{4,5},{5,4},{6,7},{7,6},{8,9},{9,8},{10,11... | collective-permute-start | bytes 1966088 | tf_op jit(solution)/shard_map/ppermute | solution.py:315
  251.4 15.9 %copy-start.2 = (bf16[512,3001]{1,0:T(8,128)(2,1)S(1)}, bf16[512,3001]{1,0:T(8,128)(2,1)}, u32[]{:S(2)}) copy-start(bf16[512,3001]{1,0:T(8,128)(2,1)} %get-tuple-element.23.table_low) | copy-start | bytes 9219076
  251.4 15.9 %copy-start.3 = (bf16[512,3001]{1,0:T(8,128)(2,1)S(1)}, bf16[512,3001]{1,0:T(8,128)(2,1)}, u32[]{:S(2)}) copy-start(bf16[512,3001]{1,0:T(8,128)(2,1)} %get-tuple-element.24.table_high) | copy-start | bytes 9219076
  251.4 15.9 %copy-start.5 = (f32[4,160,512]{2,1,0:T(8,128)S(1)}, f32[4,160,512]{2,1,0:T(8,128)}, u32[]{:S(2)}) copy-start(f32[4,160,512]{2,1,0:T(8,128)} %copy-done.4) | copy-start | bytes 3932164
  251.4 30.5 %collective-permute-start.2 = (f32[160,128]{1,0:T(8,128)S(1)}, f32[160,128]{1,0:T(8,128)S(1)}, u32[]{:S(2)}, u32[]{:S(2)}) collective-permute-start(f32[160,128]{1,0:T(8,128)S(1)} %get-tuple-element.22.count), channel_id=1, source_target_pairs={{0,1},{1,0},{2,3},{3,2},{4,5},{5,4},{6,7},{7,6},{8,9},{9,8},{10,11... | collective-permute-start | bytes 245768 | tf_op jit(solution)/shard_map/ppermute | solution.py:315

commit v2 on v1

v2 whole, which is shorter than its diff:
```python
import functools
import math

import jax
import jax.numpy as jnp
from jax import lax
from jax.experimental import pallas as pl
from jax.experimental.pallas import tpu as pltpu
from jax.sharding import PartitionSpec as P

CH = 10240
F = 384
F0 = 12
NFFT = 6000
MAXLAG = 1500
SB = 4
SRC = 8
LAGS = 3001
BLOCKS = 64
WIDE = 160
WINS = 64
SLOTS = 128
ROWS = 2 * SLOTS
BINS_A = 256
BINS_B = 128
CAP = 120
PACK = 4
STEP_A = 16
STEP_B = 16
LAG_TILE = 512


def iota(shape, dim):
    return lax.broadcasted_iota(jnp.int32, shape, dim)


def one_hot(where):
    return jnp.where(where, 1.0, 0.0).astype(jnp.bfloat16)


def dot(a, b):
    return jnp.dot(a, b, preferred_element_type=jnp.float32)


def source_kernel(tm_ref, mask_ref, a0, a1, a2, b0, b1, b2, out):
    middle = BLOCKS // 2
    flags = mask_ref[...].astype(jnp.float32).astype(jnp.bfloat16)
    shift = SB * (1 - tm_ref[0])
    lane = iota((WIDE, 128), 1)
    row = iota((WIDE, 128), 0)
    source = (lane + shift) % SRC
    first = dot(flags, one_hot((row == source % SB) & (source < SB) & (lane < SRC)))
    second = dot(flags, one_hot((row == source % SB) & (source >= SB) & (lane < SRC)))
    kept = dot(flags, one_hot(row == lane // 2))
    take = iota((2 * SRC, 16), 0)
    lane = iota((2 * SRC, 16), 1)
    source = (take % SRC + shift) % SRC
    hit = lane == 2 * (source % SB) + take // SRC
    pick_a = one_hot(hit & (source < SB) & (kept[0:1, :16] > 0.5))
    pick_b = one_hot(hit & (source >= SB) & (kept[middle : middle + 1, :16] > 0.5))
    rows = [
        dot(pick_a, ra.reshape(16, 128)[...]) + dot(pick_b, rb.reshape(16, 128)[...])
        for ra, rb in ((a0, b0), (a1, b1), (a2, b2))
    ]
    squares = sum(r * r for r in rows)
    energy = jnp.sum(squares[:SRC] + squares[SRC:], axis=1, keepdims=True) / F
    factor = lax.rsqrt(energy + 1e-06)
    factor = jnp.concatenate([factor, factor], axis=0)
    for k, r in enumerate(rows):
        out[0, :, k * 128 : (k + 1) * 128] = (r * factor).astype(jnp.bfloat16)
    line = iota((2 * SRC, 128), 0)
    flag_line = first[0:1] + second[middle : middle + 1]
    out[0, :, F:] = jnp.where(line == 0, flag_line, 0.0).astype(jnp.bfloat16)


def source_rows(tm_index, mask, spectra):
    head = lambda k, at: pl.BlockSpec((8, 2, 128), lambda i: (at, 0, k))
    middle = BLOCKS // 2 * WIDE // 8
    return pl.pallas_call(
        source_kernel,
        grid=(1,),
        in_specs=[
            pl.BlockSpec(memory_space=pltpu.SMEM),
            pl.BlockSpec((BLOCKS, WIDE), lambda i: (0, 0)),
            *[head(k, 0) for k in range(3)],
            *[head(k, middle) for k in range(3)],
        ],
        out_specs=pl.BlockSpec((1, 2 * SRC, F + 128), lambda i: (0, 0, 0)),
        out_shape=jax.ShapeDtypeStruct((1, 2 * SRC, F + 128), jnp.bfloat16),
        cost_estimate=pl.CostEstimate(flops=10_000_000, bytes_accessed=100_000, transcendentals=0),
        name="source_rows",
    )(tm_index, mask, *[spectra] * 6)


def pack_kernel(mask_ref, x0, x1, x2, send_a, send_b, slot_ref, key_ref):
    step = pl.program_id(0)

    @pl.when(step == 0)
    def _():
        flags = mask_ref[...].astype(jnp.float32).astype(jnp.bfloat16)
        lane = iota((WIDE, 2 * WIDE), 1)
        row = iota((WIDE, 2 * WIDE), 0)
        before = dot(flags, one_hot(row < lane // 2))
        kept = dot(flags, one_hot(row == lane // 2))
        part = (iota((BLOCKS, 2 * WIDE), 1) % 2).astype(jnp.float32)
        slot_ref[...] = jnp.where(kept > 0.5, before + part * SLOTS, -1.0)
        lane = iota((WIDE, BINS_A), 1)
        row = iota((WIDE, BINS_A), 0)
        before = dot(flags, one_hot(row < lane))
        key_ref[...] = jnp.where(dot(flags, one_hot(row == lane)) > 0.5, before, -1.0)

    place = iota((ROWS, 2 * WIDE), 0).astype(jnp.float32).astype(jnp.bfloat16)
    for n in range(PACK):
        block = step * PACK + n
        slot = slot_ref[pl.ds(block, 1), :].astype(jnp.bfloat16)
        pick = jnp.where(place == slot, jnp.ones_like(place), jnp.zeros_like(place))
        at = pl.ds(n * 2 * WIDE, 2 * WIDE)
        band = jnp.concatenate([r.reshape(PACK * 2 * WIDE, 128)[at, :] for r in (x0, x1, x2)], axis=1)
        rows = dot(pick, band)
        real, imag = rows[:CAP], rows[SLOTS : SLOTS + CAP]
        energy = jnp.sum(real * real + imag * imag, axis=1, keepdims=True) / F
        factor = lax.rsqrt(energy + 1e-06)
        real = (real * factor).astype(jnp.bfloat16)
        imag = (imag * factor).astype(jnp.bfloat16)
        send_a[n, :CAP] = real[:, :BINS_A]
        send_a[n, CAP:SLOTS] = jnp.broadcast_to(key_ref[pl.ds(block, 1), :], (8, BINS_A)).astype(jnp.bfloat16)
        send_a[n, SLOTS:] = imag[:, :BINS_A]
        send_b[n, :CAP] = real[:, BINS_A:]
        send_b[n, CAP:] = imag[:, BINS_A:]


def pack(mask, spectra):
    band = lambda k: pl.BlockSpec((PACK * WIDE, 2, 128), lambda b: (b, 0, k))
    return pl.pallas_call(
        pack_kernel,
        grid=(BLOCKS // PACK,),
        in_specs=[pl.BlockSpec((BLOCKS, WIDE), lambda b: (0, 0)), *[band(k) for k in range(3)]],
        out_specs=[
            pl.BlockSpec((PACK, SLOTS + CAP, BINS_A), lambda b: (b, 0, 0)),
            pl.BlockSpec((PACK, 2 * CAP, BINS_B), lambda b: (b, 0, 0)),
        ],
        out_shape=[
            jax.ShapeDtypeStruct((BLOCKS, SLOTS + CAP, BINS_A), jnp.bfloat16),
            jax.ShapeDtypeStruct((BLOCKS, 2 * CAP, BINS_B), jnp.bfloat16),
        ],
        scratch_shapes=[
            pltpu.VMEM((BLOCKS, 2 * WIDE), jnp.float32),
            pltpu.VMEM((BLOCKS, BINS_A), jnp.float32),
        ],
        cost_estimate=pl.CostEstimate(flops=2 * BLOCKS * ROWS * 2 * WIDE * F, bytes_accessed=30_000_000, transcendentals=0),
        compiler_params=pltpu.CompilerParams(vmem_limit_bytes=56 << 20),
        name="whiten_pack",
    )(mask, *[spectra] * 3)


def spread_slots(real, imag, source, pick, held, src, win):
    held[win] = dot(pick, jnp.concatenate([real, imag], axis=1))
    src[win] = source.astype(jnp.float32)


def correlate(held, src, outs, bins, steps):
    def group(i, _):
        rows = pl.ds(pl.multiple_of(i * 8, 8), 8)
        for t in range(0, bins, 128):
            re_at, im_at = slice(t, t + 128), slice(bins + t, bins + t + 128)
            sums = [[ref[q, rows, re_at], ref[q, rows, im_at]] for ref, _ in outs for q in range(SB)]
            for win in range(steps):
                b0, b1 = held[win, rows, re_at], held[win, rows, im_at]
                for n, q in enumerate([first + k for _, first in outs for k in range(SB)]):
                    a0 = jnp.broadcast_to(src[win, q : q + 1, re_at], (8, 128))
                    a1 = jnp.broadcast_to(src[win, SRC + q : SRC + q + 1, re_at], (8, 128))
                    sums[n][0] += a0 * b0 + a1 * b1
                    sums[n][1] += a1 * b0 - a0 * b1
            n = 0
            for ref, _ in outs:
                for q in range(SB):
                    ref[q, rows, re_at], ref[q, rows, im_at] = sums[n]
                    n += 1
        return 0

    lax.fori_loop(0, WIDE // 8, group, 0)


def first_kernel(got, source, theirs, mine, picks, count, held, src, total):
    step = pl.program_id(0)

    @pl.when(step == 0)
    def _():
        total[...] = jnp.zeros_like(total)
        mine[...] = jnp.zeros_like(mine)
        count[...] = jnp.zeros_like(count)

    for win in range(STEP_A):
        notes = got[win, CAP:SLOTS, :].astype(jnp.float32)
        key = jnp.transpose(notes)[:WIDE, 0:1]
        pick = one_hot(iota((WIDE, SLOTS), 1) == key.astype(jnp.int32))
        picks[win] = pick
        flags = source[win, :, F:].astype(jnp.float32)[0:1]
        count[...] += jnp.where(key > -0.5, 1.0, 0.0) * flags
        spread_slots(got[win, :CAP, :], got[win, SLOTS:, :], source[win, :, :BINS_A], pick[:, :CAP], held, src, win)
    correlate(held, src, ((total, 0), (mine, SB)), BINS_A, STEP_A)

    @pl.when(step == pl.num_programs(0) - 1)
    def _():
        theirs[...] = total[...].astype(jnp.bfloat16)


def first_sums(got, source):
    shape = (SB, WIDE, 2 * BINS_A)
    sums_spec = pl.BlockSpec(shape, lambda g: (0, 0, 0))
    return pl.pallas_call(
        first_kernel,
        grid=(WINS // STEP_A,),
        in_specs=[
            pl.BlockSpec((STEP_A, SLOTS + CAP, BINS_A), lambda g: (g, 0, 0)),
            pl.BlockSpec((STEP_A, 2 * SRC, F + 128), lambda g: (g, 0, 0)),
        ],
        out_specs=[
            sums_spec,
            sums_spec,
            pl.BlockSpec((STEP_A, WIDE, SLOTS), lambda g: (g, 0, 0)),
            pl.BlockSpec((WIDE, 128), lambda g: (0, 0)),
        ],
        out_shape=[
            jax.ShapeDtypeStruct(shape, jnp.bfloat16),
            jax.ShapeDtypeStruct(shape, jnp.float32),
            jax.ShapeDtypeStruct((WINS, WIDE, SLOTS), jnp.bfloat16),
            jax.ShapeDtypeStruct((WIDE, 128), jnp.float32),
        ],
        scratch_shapes=[
            pltpu.VMEM((STEP_A, WIDE, 2 * BINS_A), jnp.float32),
            pltpu.VMEM((STEP_A, 2 * SRC, BINS_A), jnp.float32),
            pltpu.VMEM(shape, jnp.float32),
        ],
        cost_estimate=pl.CostEstimate(flops=30_000_000_000, bytes_accessed=20_000_000, transcendentals=0),
        compiler_params=pltpu.CompilerParams(vmem_limit_bytes=32 << 20),
        name="cross_sums_first",
    )(got, source)


def second_kernel(first, got, source, picks, out, held, src, total):
    step = pl.program_id(0)

    @pl.when(step == 0)
    def _():
        total[...] = jnp.zeros_like(total)

    for win in range(STEP_B):
        real, imag = got[win, :CAP, :], got[win, CAP:, :]
        spread_slots(real, imag, source[win], picks[win, :, :CAP], held, src, win)
    correlate(held, src, ((total, first),), BINS_B, STEP_B)

    @pl.when(step == pl.num_programs(0) - 1)
    def _():
        out[...] = total[...].astype(out.dtype)


def second_sums(got, source, picks, first, dtype):
    shape = (SB, WIDE, 2 * BINS_B)
    return pl.pallas_call(
        functools.partial(second_kernel, first),
        grid=(WINS // STEP_B,),
        in_specs=[
            pl.BlockSpec((STEP_B, 2 * CAP, BINS_B), lambda g: (g, 0, 0)),
            pl.BlockSpec((STEP_B, 2 * SRC, BINS_B), lambda g: (g, 0, BINS_A // BINS_B)),
            pl.BlockSpec((STEP_B, WIDE, SLOTS), lambda g: (g, 0, 0)),
        ],
        out_specs=pl.BlockSpec(shape, lambda g: (0, 0, 0)),
        out_shape=jax.ShapeDtypeStruct(shape, dtype),
        scratch_shapes=[
            pltpu.VMEM((STEP_B, WIDE, 2 * BINS_B), jnp.float32),
            pltpu.VMEM((STEP_B, 2 * SRC, BINS_B), jnp.float32),
            pltpu.VMEM(shape, jnp.float32),
        ],
        cost_estimate=pl.CostEstimate(flops=8_000_000_000, bytes_accessed=8_000_000, transcendentals=0),
        compiler_params=pltpu.CompilerParams(vmem_limit_bytes=32 << 20),
        name="cross_sums_second",
    )(got, source, picks)


def split(x):
    high = x.astype(jnp.bfloat16)
    return high, (x - high.astype(jnp.float32)).astype(jnp.bfloat16)


def three_dots(high, low, table_high, table_low):
    t = table_high[...]
    return dot(high[...], t) + (dot(low[...], t) + dot(high[...], table_low[...]))


def load_sums(mine, theirs, high, low):
    total = mine[...] + theirs[...].astype(jnp.float32)
    h, rest = split(total)
    high[...] = h
    low[...] = rest


def lags_first_kernel(mine, theirs, table_high, table_low, out, high, low):
    @pl.when(pl.program_id(0) == 0)
    def _():
        load_sums(mine, theirs, high, low)

    out[...] = three_dots(high, low, table_high, table_low)


def lags_last_kernel(mine, theirs, table_high, table_low, before, count, count_theirs, out, high, low, scale):
    @pl.when(pl.program_id(0) == 0)
    def _():
        load_sums(mine, theirs, high, low)
        for q in range(SB):
            pairs = count[:, SB + q : SB + q + 1] + count_theirs[:, q : q + 1]
            scale[q * WIDE : (q + 1) * WIDE] = jnp.broadcast_to(1.0 / jnp.maximum(pairs, 1.0), (WIDE, 128))

    out[...] = (before[...] + three_dots(high, low, table_high, table_low)) * scale[:, 0:1]


def to_lags(mine, theirs, tables, before=None, counts=()):
    rows, depth = SB * WIDE, tables[0].shape[0]
    tile = pl.BlockSpec((rows, LAG_TILE), lambda n: (0, n))
    full = lambda shape: pl.BlockSpec(shape, lambda n: (0, 0))
    table = pl.BlockSpec((depth, LAG_TILE), lambda n: (0, n))
    last = before is not None
    return pl.pallas_call(
        lags_last_kernel if last else lags_first_kernel,
        grid=(pl.cdiv(LAGS, LAG_TILE),),
        in_specs=[full((rows, depth)), full((rows, depth)), table, table]
        + ([tile, full((WIDE, 128)), full((WIDE, 128))] if last else []),
        out_specs=tile,
        out_shape=jax.ShapeDtypeStruct((rows, LAGS), jnp.float32),
        scratch_shapes=[pltpu.VMEM((rows, depth), jnp.bfloat16)] * 2
        + ([pltpu.VMEM((rows, 128), jnp.float32)] if last else []),
        cost_estimate=pl.CostEstimate(flops=6 * rows * depth * LAGS, bytes_accessed=4 * rows * LAGS * (2 if last else 1), transcendentals=0),
        compiler_params=pltpu.CompilerParams(vmem_limit_bytes=32 << 20),
        name="to_lags_last" if last else "to_lags_first",
    )(
        mine.reshape(rows, depth),
        theirs.reshape(rows, depth),
        *tables,
        *((before, *counts) if last else ()),
    )


def lag_table(first_bin, bins, zero):
    bin_index = F0 + first_bin + zero + jnp.arange(bins, dtype=jnp.int32)
    lag_index = jnp.arange(LAGS, dtype=jnp.int32) - MAXLAG
    phase_steps = jnp.mod(bin_index[:, None] * lag_index[None, :], NFFT)
    angles = phase_steps.astype(jnp.float32) * jnp.float32(2.0 * math.pi / NFFT)
    table = jnp.concatenate([jnp.cos(angles), -jnp.sin(angles)], axis=0)
    high = lax.reduce_precision(table, 8, 7)
    return high.astype(jnp.bfloat16), (table - high).astype(jnp.bfloat16)


def swap(x):
    return lax.ppermute(x, "tm", [(0, 1), (1, 0)])


def local(spectra, mask):
    tm_index = lax.axis_index("tm").astype(jnp.int32)[None]
    flags = mask.reshape(BLOCKS, WIDE)
    spectra = spectra.reshape(CH, 2, F)
    source = source_rows(tm_index, flags, spectra)
    gathered = lax.all_gather(source, "chan", axis=0, tiled=True)
    flags, _ = lax.optimization_barrier((flags, source))
    send_a, send_b = pack(flags, spectra)
    send_a, zero = lax.optimization_barrier((send_a, jnp.int32(0)))
    tables_a = lag_table(0, BINS_A, zero)
    tables_b = lag_table(BINS_A, BINS_B, zero)
    send_b, tables_a, tables_b = lax.optimization_barrier((send_b, tables_a, tables_b))
    exchange = lambda x: lax.all_to_all(x, "chan", split_axis=0, concat_axis=0, tiled=True)
    got_a = exchange(send_a)
    got_b = exchange(send_b)
    theirs_a, mine_a, picks, count = first_sums(got_a, gathered)
    from_a = swap(theirs_a)
    count_from = swap(count)
    lagged = to_lags(mine_a, from_a, tables_a)
    got_b, lagged = lax.optimization_barrier((got_b, lagged))
    theirs_b = second_sums(got_b, gathered, picks, 0, jnp.bfloat16)
    from_b = swap(theirs_b)
    mine_b = second_sums(got_b, gathered, picks, SB, jnp.float32)
    lagged = to_lags(mine_b, from_b, tables_b, lagged, (count, count_from))
    return lagged.reshape(SB, WIDE, LAGS)


def solution(mesh):
    placed = (P("tm", "chan", None, None, None), P("tm", "chan", None))
    return jax.shard_map(
        local, mesh=mesh, in_specs=placed, out_specs=P("tm", "chan", None), check_vma=False
    )
```

time: 291 us -> 314 us (1.079)
  waiting for transfers between devices: 111 us -> 147 us
  Pallas kernels: 118 us -> 91 us
  between operations: 0.12 us -> 13.6 us
  other arithmetic: 25.3 us -> 28.7 us
    all_gather x0 -> x1, waiting for transfers between devices: none -> 57.3 us  [local(): gathered = lax.all_gather(source, 'chan', axis=0, tiled=True)]
    all_to_all x2, waiting for transfers between devices: 102 us -> 73.3 us  [local(): lax.all_to_all(x, 'chan', split_axis=0, concat_axis=0, tiled=True)]
    pallas_call x2 -> x3, Pallas kernels: 79.4 us -> 55.3 us  [the longest x1 31.7 us: first_sums(): pl.pallas_call(first_kernel, grid=(WINS // STEP_A,), in_specs=[pl.BlockSp...]
    ppermute x3, waiting for transfers between devices: 8.65 us -> 15.5 us  [swap(): return lax.ppermute(x, 'tm', [(0, 1), (1, 0)])]
    unnamed x17 -> x19, local copies, waits for them, and re-layouts: 10.2 us -> 9.46 us
  transfers between devices with their start and end apart: 5 -> 6, of which waited for: 4 -> 3; matrix products, arithmetic and copies ran while one was open for 8% -> 9% of each run, Pallas kernels for 22% -> 19%
where the time goes in v2:
time: 314 us; the launch traced here: 313 us
  waiting for transfers between devices  147 us (47%)
  Pallas kernels  91 us (29%)
  other arithmetic  28.7 us (9%)
  starting transfers between devices  23.1 us (7%)
  between operations  13.6 us (4%)
  local copies, waits for them, and re-layouts  10.2 us (3%)
    all_to_all x2, waiting for transfers between devices, local(): lax.all_to_all(x, 'chan', split_axis=0, concat_axis=0, tiled=True)  73.3 us
    all_gather x1, waiting for transfers between devices, local(): gathered = lax.all_gather(source, 'chan', axis=0, tiled=True)  57.3 us
    pallas_call x1, Pallas kernels, first_sums(): pl.pallas_call(first_kernel, grid=(WINS // STEP_A,), in_specs=[pl.BlockSp...  31.7 us
    pallas_call x1, Pallas kernels, pack(): pl.pallas_call(pack_kernel, grid=(BLOCKS // PACK,), in_specs=[pl.BlockSpe...  21.6 us
    cos x2, other arithmetic, lag_table(): table = jnp.concatenate([jnp.cos(angles), -jnp.sin(angles)], axis=0)  20.7 us
    pallas_call x2, Pallas kernels, second_sums(): pl.pallas_call(functools.partial(second_kernel, first), grid=(WINS // STE...  20.4 us
    all_to_all x2, starting transfers between devices, local(): lax.all_to_all(x, 'chan', split_axis=0, concat_axis=0, tiled=True)  20 us
    ppermute x3, waiting for transfers between devices, swap(): return lax.ppermute(x, 'tm', [(0, 1), (1, 0)])  15.5 us
  transfers between devices with their start and end apart: 6, of which 3 were waited for; matrix products, arithmetic and copies ran while one was open for 9% of the time, Pallas kernels for 19%

profile of v2, /device:TPU:0, one launch (start us, length us, event | category | flops | bytes accessed | tf_op | source)
XLA Modules:
  0.0 313.4 jit_solution(6791263970758787392)
XLA Ops:
  6.5 0.5 broadcast.25
  7.0 1.5 reduce.3
  8.6 0.7 reshape.33.mask_ref
  9.3 2.0 source_rows.1
  11.2 21.6 %whiten_pack.1 = (bf16[64,248,256]{2,1,0:T(8,128)(2,1)}, bf16[64,240,128]{2,1,0:T(8,128)(2,1)}) custom-call(s32[64,160]{1,0:T(8,128)} %reshape.33.mask_ref, bf16[10240,2,384]{2,1,0:T(2,128)(2,1)} %bitcast.19, bf16[10240,2,384]{2,1,0:T(2,128)(2,1)} %bitcast.20, bf16[10240,2,384]{2,1,0:T(2,128)(2,1)} %bitcast.21), custom_call_target="tpu_custom_call" | custom-call | flops 4026531840 | bytes 30000000 | tf_op jit(solution)/shard_map/whiten_pack/pallas_call | solution.py:134
  32.9 11.6 %all-to-all-start.1 = ((bf16[64,248,256]{2,1,0:T(8,128)(2,1)}), bf16[64,248,256]{2,1,0:T(8,128)(2,1)}, u32[]{:S(2)}, u32[]{:S(2)}) async-start(bf16[64,248,256]{2,1,0:T(8,128)(2,1)} %get-tuple-element.26), calls=%async_computation.1 | async-start | bytes 16252928 | tf_op jit(solution)/shard_map/all_to_all | solution.py:369
  44.5 0.0 all-gather.2.cloned.1.call-start
  44.5 0.7 all-gather.2.cloned.1.call-update
  45.2 7.9 %fusion.12 = (f32[128,3001]{1,0:T(8,128)}, f32[128,3001]{1,0:T(8,128)}) fusion(s32[3001]{0:T(1024)S(1)} %iota_add_fusion, s32[128]{0:T(128)S(1)} %iota_add_fusion.2), kind=kLoop, calls=%fused_computation.24 | loop fusion | flops 3841280 | bytes 3085540 | tf_op jit(solution)/shard_map/cos | solution.py:348
  53.1 2.4 fusion.1
  55.5 12.9 %fusion.6 = (f32[256,3001]{1,0:T(8,128)S(1)}, f32[256,3001]{1,0:T(8,128)S(1)}) fusion(s32[3001]{0:T(1024)S(1)} %iota_add_fusion, s32[256]{0:T(256)S(1)} %iota_add_fusion.1), kind=kLoop, calls=%fused_computation.15 | loop fusion | flops 7682560 | bytes 6159076 | tf_op jit(solution)/shard_map/cos | solution.py:348
  68.4 4.0 %fusion = (bf16[512,3001]{1,0:T(8,128)(2,1)}, bf16[512,3001]{1,0:T(8,128)(2,1)}) fusion(f32[256,3001]{1,0:T(8,128)S(1)} %get-tuple-element.42, f32[256,3001]{1,0:T(8,128)S(1)} %get-tuple-element.41), kind=kLoop, calls=%fused_computation.2 | loop fusion | flops 7682560 | bytes 12292096 | tf_op jit(solution)/shard_map/convert_element_type | solution.py:350
  72.4 73.3 %all-to-all-done.1.got = bf16[64,248,256]{2,1,0:T(8,128)(2,1)} async-done(((bf16[64,248,256]{2,1,0:T(8,128)(2,1)}), bf16[64,248,256]{2,1,0:T(8,128)(2,1)}, u32[]{:S(2)}, u32[]{:S(2)}) %all-to-all-start.1) | async-done | bytes 8126496 | tf_op jit(solution)/shard_map/all_to_all | solution.py:369
  145.7 8.4 %all-to-all-start = ((bf16[64,240,128]{2,1,0:T(8,128)(2,1)}), bf16[64,240,128]{2,1,0:T(8,128)(2,1)}, u32[]{:S(2)}, u32[]{:S(2)}) async-start(bf16[64,240,128]{2,1,0:T(8,128)(2,1)} %get-tuple-element.25), calls=%async_computation | async-start | bytes 7864320 | tf_op jit(solution)/shard_map/all_to_all | solution.py:369
  154.1 57.3 %all-gather.2.cloned.1.call-done.source = bf16[64,16,512]{2,1,0:T(8,128)(2,1)} async-done(((bf16[1,16,512]{2,1,0:T(8,128)(2,1)}), bf16[64,16,512]{2,1,0:T(8,128)(2,1)}) %all-gather.2.cloned.1.call-update) | async-done | bytes 1048592 | tf_op jit(solution)/shard_map/all_gather | solution.py:362
  211.5 0.0 copy-start.3
  211.5 1.2 copy-done.3
  212.7 0.0 copy-start.1
  212.7 0.0 copy-start.2
  212.7 31.7 %cross_sums_first.1 = (bf16[4,160,512]{2,1,0:T(8,128)(2,1)S(1)}, f32[4,160,512]{2,1,0:T(8,128)S(1)}, bf16[64,160,128]{2,1,0:T(8,128)(2,1)S(1)}, f32[160,128]{1,0:T(8,128)S(1)}) custom-call(bf16[64,248,256]{2,1,0:T(8,128)(2,1)} %all-to-all-done.1.got, bf16[64,16,512]{2,1,0:T(8,128)(2,1)S(1)} %copy-done.3), custom_call_target="tpu_custom_call" | custom-call | flops 30000001024 | bytes 20000000 | tf_op jit(solution)/shard_map/cross_sums_first/pallas_call | solution.py:211
  244.4 0.0 copy-start.5
  244.4 1.5 copy-done.5
  245.9 1.0 collective-permute-start
  246.9 1.0 collective-permute-start.2
  247.9 15.5 %collective-permute-done = bf16[4,160,512]{2,1,0:T(8,128)(2,1)S(1)} collective-permute-done((bf16[4,160,512]{2,1,0:T(8,128)(2,1)S(1)}, bf16[4,160,512]{2,1,0:T(8,128)(2,1)S(1)}, u32[]{:S(2)}, u32[]{:S(2)}) %collective-permute-start) | collective-permute-done | bytes 655392 | tf_op jit(solution)/shard_map/ppermute | solution.py:354
  263.5 0.0 copy-done.1
  263.5 0.0 copy-done.2
  263.5 8.3 %to_lags_first.1.before = f32[640,3001]{1,0:T(8,128)S(1)} custom-call(f32[640,512]{1,0:T(8,128)S(1)} %bitcast.12, bf16[640,512]{1,0:T(8,128)(2,1)S(1)} %bitcast.11, bf16[512,3001]{1,0:T(8,128)(2,1)S(1)} %copy-done.2, bf16[512,3001]{1,0:T(8,128)(2,1)S(1)} %copy-done.1), custom_call_target="tpu_custom_call" | custom-call | flops 5900206080 | bytes 7682560 | tf_op jit(solution)/shard_map/to_lags_first/pallas_call | solution.py:323
  271.8 0.0 copy-start
  271.8 3.2 %copy-done = f32[640,3001]{1,0:T(8,128)} copy-done((f32[640,3001]{1,0:T(8,128)}, f32[640,3001]{1,0:T(8,128)S(1)}, u32[]{:S(2)}) %copy-start) | copy-done | bytes 7682584
  275.0 0.0 all-to-all-done.got
  275.0 0.0 copy-start.4
  275.0 1.2 copy-done.4
  276.2 0.0 copy-start.6
  276.2 1.7 copy-done.6
  278.0 0.0 slice-start
  278.0 10.3 %cross_sums_second.3 = bf16[4,160,256]{2,1,0:T(8,128)(2,1)S(1)} custom-call(bf16[64,240,128]{2,1,0:T(8,128)(2,1)} %all-to-all-done.got, bf16[64,16,512]{2,1,0:T(8,128)(2,1)S(1)} %copy-done.4, bf16[64,160,128]{2,1,0:T(8,128)(2,1)S(1)} %copy-done.6), custom_call_target="tpu_custom_call" | custom-call | flops 8000000000 | bytes 8000000 | tf_op jit(solution)/shard_map/cross_sums_second/pallas_call | solution.py:260
  288.3 0.0 slice-start.1
  288.3 1.1 collective-permute-start.1
  289.4 10.1 %cross_sums_second.2 = f32[4,160,256]{2,1,0:T(8,128)S(1)} custom-call(bf16[64,240,128]{2,1,0:T(8,128)(2,1)} %all-to-all-done.got, bf16[64,16,512]{2,1,0:T(8,128)(2,1)S(1)} %copy-done.4, bf16[64,160,128]{2,1,0:T(8,128)(2,1)S(1)} %copy-done.6), custom_call_target="tpu_custom_call" | custom-call | flops 8000000000 | bytes 8000000 | tf_op jit(solution)/shard_map/cross_sums_second/pallas_call | solution.py:260
  299.5 0.0 collective-permute-done.2.count_theirs
  299.6 0.0 collective-permute-done.1
  299.6 0.0 slice-done
  299.6 0.0 slice-done.1
  299.6 7.0 %to_lags_last.1 = f32[640,3001]{1,0:T(8,128)} custom-call(f32[640,256]{1,0:T(8,128)S(1)} %bitcast.9, bf16[640,256]{1,0:T(8,128)(2,1)S(1)} %bitcast.10, bf16[256,3001]{1,0:T(8,128)(2,1)S(1)} %get-tuple-element.33.table_high, bf16[256,3001]{1,0:T(8,128)(2,1)S(1)} %get-tuple-element.34.table_low, f32[640,3001]{1,0:T(8,128)S(1)} %bitcast.8, ...), custom_call_target="tpu_custom_call" | custom-call | flops 2950103040 | bytes 15365120 | tf_op jit(solution)/shard_map/to_lags_last/pallas_call | solution.py:323
  (4 shorter events, 0.0 us)
Async XLA Ops:
  32.9 112.9 %all-to-all-start.1 = ((bf16[64,248,256]{2,1,0:T(8,128)(2,1)}), bf16[64,248,256]{2,1,0:T(8,128)(2,1)}, u32[]{:S(2)}, u32[]{:S(2)}) async-start(bf16[64,248,256]{2,1,0:T(8,128)(2,1)} %get-tuple-element.26), calls=%async_computation.1 | async-start | bytes 16252928 | tf_op jit(solution)/shard_map/all_to_all | solution.py:369
  44.5 167.0 %all-gather.2.cloned.1.call-start = ((), (), s32[]{:S(2)}) async-start(), calls=%async_computation.2 | async-start | bytes 1064960 | tf_op jit(solution)/shard_map/all_gather | solution.py:362
  145.7 129.3 %all-to-all-start = ((bf16[64,240,128]{2,1,0:T(8,128)(2,1)}), bf16[64,240,128]{2,1,0:T(8,128)(2,1)}, u32[]{:S(2)}, u32[]{:S(2)}) async-start(bf16[64,240,128]{2,1,0:T(8,128)(2,1)} %get-tuple-element.25), calls=%async_computation | async-start | bytes 7864320 | tf_op jit(solution)/shard_map/all_to_all | solution.py:369
  211.5 1.2 copy-start.3
  212.7 50.8 %copy-start.1 = (bf16[512,3001]{1,0:T(8,128)(2,1)S(1)}, bf16[512,3001]{1,0:T(8,128)(2,1)}, u32[]{:S(2)}) copy-start(bf16[512,3001]{1,0:T(8,128)(2,1)} %get-tuple-element.30.table_low) | copy-start | bytes 9219076
  212.7 50.8 %copy-start.2 = (bf16[512,3001]{1,0:T(8,128)(2,1)S(1)}, bf16[512,3001]{1,0:T(8,128)(2,1)}, u32[]{:S(2)}) copy-start(bf16[512,3001]{1,0:T(8,128)(2,1)} %get-tuple-element.29.table_high) | copy-start | bytes 9219076
  244.4 1.5 copy-start.5
  245.9 17.6 %collective-permute-start = (bf16[4,160,512]{2,1,0:T(8,128)(2,1)S(1)}, bf16[4,160,512]{2,1,0:T(8,128)(2,1)S(1)}, u32[]{:S(2)}, u32[]{:S(2)}) collective-permute-start(bf16[4,160,512]{2,1,0:T(8,128)(2,1)S(1)} %get-tuple-element.28), channel_id=1, source_target_pairs={{0,1},{1,0},{2,3},{3,2},{4,5},{5,4},{6,7},{7,6},{8,9},{9,8},{10,11... | collective-permute-start | bytes 1966088 | tf_op jit(solution)/shard_map/ppermute | solution.py:354
  246.9 52.6 %collective-permute-start.2 = (f32[160,128]{1,0:T(8,128)S(1)}, f32[160,128]{1,0:T(8,128)S(1)}, u32[]{:S(2)}, u32[]{:S(2)}) collective-permute-start(f32[160,128]{1,0:T(8,128)S(1)} %get-tuple-element.36.count), channel_id=1, source_target_pairs={{0,1},{1,0},{2,3},{3,2},{4,5},{5,4},{6,7},{7,6},{8,9},{9,8},{10,11... | collective-permute-start | bytes 245768 | tf_op jit(solution)/shard_map/ppermute | solution.py:354
  271.8 3.2 %copy-start = (f32[640,3001]{1,0:T(8,128)}, f32[640,3001]{1,0:T(8,128)S(1)}, u32[]{:S(2)}) copy-start(f32[640,3001]{1,0:T(8,128)S(1)} %to_lags_first.1.before) | copy-start | bytes 23047684
  275.0 1.2 copy-start.4
  276.2 1.7 copy-start.6
  278.0 21.6 %slice-start = ((s8[7864320]{0:T(1024)(128)(4,1)}), s8[4194304]{0:T(1024)(128)(4,1)S(1)}, s32[]{:S(2)}) async-start(s8[7864320]{0:T(1024)(128)(4,1)} %bitcast.7), calls=%async_computation.3 | async-start | bytes 8388608
  288.3 11.3 %slice-start.1 = ((s8[7864320]{0:T(1024)(128)(4,1)}), s8[3670016]{0:T(1024)(128)(4,1)S(1)}, s32[]{:S(2)}) async-start(s8[7864320]{0:T(1024)(128)(4,1)} %bitcast.7), calls=%async_computation.4 | async-start | bytes 7340032
  288.3 11.3 %collective-permute-start.1 = (bf16[4,160,256]{2,1,0:T(8,128)(2,1)S(1)}, bf16[4,160,256]{2,1,0:T(8,128)(2,1)S(1)}, u32[]{:S(2)}, u32[]{:S(2)}) collective-permute-start(bf16[4,160,256]{2,1,0:T(8,128)(2,1)S(1)} %cross_sums_second.3), channel_id=1, source_target_pairs={{0,1},{1,0},{2,3},{3,2},{4,5},{5,4},{6,7},{7,6},{8,9},{9,8},{10,11... | collective-permute-start | bytes 983048 | tf_op jit(solution)/shard_map/ppermute | solution.py:354
Sparse Core Ops, SparseCore 0:
  48.5 162.8 all-gather.1

commit v3 on v2

--- a/solution.py
+++ b/solution.py
@@ -24,7 +24,8 @@
 BINS_A = 256
 BINS_B = 128
 CAP = 120
-PACK = 4
+PACK = 8
+GRANT = 56 << 20
 STEP_A = 16
 STEP_B = 16
 LAG_TILE = 512
@@ -92,7 +93,7 @@
     )(tm_index, mask, *[spectra] * 6)
 
 
-def pack_kernel(mask_ref, x0, x1, x2, send_a, send_b, slot_ref, key_ref):
+def pack_kernel(mask_ref, src_ref, x0, x1, x2, send_a, send_b, slot_ref, key_ref):
     step = pl.program_id(0)
 
     @pl.when(step == 0)
@@ -109,6 +110,8 @@
         before = dot(flags, one_hot(row < lane))
         key_ref[...] = jnp.where(dot(flags, one_hot(row == lane)) > 0.5, before, -1.0)
 
+    flag_line = src_ref[0, :1, F:].astype(jnp.float32)
+    flag_line = jnp.concatenate([flag_line, flag_line], axis=1)
     place = iota((ROWS, 2 * WIDE), 0).astype(jnp.float32).astype(jnp.bfloat16)
     for n in range(PACK):
         block = step * PACK + n
@@ -122,99 +125,111 @@
         factor = lax.rsqrt(energy + 1e-06)
         real = (real * factor).astype(jnp.bfloat16)
         imag = (imag * factor).astype(jnp.bfloat16)
-        send_a[n, :CAP] = real[:, :BINS_A]
-        send_a[n, CAP:SLOTS] = jnp.broadcast_to(key_ref[pl.ds(block, 1), :], (8, BINS_A)).astype(jnp.bfloat16)
-        send_a[n, SLOTS:] = imag[:, :BINS_A]
-        send_b[n, :CAP] = real[:, BINS_A:]
-        send_b[n, CAP:] = imag[:, BINS_A:]
-
-
-def pack(mask, spectra):
+        for out, lo, hi in ((send_a, 0, BINS_A), (send_b, BINS_A, F)):
+            out[n, :CAP] = real[:, lo:hi]
+            out[n, CAP:SLOTS] = src_ref[0, :SRC, lo:hi]
+            out[n, SLOTS : SLOTS + CAP] = imag[:, lo:hi]
+            out[n, SLOTS + CAP : ROWS] = src_ref[0, SRC:, lo:hi]
+        line = iota((8, BINS_A), 0)
+        notes = jnp.where(line == 0, key_ref[pl.ds(block, 1), :], flag_line)
+        send_a[n, ROWS:] = notes.astype(jnp.bfloat16)
+
+
+def pack(mask, source, spectra):
     band = lambda k: pl.BlockSpec((PACK * WIDE, 2, 128), lambda b: (b, 0, k))
     return pl.pallas_call(
         pack_kernel,
         grid=(BLOCKS // PACK,),
-        in_specs=[pl.BlockSpec((BLOCKS, WIDE), lambda b: (0, 0)), *[band(k) for k in range(3)]],
+        in_specs=[
+            pl.BlockSpec((BLOCKS, WIDE), lambda b: (0, 0)),
+            pl.BlockSpec((1, 2 * SRC, F + 128), lambda b: (0, 0, 0)),
+            *[band(k) for k in range(3)],
+        ],
         out_specs=[
-            pl.BlockSpec((PACK, SLOTS + CAP, BINS_A), lambda b: (b, 0, 0)),
-            pl.BlockSpec((PACK, 2 * CAP, BINS_B), lambda b: (b, 0, 0)),
+            pl.BlockSpec((PACK, ROWS + 8, BINS_A), lambda b: (b, 0, 0)),
+            pl.BlockSpec((PACK, ROWS, BINS_B), lambda b: (b, 0, 0)),
         ],
         out_shape=[
-            jax.ShapeDtypeStruct((BLOCKS, SLOTS + CAP, BINS_A), jnp.bfloat16),
-            jax.ShapeDtypeStruct((BLOCKS, 2 * CAP, BINS_B), jnp.bfloat16),
+            jax.ShapeDtypeStruct((BLOCKS, ROWS + 8, BINS_A), jnp.bfloat16),
+            jax.ShapeDtypeStruct((BLOCKS, ROWS, BINS_B), jnp.bfloat16),
         ],
         scratch_shapes=[
             pltpu.VMEM((BLOCKS, 2 * WIDE), jnp.float32),
             pltpu.VMEM((BLOCKS, BINS_A), jnp.float32),
         ],
         cost_estimate=pl.CostEstimate(flops=2 * BLOCKS * ROWS * 2 * WIDE * F, bytes_accessed=30_000_000, transcendentals=0),
-        compiler_params=pltpu.CompilerParams(vmem_limit_bytes=56 << 20),
+        compiler_params=pltpu.CompilerParams(vmem_limit_bytes=GRANT),
         name="whiten_pack",
-    )(mask, *[spectra] * 3)
-
-
-def spread_slots(real, imag, source, pick, held, src, win):
-    held[win] = dot(pick, jnp.concatenate([real, imag], axis=1))
-    src[win] = source.astype(jnp.float32)
-
-
-def correlate(held, src, outs, bins, steps):
+    )(mask, source, *[spectra] * 3)
+
+
+def spread_slots(got, pick, held, src, win, bins):
+    rows = jnp.concatenate([got[win, :SLOTS, :], got[win, SLOTS:ROWS, :]], axis=1)
+    held[win] = dot(pick, rows)
+    real = rows[CAP:, :bins].astype(jnp.float32)
+    imag = rows[CAP:, bins:].astype(jnp.float32)
+    src[win, :SRC] = real
+    src[win, SRC : 2 * SRC] = imag
+    src[win, 2 * SRC :] = real + imag
+
+
+def correlate(held, src, total, sources, bins, steps):
     def group(i, _):
         rows = pl.ds(pl.multiple_of(i * 8, 8), 8)
         for t in range(0, bins, 128):
-            re_at, im_at = slice(t, t + 128), slice(bins + t, bins + t + 128)
-            sums = [[ref[q, rows, re_at], ref[q, rows, im_at]] for ref, _ in outs for q in range(SB)]
+            lanes = [slice(k * bins + t, k * bins + t + 128) for k in range(3)]
+            sums = [[total[n, rows, at] for at in lanes] for n in range(len(sources))]
             for win in range(steps):
-                b0, b1 = held[win, rows, re_at], held[win, rows, im_at]
-                for n, q in enumerate([first + k for _, first in outs for k in range(SB)]):
-                    a0 = jnp.broadcast_to(src[win, q : q + 1, re_at], (8, 128))
-                    a1 = jnp.broadcast_to(src[win, SRC + q : SRC + q + 1, re_at], (8, 128))
-                    sums[n][0] += a0 * b0 + a1 * b1
-                    sums[n][1] += a1 * b0 - a0 * b1
-            n = 0
-            for ref, _ in outs:
-                for q in range(SB):
-                    ref[q, rows, re_at], ref[q, rows, im_at] = sums[n]
-                    n += 1
+                b0, b1 = held[win, rows, lanes[0]], held[win, rows, lanes[1]]
+                for n, q in enumerate(sources):
+                    for k, b in enumerate((b0, b1, b0 - b1)):
+                        a = src[win, k * SRC + q : k * SRC + q + 1, lanes[0]]
+                        sums[n][k] += jnp.broadcast_to(a, (8, 128)) * b
+            for n in range(len(sources)):
+                for at, value in zip(lanes, sums[n]):
+                    total[n, rows, at] = value
         return 0
 
     lax.fori_loop(0, WIDE // 8, group, 0)
 
 
-def first_kernel(got, source, theirs, mine, picks, count, held, src, total):
+def store_sums(total, n, out, q, bins):
+    p, m, r = (total[n, :, k * bins : (k + 1) * bins] for k in range(3))
+    out[q, :, :bins] = (p + m).astype(out.dtype)
+    out[q, :, bins:] = (r - p + m).astype(out.dtype)
+
+
+def first_kernel(got, theirs, mine, picks, count, held, src, total):
     step = pl.program_id(0)
 
     @pl.when(step == 0)
     def _():
         total[...] = jnp.zeros_like(total)
-        mine[...] = jnp.zeros_like(mine)
         count[...] = jnp.zeros_like(count)
 
     for win in range(STEP_A):
-        notes = got[win, CAP:SLOTS, :].astype(jnp.float32)
+        notes = got[win, ROWS:, :].astype(jnp.float32)
         key = jnp.transpose(notes)[:WIDE, 0:1]
         pick = one_hot(iota((WIDE, SLOTS), 1) == key.astype(jnp.int32))
         picks[win] = pick
-        flags = source[win, :, F:].astype(jnp.float32)[0:1]
-        count[...] += jnp.where(key > -0.5, 1.0, 0.0) * flags
-        spread_slots(got[win, :CAP, :], got[win, SLOTS:, :], source[win, :, :BINS_A], pick[:, :CAP], held, src, win)
-    correlate(held, src, ((total, 0), (mine, SB)), BINS_A, STEP_A)
+        count[...] += jnp.where(key > -0.5, 1.0, 0.0) * notes[1:2, :128]
+        spread_slots(got, pick, held, src, win, BINS_A)
+    correlate(held, src, total, range(SRC), BINS_A, STEP_A)
 
     @pl.when(step == pl.num_programs(0) - 1)
     def _():
-        theirs[...] = total[...].astype(jnp.bfloat16)
-
-
-def first_sums(got, source):
+        for q in range(SB):
+            store_sums(total, q, theirs, q, BINS_A)
+            store_sums(total, SB + q, mine, q, BINS_A)
+
+
+def first_sums(got):
     shape = (SB, WIDE, 2 * BINS_A)
     sums_spec = pl.BlockSpec(shape, lambda g: (0, 0, 0))
     return pl.pallas_call(
         first_kernel,
         grid=(WINS // STEP_A,),
-        in_specs=[
-            pl.BlockSpec((STEP_A, SLOTS + CAP, BINS_A), lambda g: (g, 0, 0)),
-            pl.BlockSpec((STEP_A, 2 * SRC, F + 128), lambda g: (g, 0, 0)),
-        ],
+        in_specs=[pl.BlockSpec((STEP_A, ROWS + 8, BINS_A), lambda g: (g, 0, 0))],
         out_specs=[
             sums_spec,
             sums_spec,
@@ -229,16 +244,16 @@
         ],
         scratch_shapes=[
             pltpu.VMEM((STEP_A, WIDE, 2 * BINS_A), jnp.float32),
-            pltpu.VMEM((STEP_A, 2 * SRC, BINS_A), jnp.float32),
-            pltpu.VMEM(shape, jnp.float32),
+            pltpu.VMEM((STEP_A, 3 * SRC, BINS_A), jnp.float32),
+            pltpu.VMEM((SRC, WIDE, 3 * BINS_A), jnp.float32),
         ],
         cost_estimate=pl.CostEstimate(flops=30_000_000_000, bytes_accessed=20_000_000, transcendentals=0),
-        compiler_params=pltpu.CompilerParams(vmem_limit_bytes=32 << 20),
+        compiler_params=pltpu.CompilerParams(vmem_limit_bytes=GRANT),
         name="cross_sums_first",
-    )(got, source)
-
-
-def second_kernel(first, got, source, picks, out, held, src, total):
+    )(got)
+
+
+def second_kernel(first, got, picks, out, held, src, total):
     step = pl.program_id(0)
 
     @pl.when(step == 0)
@@ -246,36 +261,35 @@
         total[...] = jnp.zeros_like(total)
 
     for win in range(STEP_B):
-        real, imag = got[win, :CAP, :], got[win, CAP:, :]
-        spread_slots(real, imag, source[win], picks[win, :, :CAP], held, src, win)
-    correlate(held, src, ((total, first),), BINS_B, STEP_B)
+        spread_slots(got, picks[win], held, src, win, BINS_B)
+    correlate(held, src, total, range(first, first + SB), BINS_B, STEP_B)
 
     @pl.when(step == pl.num_programs(0) - 1)
     def _():
-        out[...] = total[...].astype(out.dtype)
-
-
-def second_sums(got, source, picks, first, dtype):
+        for q in range(SB):
+            store_sums(total, q, out, q, BINS_B)
+
+
+def second_sums(got, picks, first, dtype):
     shape = (SB, WIDE, 2 * BINS_B)
     return pl.pallas_call(
         functools.partial(second_kernel, first),
         grid=(WINS // STEP_B,),
         in_specs=[
-            pl.BlockSpec((STEP_B, 2 * CAP, BINS_B), lambda g: (g, 0, 0)),
-            pl.BlockSpec((STEP_B, 2 * SRC, BINS_B), lambda g: (g, 0, BINS_A // BINS_B)),
+            pl.BlockSpec((STEP_B, ROWS, BINS_B), lambda g: (g, 0, 0)),
             pl.BlockSpec((STEP_B, WIDE, SLOTS), lambda g: (g, 0, 0)),
         ],
         out_specs=pl.BlockSpec(shape, lambda g: (0, 0, 0)),
         out_shape=jax.ShapeDtypeStruct(shape, dtype),
         scratch_shapes=[
             pltpu.VMEM((STEP_B, WIDE, 2 * BINS_B), jnp.float32),
-            pltpu.VMEM((STEP_B, 2 * SRC, BINS_B), jnp.float32),
-            pltpu.VMEM(shape, jnp.float32),
+            pltpu.VMEM((STEP_B, 3 * SRC, BINS_B), jnp.float32),
+            pltpu.VMEM((SB, WIDE, 3 * BINS_B), jnp.float32),
         ],
         cost_estimate=pl.CostEstimate(flops=8_000_000_000, bytes_accessed=8_000_000, transcendentals=0),
-        compiler_params=pltpu.CompilerParams(vmem_limit_bytes=32 << 20),
+        compiler_params=pltpu.CompilerParams(vmem_limit_bytes=GRANT),
         name="cross_sums_second",
-    )(got, source, picks)
+    )(got, picks)
 
 
 def split(x):
@@ -330,7 +344,7 @@
         scratch_shapes=[pltpu.VMEM((rows, depth), jnp.bfloat16)] * 2
         + ([pltpu.VMEM((rows, 128), jnp.float32)] if last else []),
         cost_estimate=pl.CostEstimate(flops=6 * rows * depth * LAGS, bytes_accessed=4 * rows * LAGS * (2 if last else 1), transcendentals=0),
-        compiler_params=pltpu.CompilerParams(vmem_limit_bytes=32 << 20),
+        compiler_params=pltpu.CompilerParams(vmem_limit_bytes=GRANT // 2 if last else GRANT),
         name="to_lags_last" if last else "to_lags_first",
     )(
         mine.reshape(rows, depth),
@@ -359,9 +373,7 @@
     flags = mask.reshape(BLOCKS, WIDE)
     spectra = spectra.reshape(CH, 2, F)
     source = source_rows(tm_index, flags, spectra)
-    gathered = lax.all_gather(source, "chan", axis=0, tiled=True)
-    flags, _ = lax.optimization_barrier((flags, source))
-    send_a, send_b = pack(flags, spectra)
+    send_a, send_b = pack(flags, source, spectra)
     send_a, zero = lax.optimization_barrier((send_a, jnp.int32(0)))
     tables_a = lag_table(0, BINS_A, zero)
     tables_b = lag_table(BINS_A, BINS_B, zero)
@@ -369,14 +381,14 @@
     exchange = lambda x: lax.all_to_all(x, "chan", split_axis=0, concat_axis=0, tiled=True)
     got_a = exchange(send_a)
     got_b = exchange(send_b)
-    theirs_a, mine_a, picks, count = first_sums(got_a, gathered)
+    theirs_a, mine_a, picks, count = first_sums(got_a)
     from_a = swap(theirs_a)
     count_from = swap(count)
     lagged = to_lags(mine_a, from_a, tables_a)
     got_b, lagged = lax.optimization_barrier((got_b, lagged))
-    theirs_b = second_sums(got_b, gathered, picks, 0, jnp.bfloat16)
+    theirs_b = second_sums(got_b, picks, 0, jnp.bfloat16)
     from_b = swap(theirs_b)
-    mine_b = second_sums(got_b, gathered, picks, SB, jnp.float32)
+    mine_b = second_sums(got_b, picks, SB, jnp.float32)
     lagged = to_lags(mine_b, from_b, tables_b, lagged, (count, count_from))
     return lagged.reshape(SB, WIDE, LAGS)
 

time: 314 us -> 265 us (0.84)
  waiting for transfers between devices: 147 us -> 113 us
  between operations: 13.6 us -> 0.11 us
  local copies, waits for them, and re-layouts: 10.2 us -> 5.98 us
    all_gather x1 -> x0, waiting for transfers between devices: 57.3 us -> none  [local(): gathered = lax.all_gather(source, 'chan', axis=0, tiled=True)]
    ppermute x3, waiting for transfers between devices: 15.5 us -> 30.6 us  [swap(): return lax.ppermute(x, 'tm', [(0, 1), (1, 0)])]
    all_to_all x2, waiting for transfers between devices: 73.3 us -> 81.9 us  [local(): lax.all_to_all(x, 'chan', split_axis=0, concat_axis=0, tiled=True)]
    unnamed x19 -> x15, local copies, waits for them, and re-layouts: 9.46 us -> 5.27 us
    pallas_call x2, Pallas kernels: 15.3 us -> 19.1 us  [to_lags(): pl.pallas_call(lags_last_kernel if last else lags_first_kernel, grid=(pl....]
    pallas_call x1, Pallas kernels: 21.6 us -> 18.1 us  [pack(): pl.pallas_call(pack_kernel, grid=(BLOCKS // PACK,), in_specs=[pl.BlockSpe...]
  transfers between devices with their start and end apart: 6 -> 5, of which waited for: 3 -> 2; matrix products, arithmetic and copies ran while one was open for 9% -> 10% of each run, Pallas kernels for 19% -> 25%
where the time goes in v3:
time: 265 us; the launch traced here: 262 us
  waiting for transfers between devices  113 us (43%)
  Pallas kernels  92 us (35%)
  other arithmetic  27.1 us (10%)
  starting transfers between devices  24.3 us (9%)
  local copies, waits for them, and re-layouts  5.98 us (2%)
    all_to_all x2, waiting for transfers between devices, local(): lax.all_to_all(x, 'chan', split_axis=0, concat_axis=0, tiled=True)  81.9 us
    ppermute x3, waiting for transfers between devices, swap(): return lax.ppermute(x, 'tm', [(0, 1), (1, 0)])  30.6 us
    pallas_call x1, Pallas kernels, first_sums(): pl.pallas_call(first_kernel, grid=(WINS // STEP_A,), in_specs=[pl.BlockSp...  29.9 us
    pallas_call x2, Pallas kernels, second_sums(): pl.pallas_call(functools.partial(second_kernel, first), grid=(WINS // STE...  23 us
    all_to_all x2, starting transfers between devices, local(): lax.all_to_all(x, 'chan', split_axis=0, concat_axis=0, tiled=True)  21.3 us
    cos x2, other arithmetic, lag_table(): table = jnp.concatenate([jnp.cos(angles), -jnp.sin(angles)], axis=0)  19.2 us
    pallas_call x2, Pallas kernels, to_lags(): pl.pallas_call(lags_last_kernel if last else lags_first_kernel, grid=(pl....  19.1 us
    pallas_call x1, Pallas kernels, pack(): pl.pallas_call(pack_kernel, grid=(BLOCKS // PACK,), in_specs=[pl.BlockSpe...  18.1 us
  transfers between devices with their start and end apart: 5, of which 2 were waited for; matrix products, arithmetic and copies ran while one was open for 10% of the time, Pallas kernels for 25%

profile of v3, /device:TPU:0, one launch (start us, length us, event | category | flops | bytes accessed | tf_op | source)
XLA Modules:
  0.0 262.0 jit_solution(5233006103751939761)
XLA Ops:
  0.0 0.5 broadcast.25
  0.5 1.5 reduce.3
  2.0 0.7 reshape.33.mask_ref
  2.7 2.0 source_rows.1.src_ref
  4.7 18.1 %whiten_pack.1 = (bf16[64,264,256]{2,1,0:T(8,128)(2,1)}, bf16[64,256,128]{2,1,0:T(8,128)(2,1)}) custom-call(s32[64,160]{1,0:T(8,128)} %reshape.33.mask_ref, bf16[1,16,512]{2,1,0:T(8,128)(2,1)} %source_rows.1.src_ref, bf16[10240,2,384]{2,1,0:T(2,128)(2,1)} %bitcast.17, bf16[10240,2,384]{2,1,0:T(2,128)(2,1)} %bitcast.18, bf16[10240,2,384]{2,1,0:T(2,128)(2,1)} %bitcast.19), custom_call_target="tpu_custom_call" | custom-call | flops 4026531840 | bytes 30000000 | tf_op jit(solution)/shard_map/whiten_pack/pallas_call | solution.py:140
  22.8 11.6 %all-to-all-start.1 = ((bf16[64,264,256]{2,1,0:T(8,128)(2,1)}), bf16[64,264,256]{2,1,0:T(8,128)(2,1)}, u32[]{:S(2)}, u32[]{:S(2)}) async-start(bf16[64,264,256]{2,1,0:T(8,128)(2,1)} %get-tuple-element.24), calls=%async_computation.1 | async-start | bytes 17301504 | tf_op jit(solution)/shard_map/all_to_all | solution.py:381
  34.4 6.4 %fusion.12 = (f32[128,3001]{1,0:T(8,128)S(1)}, f32[128,3001]{1,0:T(8,128)S(1)}) fusion(s32[3001]{0:T(1024)S(1)} %iota_add_fusion, s32[128]{0:T(128)S(1)} %iota_add_fusion.2), kind=kLoop, calls=%fused_computation.24 | loop fusion | flops 3841280 | bytes 3085540 | tf_op jit(solution)/shard_map/cos | solution.py:362
  40.8 2.3 fusion.1
  43.1 12.8 %fusion.6 = (f32[256,3001]{1,0:T(8,128)S(1)}, f32[256,3001]{1,0:T(8,128)S(1)}) fusion(s32[3001]{0:T(1024)S(1)} %iota_add_fusion, s32[256]{0:T(256)S(1)} %iota_add_fusion.1), kind=kLoop, calls=%fused_computation.15 | loop fusion | flops 7682560 | bytes 6159076 | tf_op jit(solution)/shard_map/cos | solution.py:362
  55.9 4.0 %fusion = (bf16[512,3001]{1,0:T(8,128)(2,1)}, bf16[512,3001]{1,0:T(8,128)(2,1)}) fusion(f32[256,3001]{1,0:T(8,128)S(1)} %get-tuple-element.40, f32[256,3001]{1,0:T(8,128)S(1)} %get-tuple-element.39), kind=kLoop, calls=%fused_computation.2 | loop fusion | flops 7682560 | bytes 12292096 | tf_op jit(solution)/shard_map/convert_element_type | solution.py:364
  59.9 81.9 %all-to-all-done.1.got = bf16[64,264,256]{2,1,0:T(8,128)(2,1)} async-done(((bf16[64,264,256]{2,1,0:T(8,128)(2,1)}), bf16[64,264,256]{2,1,0:T(8,128)(2,1)}, u32[]{:S(2)}, u32[]{:S(2)}) %all-to-all-start.1) | async-done | bytes 8650784 | tf_op jit(solution)/shard_map/all_to_all | solution.py:381
  141.8 9.7 %all-to-all-start = ((bf16[64,256,128]{2,1,0:T(8,128)(2,1)}), bf16[64,256,128]{2,1,0:T(8,128)(2,1)}, u32[]{:S(2)}, u32[]{:S(2)}) async-start(bf16[64,256,128]{2,1,0:T(8,128)(2,1)} %get-tuple-element.23), calls=%async_computation | async-start | bytes 8388608 | tf_op jit(solution)/shard_map/all_to_all | solution.py:381
  151.5 29.9 %cross_sums_first.1 = (bf16[4,160,512]{2,1,0:T(8,128)(2,1)}, f32[4,160,512]{2,1,0:T(8,128)}, bf16[64,160,128]{2,1,0:T(8,128)(2,1)}, f32[160,128]{1,0:T(8,128)}) custom-call(bf16[64,264,256]{2,1,0:T(8,128)(2,1)} %all-to-all-done.1.got), custom_call_target="tpu_custom_call" | custom-call | flops 30000001024 | bytes 20000000 | tf_op jit(solution)/shard_map/cross_sums_first/pallas_call | solution.py:229
  181.4 1.0 collective-permute-start
  182.4 1.0 collective-permute-start.2
  183.5 30.6 %collective-permute-done = bf16[4,160,512]{2,1,0:T(8,128)(2,1)S(1)} collective-permute-done((bf16[4,160,512]{2,1,0:T(8,128)(2,1)}, bf16[4,160,512]{2,1,0:T(8,128)(2,1)S(1)}, u32[]{:S(2)}, u32[]{:S(2)}) %collective-permute-start) | collective-permute-done | bytes 655392 | tf_op jit(solution)/shard_map/ppermute | solution.py:368
  214.1 0.0 copy-start.4
  214.1 0.8 copy-done.4
  214.9 11.4 %to_lags_first.1.before = f32[640,3001]{1,0:T(8,128)} custom-call(f32[640,512]{1,0:T(8,128)} %bitcast.21, bf16[640,512]{1,0:T(8,128)(2,1)} %bitcast.20, bf16[512,3001]{1,0:T(8,128)(2,1)} %get-tuple-element.27.table_high, bf16[512,3001]{1,0:T(8,128)(2,1)} %get-tuple-element.28.table_low), custom_call_target="tpu_custom_call" | custom-call | flops 5900206080 | bytes 7682560 | tf_op jit(solution)/shard_map/to_lags_first/pallas_call | solution.py:337
  226.3 0.0 all-to-all-done.got
  226.3 0.0 slice-start
  226.3 11.5 %cross_sums_second.3 = bf16[4,160,256]{2,1,0:T(8,128)(2,1)} custom-call(bf16[64,256,128]{2,1,0:T(8,128)(2,1)} %all-to-all-done.got, bf16[64,160,128]{2,1,0:T(8,128)(2,1)} %get-tuple-element.30.picks), custom_call_target="tpu_custom_call" | custom-call | flops 8000000000 | bytes 8000000 | tf_op jit(solution)/shard_map/cross_sums_second/pallas_call | solution.py:275
  237.8 0.0 slice-start.1
  237.8 0.0 copy-start.3
  237.8 1.0 collective-permute-start.1
  238.8 11.5 %cross_sums_second.2 = f32[4,160,256]{2,1,0:T(8,128)} custom-call(bf16[64,256,128]{2,1,0:T(8,128)(2,1)} %all-to-all-done.got, bf16[64,160,128]{2,1,0:T(8,128)(2,1)} %get-tuple-element.30.picks), custom_call_target="tpu_custom_call" | custom-call | flops 8000000000 | bytes 8000000 | tf_op jit(solution)/shard_map/cross_sums_second/pallas_call | solution.py:275
  250.4 0.0 collective-permute-done.2.count_theirs
  250.4 0.0 collective-permute-done.1
  250.4 0.0 slice-done
  250.4 0.0 slice-done.1
  250.4 0.0 copy-done.3
  250.4 0.0 copy-start
  250.4 1.4 copy-done
  251.8 0.0 copy-start.1
  251.8 1.4 copy-done.1
  253.2 0.0 copy-start.2
  253.2 1.1 copy-done.2
  254.3 7.7 %to_lags_last.1 = f32[640,3001]{1,0:T(8,128)} custom-call(f32[640,256]{1,0:T(8,128)S(1)} %bitcast.9, bf16[640,256]{1,0:T(8,128)(2,1)S(1)} %bitcast.10, bf16[256,3001]{1,0:T(8,128)(2,1)S(1)} %copy-done.1, bf16[256,3001]{1,0:T(8,128)(2,1)S(1)} %copy-done, f32[640,3001]{1,0:T(8,128)S(1)} %bitcast.8, f32[160,128]{1,0:T(8,128)S(1)} %copy-done.3, ...), custom_call_target="tpu_custom_call" | custom-call | flops 2950103040 | bytes 15365120 | tf_op jit(solution)/shard_map/to_lags_last/pallas_call | solution.py:337
  (4 shorter events, 0.0 us)
Async XLA Ops:
  22.8 119.1 %all-to-all-start.1 = ((bf16[64,264,256]{2,1,0:T(8,128)(2,1)}), bf16[64,264,256]{2,1,0:T(8,128)(2,1)}, u32[]{:S(2)}, u32[]{:S(2)}) async-start(bf16[64,264,256]{2,1,0:T(8,128)(2,1)} %get-tuple-element.24), calls=%async_computation.1 | async-start | bytes 17301504 | tf_op jit(solution)/shard_map/all_to_all | solution.py:381
  141.8 84.5 %all-to-all-start = ((bf16[64,256,128]{2,1,0:T(8,128)(2,1)}), bf16[64,256,128]{2,1,0:T(8,128)(2,1)}, u32[]{:S(2)}, u32[]{:S(2)}) async-start(bf16[64,256,128]{2,1,0:T(8,128)(2,1)} %get-tuple-element.23), calls=%async_computation | async-start | bytes 8388608 | tf_op jit(solution)/shard_map/all_to_all | solution.py:381
  181.4 32.6 %collective-permute-start = (bf16[4,160,512]{2,1,0:T(8,128)(2,1)}, bf16[4,160,512]{2,1,0:T(8,128)(2,1)S(1)}, u32[]{:S(2)}, u32[]{:S(2)}) collective-permute-start(bf16[4,160,512]{2,1,0:T(8,128)(2,1)} %get-tuple-element.26), channel_id=1, source_target_pairs={{0,1},{1,0},{2,3},{3,2},{4,5},{5,4},{6,7},{7,6},{8,9},{9,8},{10,11... | collective-permute-start | bytes 1966088 | tf_op jit(solution)/shard_map/ppermute | solution.py:368
  182.4 68.0 %collective-permute-start.2 = (f32[160,128]{1,0:T(8,128)}, f32[160,128]{1,0:T(8,128)}, u32[]{:S(2)}, u32[]{:S(2)}) collective-permute-start(f32[160,128]{1,0:T(8,128)} %get-tuple-element.34.count), channel_id=1, source_target_pairs={{0,1},{1,0},{2,3},{3,2},{4,5},{5,4},{6,7},{7,6},{8,9},{9,8},{10,11... | collective-permute-start | bytes 245768 | tf_op jit(solution)/shard_map/ppermute | solution.py:368
  214.1 0.9 copy-start.4
  226.3 24.1 %slice-start = ((s8[7864320]{0:T(1024)(128)(4,1)}), s8[4194304]{0:T(1024)(128)(4,1)S(1)}, s32[]{:S(2)}) async-start(s8[7864320]{0:T(1024)(128)(4,1)} %bitcast.7), calls=%async_computation.2 | async-start | bytes 8388608
  237.8 12.6 %slice-start.1 = ((s8[7864320]{0:T(1024)(128)(4,1)}), s8[3670016]{0:T(1024)(128)(4,1)S(1)}, s32[]{:S(2)}) async-start(s8[7864320]{0:T(1024)(128)(4,1)} %bitcast.7), calls=%async_computation.3 | async-start | bytes 7340032
  237.8 12.6 %copy-start.3 = (f32[160,128]{1,0:T(8,128)S(1)}, f32[160,128]{1,0:T(8,128)}, u32[]{:S(2)}) copy-start(f32[160,128]{1,0:T(8,128)} %get-tuple-element.34.count) | copy-start | bytes 245764
  237.8 12.6 %collective-permute-start.1 = (bf16[4,160,256]{2,1,0:T(8,128)(2,1)}, bf16[4,160,256]{2,1,0:T(8,128)(2,1)S(1)}, u32[]{:S(2)}, u32[]{:S(2)}) collective-permute-start(bf16[4,160,256]{2,1,0:T(8,128)(2,1)} %cross_sums_second.3), channel_id=1, source_target_pairs={{0,1},{1,0},{2,3},{3,2},{4,5},{5,4},{6,7},{7,6},{8,9},{9,8},{10,11... | collective-permute-start | bytes 983048 | tf_op jit(solution)/shard_map/ppermute | solution.py:368
  250.4 1.4 copy-start
  251.8 1.4 copy-start.1
  253.2 1.1 copy-start.2

commit v4 on v3

--- a/solution.py
+++ b/solution.py
@@ -26,9 +26,11 @@
 CAP = 120
 PACK = 8
 GRANT = 56 << 20
+LAG_GRANT = 44 << 20
 STEP_A = 16
 STEP_B = 16
-LAG_TILE = 512
+TALL = 32
+LAG_TILE = 1024
 
 
 def iota(shape, dim):
@@ -168,29 +170,34 @@
     held[win] = dot(pick, rows)
     real = rows[CAP:, :bins].astype(jnp.float32)
     imag = rows[CAP:, bins:].astype(jnp.float32)
-    src[win, :SRC] = real
-    src[win, SRC : 2 * SRC] = imag
-    src[win, 2 * SRC :] = real + imag
+    for k, rows in enumerate((real, imag, real + imag)):
+        for t in range(bins // 128):
+            src[win, t, k * SRC : (k + 1) * SRC] = rows[:, t * 128 : (t + 1) * 128]
 
 
 def correlate(held, src, total, sources, bins, steps):
     def group(i, _):
-        rows = pl.ds(pl.multiple_of(i * 8, 8), 8)
+        rows = [pl.ds(pl.multiple_of(i * TALL + r, 8), 8) for r in range(0, TALL, 8)]
         for t in range(0, bins, 128):
             lanes = [slice(k * bins + t, k * bins + t + 128) for k in range(3)]
-            sums = [[total[n, rows, at] for at in lanes] for n in range(len(sources))]
-            for win in range(steps):
-                b0, b1 = held[win, rows, lanes[0]], held[win, rows, lanes[1]]
-                for n, q in enumerate(sources):
-                    for k, b in enumerate((b0, b1, b0 - b1)):
-                        a = src[win, k * SRC + q : k * SRC + q + 1, lanes[0]]
-                        sums[n][k] += jnp.broadcast_to(a, (8, 128)) * b
-            for n in range(len(sources)):
-                for at, value in zip(lanes, sums[n]):
-                    total[n, rows, at] = value
+            for some in range(0, len(sources), SB):
+                sums = [[[total[some + n, row, at] for row in rows] for at in lanes] for n in range(SB)]
+                for win in range(steps):
+                    real = [held[win, row, lanes[0]] for row in rows]
+                    imag = [held[win, row, lanes[1]] for row in rows]
+                    less = [x - y for x, y in zip(real, imag)]
+                    for n in range(SB):
+                        for k, values in enumerate((real, imag, less)):
+                            a = src[win, t // 128, pl.ds(k * SRC + sources[some + n], 8, stride=0), :]
+                            for r, b in enumerate(values):
+                                sums[n][k][r] += a * b
+                for n in range(SB):
+                    for k, at in enumerate(lanes):
+                        for r, row in enumerate(rows):
+                            total[some + n, row, at] = sums[n][k][r]
         return 0
 
-    lax.fori_loop(0, WIDE // 8, group, 0)
+    lax.fori_loop(0, WIDE // TALL, group, 0)
 
 
 def store_sums(total, n, out, q, bins):
@@ -244,7 +251,7 @@
         ],
         scratch_shapes=[
             pltpu.VMEM((STEP_A, WIDE, 2 * BINS_A), jnp.float32),
-            pltpu.VMEM((STEP_A, 3 * SRC, BINS_A), jnp.float32),
+            pltpu.VMEM((STEP_A, BINS_A // 128, 3 * SRC, 128), jnp.float32),
             pltpu.VMEM((SRC, WIDE, 3 * BINS_A), jnp.float32),
         ],
         cost_estimate=pl.CostEstimate(flops=30_000_000_000, bytes_accessed=20_000_000, transcendentals=0),
@@ -283,7 +290,7 @@
         out_shape=jax.ShapeDtypeStruct(shape, dtype),
         scratch_shapes=[
             pltpu.VMEM((STEP_B, WIDE, 2 * BINS_B), jnp.float32),
-            pltpu.VMEM((STEP_B, 3 * SRC, BINS_B), jnp.float32),
+            pltpu.VMEM((STEP_B, BINS_B // 128, 3 * SRC, 128), jnp.float32),
             pltpu.VMEM((SB, WIDE, 3 * BINS_B), jnp.float32),
         ],
         cost_estimate=pl.CostEstimate(flops=8_000_000_000, bytes_accessed=8_000_000, transcendentals=0),
@@ -292,76 +299,50 @@
     )(got, picks)
 
 
-def split(x):
-    high = x.astype(jnp.bfloat16)
-    return high, (x - high.astype(jnp.float32)).astype(jnp.bfloat16)
-
-
-def three_dots(high, low, table_high, table_low):
-    t = table_high[...]
-    return dot(high[...], t) + (dot(low[...], t) + dot(high[...], table_low[...]))
-
-
-def load_sums(mine, theirs, high, low):
-    total = mine[...] + theirs[...].astype(jnp.float32)
-    h, rest = split(total)
-    high[...] = h
-    low[...] = rest
-
-
-def lags_first_kernel(mine, theirs, table_high, table_low, out, high, low):
+def lags_kernel(mine_a, from_a, mine_b, from_b, table, count, count_from, out, held, scale):
     @pl.when(pl.program_id(0) == 0)
     def _():
-        load_sums(mine, theirs, high, low)
-
-    out[...] = three_dots(high, low, table_high, table_low)
-
-
-def lags_last_kernel(mine, theirs, table_high, table_low, before, count, count_theirs, out, high, low, scale):
-    @pl.when(pl.program_id(0) == 0)
-    def _():
-        load_sums(mine, theirs, high, low)
+        for mine, got, at in ((mine_a, from_a, slice(0, 2 * BINS_A)), (mine_b, from_b, slice(2 * BINS_A, 2 * F))):
+            held[:, at] = (mine[...] + got[...].astype(jnp.float32)).astype(jnp.bfloat16)
         for q in range(SB):
-            pairs = count[:, SB + q : SB + q + 1] + count_theirs[:, q : q + 1]
+            pairs = count[:, SB + q : SB + q + 1] + count_from[:, q : q + 1]
             scale[q * WIDE : (q + 1) * WIDE] = jnp.broadcast_to(1.0 / jnp.maximum(pairs, 1.0), (WIDE, 128))
 
-    out[...] = (before[...] + three_dots(high, low, table_high, table_low)) * scale[:, 0:1]
-
-
-def to_lags(mine, theirs, tables, before=None, counts=()):
-    rows, depth = SB * WIDE, tables[0].shape[0]
-    tile = pl.BlockSpec((rows, LAG_TILE), lambda n: (0, n))
+    out[...] = dot(held[...], table[...]) * scale[:, 0:1]
+
+
+def to_lags(mine_a, from_a, mine_b, from_b, table, count, count_from):
+    rows = SB * WIDE
     full = lambda shape: pl.BlockSpec(shape, lambda n: (0, 0))
-    table = pl.BlockSpec((depth, LAG_TILE), lambda n: (0, n))
-    last = before is not None
-    return pl.pallas_call(
-        lags_last_kernel if last else lags_first_kernel,
+    sums = [full((rows, 2 * bins)) for bins in (BINS_A, BINS_A, BINS_B, BINS_B)]
+    tiled = pl.BlockSpec((2 * F, LAG_TILE), lambda n: (0, n))
+    return pl.pallas_call(
+        lags_kernel,
         grid=(pl.cdiv(LAGS, LAG_TILE),),
-        in_specs=[full((rows, depth)), full((rows, depth)), table, table]
-        + ([tile, full((WIDE, 128)), full((WIDE, 128))] if last else []),
-        out_specs=tile,
+        in_specs=[*sums, tiled, full((WIDE, 128)), full((WIDE, 128))],
+        out_specs=pl.BlockSpec((rows, LAG_TILE), lambda n: (0, n)),
         out_shape=jax.ShapeDtypeStruct((rows, LAGS), jnp.float32),
-        scratch_shapes=[pltpu.VMEM((rows, depth), jnp.bfloat16)] * 2
-        + ([pltpu.VMEM((rows, 128), jnp.float32)] if last else []),
-        cost_estimate=pl.CostEstimate(flops=6 * rows * depth * LAGS, bytes_accessed=4 * rows * LAGS * (2 if last else 1), transcendentals=0),
-        compiler_params=pltpu.CompilerParams(vmem_limit_bytes=GRANT // 2 if last else GRANT),
-        name="to_lags_last" if last else "to_lags_first",
-    )(
-        mine.reshape(rows, depth),
-        theirs.reshape(rows, depth),
-        *tables,
-        *((before, *counts) if last else ()),
-    )
-
-
-def lag_table(first_bin, bins, zero):
-    bin_index = F0 + first_bin + zero + jnp.arange(bins, dtype=jnp.int32)
+        scratch_shapes=[
+            pltpu.VMEM((rows, 2 * F), jnp.bfloat16),
+            pltpu.VMEM((rows, 128), jnp.float32),
+        ],
+        cost_estimate=pl.CostEstimate(flops=4 * rows * F * LAGS, bytes_accessed=4 * rows * LAGS * 2, transcendentals=0),
+        compiler_params=pltpu.CompilerParams(vmem_limit_bytes=LAG_GRANT),
+        name="to_lags",
+    )(*(x.reshape(rows, -1) for x in (mine_a, from_a, mine_b, from_b)), table, count, count_from)
+
+
+def lag_table(zero):
+    row = jnp.arange(2 * F, dtype=jnp.int32) + zero
+    last = row >= 2 * BINS_A
+    bins = jnp.where(last, BINS_B, BINS_A)
+    inside = jnp.where(last, row - 2 * BINS_A, row)
+    bin_index = F0 + jnp.where(last, BINS_A, 0) + inside % bins
     lag_index = jnp.arange(LAGS, dtype=jnp.int32) - MAXLAG
     phase_steps = jnp.mod(bin_index[:, None] * lag_index[None, :], NFFT)
     angles = phase_steps.astype(jnp.float32) * jnp.float32(2.0 * math.pi / NFFT)
-    table = jnp.concatenate([jnp.cos(angles), -jnp.sin(angles)], axis=0)
-    high = lax.reduce_precision(table, 8, 7)
-    return high.astype(jnp.bfloat16), (table - high).astype(jnp.bfloat16)
+    table = jnp.where((inside < bins)[:, None], jnp.cos(angles), -jnp.sin(angles))
+    return table.astype(jnp.bfloat16)
 
 
 def swap(x):
@@ -375,21 +356,18 @@
     source = source_rows(tm_index, flags, spectra)
     send_a, send_b = pack(flags, source, spectra)
     send_a, zero = lax.optimization_barrier((send_a, jnp.int32(0)))
-    tables_a = lag_table(0, BINS_A, zero)
-    tables_b = lag_table(BINS_A, BINS_B, zero)
-    send_b, tables_a, tables_b = lax.optimization_barrier((send_b, tables_a, tables_b))
+    table = lag_table(zero)
+    send_b, table = lax.optimization_barrier((send_b, table))
     exchange = lambda x: lax.all_to_all(x, "chan", split_axis=0, concat_axis=0, tiled=True)
     got_a = exchange(send_a)
     got_b = exchange(send_b)
     theirs_a, mine_a, picks, count = first_sums(got_a)
     from_a = swap(theirs_a)
     count_from = swap(count)
-    lagged = to_lags(mine_a, from_a, tables_a)
-    got_b, lagged = lax.optimization_barrier((got_b, lagged))
     theirs_b = second_sums(got_b, picks, 0, jnp.bfloat16)
     from_b = swap(theirs_b)
     mine_b = second_sums(got_b, picks, SB, jnp.float32)
-    lagged = to_lags(mine_b, from_b, tables_b, lagged, (count, count_from))
+    lagged = to_lags(mine_a, from_a, mine_b, from_b, table, count, count_from)
     return lagged.reshape(SB, WIDE, LAGS)
 
 

time: 265 us -> 235 us (0.89)
  waiting for transfers between devices: 113 us -> 90.6 us
  Pallas kernels: 92 us -> 74.2 us
  other arithmetic: 27.1 us -> 42.5 us
  local copies, waits for them, and re-layouts: 5.98 us -> 2.32 us
    convert_element_type x2 -> x1, other arithmetic: 6.31 us -> 40.8 us  [lag_table(): return table.astype(jnp.bfloat16)]
    ppermute x3, waiting for transfers between devices: 30.6 us -> 0.01 us  [swap(): return lax.ppermute(x, 'tm', [(0, 1), (1, 0)])]
    cos x2 -> x0, other arithmetic: 19.2 us -> none  [lag_table(): table = jnp.concatenate([jnp.cos(angles), -jnp.sin(angles)], axis=0)]
    pallas_call x2 -> x1, Pallas kernels: 19.1 us -> 6.25 us  [to_lags(): pl.pallas_call(lags_kernel, grid=(pl.cdiv(LAGS, LAG_TILE),), in_specs=[*s...]
    all_to_all x2, waiting for transfers between devices: 81.9 us -> 90.6 us  [local(): lax.all_to_all(x, 'chan', split_axis=0, concat_axis=0, tiled=True)]
    pallas_call x2, Pallas kernels: 23 us -> 18.9 us  [second_sums(): pl.pallas_call(functools.partial(second_kernel, first), grid=(WINS // STE...]
    unnamed x15 -> x11, local copies, waits for them, and re-layouts: 5.27 us -> 1.61 us
  transfers between devices with their start and end apart: 5 -> 5, of which waited for: 2 -> 2; matrix products, arithmetic and copies ran while one was open for 10% -> 17% of each run, Pallas kernels for 25% -> 20%
where the time goes in v4:
time: 235 us; the launch traced here: 234 us
  waiting for transfers between devices  90.6 us (39%)
  Pallas kernels  74.2 us (32%)
  other arithmetic  42.5 us (18%)
  starting transfers between devices  24.4 us (10%)
    all_to_all x2, waiting for transfers between devices, local(): lax.all_to_all(x, 'chan', split_axis=0, concat_axis=0, tiled=True)  90.6 us
    convert_element_type x1, other arithmetic, lag_table(): return table.astype(jnp.bfloat16)  40.8 us
    pallas_call x1, Pallas kernels, first_sums(): pl.pallas_call(first_kernel, grid=(WINS // STEP_A,), in_specs=[pl.BlockSp...  29 us
    all_to_all x2, starting transfers between devices, local(): lax.all_to_all(x, 'chan', split_axis=0, concat_axis=0, tiled=True)  21.3 us
    pallas_call x2, Pallas kernels, second_sums(): pl.pallas_call(functools.partial(second_kernel, first), grid=(WINS // STE...  18.9 us
    pallas_call x1, Pallas kernels, pack(): pl.pallas_call(pack_kernel, grid=(BLOCKS // PACK,), in_specs=[pl.BlockSpe...  18.1 us
    pallas_call x1, Pallas kernels, to_lags(): pl.pallas_call(lags_kernel, grid=(pl.cdiv(LAGS, LAG_TILE),), in_specs=[*s...  6.25 us
  transfers between devices with their start and end apart: 5, of which 2 were waited for; matrix products, arithmetic and copies ran while one was open for 17% of the time, Pallas kernels for 20%

profile of v4, /device:TPU:0, one launch (start us, length us, event | category | flops | bytes accessed | tf_op | source)
XLA Modules:
  0.0 234.1 jit_solution(18361561772449075024)
XLA Ops:
  0.0 0.5 broadcast.92
  0.5 1.5 reduce.3
  2.0 0.7 reshape.47.mask_ref
  2.7 2.0 source_rows.1.src_ref
  4.7 18.1 %whiten_pack.1 = (bf16[64,264,256]{2,1,0:T(8,128)(2,1)}, bf16[64,256,128]{2,1,0:T(8,128)(2,1)}) custom-call(s32[64,160]{1,0:T(8,128)} %reshape.47.mask_ref, bf16[1,16,512]{2,1,0:T(8,128)(2,1)} %source_rows.1.src_ref, bf16[10240,2,384]{2,1,0:T(2,128)(2,1)} %bitcast.19, bf16[10240,2,384]{2,1,0:T(2,128)(2,1)} %bitcast.20, bf16[10240,2,384]{2,1,0:T(2,128)(2,1)} %bitcast.21), custom_call_target="tpu_custom_call" | custom-call | flops 4026531840 | bytes 30000000 | tf_op jit(solution)/shard_map/whiten_pack/pallas_call | solution.py:142
  22.8 11.6 %all-to-all-start = ((bf16[64,264,256]{2,1,0:T(8,128)(2,1)}), bf16[64,264,256]{2,1,0:T(8,128)(2,1)}, u32[]{:S(2)}, u32[]{:S(2)}) async-start(bf16[64,264,256]{2,1,0:T(8,128)(2,1)} %get-tuple-element.16), calls=%async_computation | async-start | bytes 17301504 | tf_op jit(solution)/shard_map/all_to_all | solution.py:361
  34.4 0.1 fusion.6
  34.5 40.8 %select_convert_fusion.table = bf16[768,3001]{1,0:T(8,128)(2,1)} fusion(s32[3001]{0:T(1024)S(1)} %iota_add_fusion, s32[768]{0:T(1024)S(1)} %fusion.6, pred[768]{0:T(1024)(128)(4,1)S(1)} %select_compare_fusion), kind=kLoop, calls=%fused_computation.3 | loop fusion | flops 27657216 | bytes 4625380 | tf_op jit(solution)/shard_map/convert_element_type | solution.py:345
  75.3 66.6 %all-to-all-done.got = bf16[64,264,256]{2,1,0:T(8,128)(2,1)} async-done(((bf16[64,264,256]{2,1,0:T(8,128)(2,1)}), bf16[64,264,256]{2,1,0:T(8,128)(2,1)}, u32[]{:S(2)}, u32[]{:S(2)}) %all-to-all-start) | async-done | bytes 8650784 | tf_op jit(solution)/shard_map/all_to_all | solution.py:361
  141.9 9.7 %all-to-all-start.1 = ((bf16[64,256,128]{2,1,0:T(8,128)(2,1)}), bf16[64,256,128]{2,1,0:T(8,128)(2,1)}, u32[]{:S(2)}, u32[]{:S(2)}) async-start(bf16[64,256,128]{2,1,0:T(8,128)(2,1)} %get-tuple-element.21), calls=%async_computation.1 | async-start | bytes 8388608 | tf_op jit(solution)/shard_map/all_to_all | solution.py:361
  151.6 29.0 %cross_sums_first.1 = (bf16[4,160,512]{2,1,0:T(8,128)(2,1)}, f32[4,160,512]{2,1,0:T(8,128)}, bf16[64,160,128]{2,1,0:T(8,128)(2,1)}, f32[160,128]{1,0:T(8,128)}) custom-call(bf16[64,264,256]{2,1,0:T(8,128)(2,1)} %all-to-all-done.got), custom_call_target="tpu_custom_call" | custom-call | flops 30000001024 | bytes 20000000 | tf_op jit(solution)/shard_map/cross_sums_first/pallas_call | solution.py:236
  180.6 1.0 collective-permute-start
  181.6 24.1 %all-to-all-done.1.got = bf16[64,256,128]{2,1,0:T(8,128)(2,1)} async-done(((bf16[64,256,128]{2,1,0:T(8,128)(2,1)}), bf16[64,256,128]{2,1,0:T(8,128)(2,1)}, u32[]{:S(2)}, u32[]{:S(2)}) %all-to-all-start.1) | async-done | bytes 4194336 | tf_op jit(solution)/shard_map/all_to_all | solution.py:361
  205.7 0.0 copy-start.2
  205.7 9.2 %cross_sums_second.3 = bf16[4,160,256]{2,1,0:T(8,128)(2,1)} custom-call(bf16[64,256,128]{2,1,0:T(8,128)(2,1)} %all-to-all-done.1.got, bf16[64,160,128]{2,1,0:T(8,128)(2,1)} %get-tuple-element.22.picks), custom_call_target="tpu_custom_call" | custom-call | flops 8000000000 | bytes 8000000 | tf_op jit(solution)/shard_map/cross_sums_second/pallas_call | solution.py:282
  214.8 1.0 collective-permute-start.1
  215.9 0.0 slice-start
  215.9 0.0 copy-done.2
  215.9 0.0 slice-start.1
  215.9 0.0 copy-start
  215.9 1.1 collective-permute-start.2
  217.0 9.8 %cross_sums_second.2 = f32[4,160,256]{2,1,0:T(8,128)} custom-call(bf16[64,256,128]{2,1,0:T(8,128)(2,1)} %all-to-all-done.1.got, bf16[64,160,128]{2,1,0:T(8,128)(2,1)} %get-tuple-element.22.picks), custom_call_target="tpu_custom_call" | custom-call | flops 8000000000 | bytes 8000000 | tf_op jit(solution)/shard_map/cross_sums_second/pallas_call | solution.py:282
  226.7 0.0 collective-permute-done.2.count_from
  226.7 0.0 collective-permute-done.1
  226.7 0.0 collective-permute-done
  226.8 0.0 slice-done
  226.8 0.0 slice-done.1
  226.8 0.0 copy-done
  226.8 0.0 copy-start.1
  226.8 1.1 copy-done.1
  227.9 6.3 %to_lags.1 = f32[640,3001]{1,0:T(8,128)} custom-call(f32[640,512]{1,0:T(8,128)S(1)} %bitcast.9, bf16[640,512]{1,0:T(8,128)(2,1)S(1)} %bitcast.10, f32[640,256]{1,0:T(8,128)S(1)} %bitcast.11, bf16[640,256]{1,0:T(8,128)(2,1)S(1)} %bitcast.12, bf16[768,3001]{1,0:T(8,128)(2,1)S(1)} %bitcast.8, f32[160,128]{1,0:T(8,128)S(1)} %copy-done.2, ...), custom_call_target="tpu_custom_call" | custom-call | flops 2950103040 | bytes 15365120 | tf_op jit(solution)/shard_map/to_lags/pallas_call | solution.py:319
  (3 shorter events, 0.0 us)
Async XLA Ops:
  22.8 119.1 %all-to-all-start = ((bf16[64,264,256]{2,1,0:T(8,128)(2,1)}), bf16[64,264,256]{2,1,0:T(8,128)(2,1)}, u32[]{:S(2)}, u32[]{:S(2)}) async-start(bf16[64,264,256]{2,1,0:T(8,128)(2,1)} %get-tuple-element.16), calls=%async_computation | async-start | bytes 17301504 | tf_op jit(solution)/shard_map/all_to_all | solution.py:361
  141.9 63.8 %all-to-all-start.1 = ((bf16[64,256,128]{2,1,0:T(8,128)(2,1)}), bf16[64,256,128]{2,1,0:T(8,128)(2,1)}, u32[]{:S(2)}, u32[]{:S(2)}) async-start(bf16[64,256,128]{2,1,0:T(8,128)(2,1)} %get-tuple-element.21), calls=%async_computation.1 | async-start | bytes 8388608 | tf_op jit(solution)/shard_map/all_to_all | solution.py:361
  180.6 46.2 %collective-permute-start = (bf16[4,160,512]{2,1,0:T(8,128)(2,1)}, bf16[4,160,512]{2,1,0:T(8,128)(2,1)S(1)}, u32[]{:S(2)}, u32[]{:S(2)}) collective-permute-start(bf16[4,160,512]{2,1,0:T(8,128)(2,1)} %get-tuple-element.18), channel_id=1, source_target_pairs={{0,1},{1,0},{2,3},{3,2},{4,5},{5,4},{6,7},{7,6},{8,9},{9,8},{10,11... | collective-permute-start | bytes 1966088 | tf_op jit(solution)/shard_map/ppermute | solution.py:349
  205.7 10.2 %copy-start.2 = (f32[160,128]{1,0:T(8,128)S(1)}, f32[160,128]{1,0:T(8,128)}, u32[]{:S(2)}) copy-start(f32[160,128]{1,0:T(8,128)} %get-tuple-element.24.count) | copy-start | bytes 245764
  214.8 11.9 %collective-permute-start.1 = (bf16[4,160,256]{2,1,0:T(8,128)(2,1)}, bf16[4,160,256]{2,1,0:T(8,128)(2,1)S(1)}, u32[]{:S(2)}, u32[]{:S(2)}) collective-permute-start(bf16[4,160,256]{2,1,0:T(8,128)(2,1)} %cross_sums_second.3), channel_id=1, source_target_pairs={{0,1},{1,0},{2,3},{3,2},{4,5},{5,4},{6,7},{7,6},{8,9},{9,8},{10,11... | collective-permute-start | bytes 983048 | tf_op jit(solution)/shard_map/ppermute | solution.py:349
  215.9 10.9 %slice-start = ((s8[4718592]{0:T(1024)(128)(4,1)}), s8[4194304]{0:T(1024)(128)(4,1)S(1)}, s32[]{:S(2)}) async-start(s8[4718592]{0:T(1024)(128)(4,1)} %bitcast.7), calls=%async_computation.2 | async-start | bytes 8388608
  215.9 10.9 %slice-start.1 = ((s8[4718592]{0:T(1024)(128)(4,1)}), s8[524288]{0:T(1024)(128)(4,1)S(1)}, s32[]{:S(2)}) async-start(s8[4718592]{0:T(1024)(128)(4,1)} %bitcast.7), calls=%async_computation.3 | async-start | bytes 1048576
  215.9 10.9 %copy-start = (f32[4,160,512]{2,1,0:T(8,128)S(1)}, f32[4,160,512]{2,1,0:T(8,128)}, u32[]{:S(2)}) copy-start(f32[4,160,512]{2,1,0:T(8,128)} %get-tuple-element.17) | copy-start | bytes 3932164
  215.9 10.9 %collective-permute-start.2 = (f32[160,128]{1,0:T(8,128)S(1)}, f32[160,128]{1,0:T(8,128)S(1)}, u32[]{:S(2)}, u32[]{:S(2)}) collective-permute-start(f32[160,128]{1,0:T(8,128)S(1)} %copy-done.2), channel_id=1, source_target_pairs={{0,1},{1,0},{2,3},{3,2},{4,5},{5,4},{6,7},{7,6},{8,9},{9,8},{10,11... | collective-permute-start | bytes 245768 | tf_op jit(solution)/shard_map/ppermute | solution.py:349
  226.8 1.1 copy-start.1

commit v5 on v4

--- a/solution.py
+++ b/solution.py
@@ -19,6 +19,7 @@
 BLOCKS = 64
 WIDE = 160
 WINS = 64
+LINES = 80
 SLOTS = 128
 ROWS = 2 * SLOTS
 BINS_A = 256
@@ -45,22 +46,24 @@
     return jnp.dot(a, b, preferred_element_type=jnp.float32)
 
 
-def source_kernel(tm_ref, mask_ref, a0, a1, a2, b0, b1, b2, out):
-    middle = BLOCKS // 2
-    flags = mask_ref[...].astype(jnp.float32).astype(jnp.bfloat16)
+def source_kernel(tm_ref, mask_ref, a0, a1, a2, b0, b1, b2, out, flag_out):
+    middle = LINES // 2
     shift = SB * (1 - tm_ref[0])
-    lane = iota((WIDE, 128), 1)
-    row = iota((WIDE, 128), 0)
+    ones = lambda at: jnp.broadcast_to(mask_ref[at : at + 1, :], (16, 128)).astype(jnp.float32).astype(jnp.bfloat16)
+    flags_a, flags_b = ones(0), ones(middle)
+    lane = iota((128, 128), 1)
+    row = iota((128, 128), 0)
     source = (lane + shift) % SRC
-    first = dot(flags, one_hot((row == source % SB) & (source < SB) & (lane < SRC)))
-    second = dot(flags, one_hot((row == source % SB) & (source >= SB) & (lane < SRC)))
-    kept = dot(flags, one_hot(row == lane // 2))
+    here = (row == source % SB) & (lane < SRC)
+    flag_out[...] = (dot(flags_a, one_hot(here & (source < SB))) + dot(flags_b, one_hot(here & (source >= SB))))[:8]
+    twice = one_hot(row == lane // 2)
+    kept_a, kept_b = dot(flags_a, twice), dot(flags_b, twice)
     take = iota((2 * SRC, 16), 0)
     lane = iota((2 * SRC, 16), 1)
     source = (take % SRC + shift) % SRC
     hit = lane == 2 * (source % SB) + take // SRC
-    pick_a = one_hot(hit & (source < SB) & (kept[0:1, :16] > 0.5))
-    pick_b = one_hot(hit & (source >= SB) & (kept[middle : middle + 1, :16] > 0.5))
+    pick_a = one_hot(hit & (source < SB) & (kept_a[:, :16] > 0.5))
+    pick_b = one_hot(hit & (source >= SB) & (kept_b[:, :16] > 0.5))
     rows = [
         dot(pick_a, ra.reshape(16, 128)[...]) + dot(pick_b, rb.reshape(16, 128)[...])
         for ra, rb in ((a0, b0), (a1, b1), (a2, b2))
@@ -71,9 +74,6 @@
     factor = jnp.concatenate([factor, factor], axis=0)
     for k, r in enumerate(rows):
         out[0, :, k * 128 : (k + 1) * 128] = (r * factor).astype(jnp.bfloat16)
-    line = iota((2 * SRC, 128), 0)
-    flag_line = first[0:1] + second[middle : middle + 1]
-    out[0, :, F:] = jnp.where(line == 0, flag_line, 0.0).astype(jnp.bfloat16)
 
 
 def source_rows(tm_index, mask, spectra):
@@ -84,40 +84,48 @@
         grid=(1,),
         in_specs=[
             pl.BlockSpec(memory_space=pltpu.SMEM),
-            pl.BlockSpec((BLOCKS, WIDE), lambda i: (0, 0)),
+            pl.BlockSpec((LINES, 128), lambda i: (0, 0)),
             *[head(k, 0) for k in range(3)],
             *[head(k, middle) for k in range(3)],
         ],
-        out_specs=pl.BlockSpec((1, 2 * SRC, F + 128), lambda i: (0, 0, 0)),
-        out_shape=jax.ShapeDtypeStruct((1, 2 * SRC, F + 128), jnp.bfloat16),
+        out_specs=[
+            pl.BlockSpec((1, 2 * SRC, F), lambda i: (0, 0, 0)),
+            pl.BlockSpec((8, 128), lambda i: (0, 0)),
+        ],
+        out_shape=[
+            jax.ShapeDtypeStruct((1, 2 * SRC, F), jnp.bfloat16),
+            jax.ShapeDtypeStruct((8, 128), jnp.float32),
+        ],
         cost_estimate=pl.CostEstimate(flops=10_000_000, bytes_accessed=100_000, transcendentals=0),
         name="source_rows",
     )(tm_index, mask, *[spectra] * 6)
 
 
-def pack_kernel(mask_ref, src_ref, x0, x1, x2, send_a, send_b, slot_ref, key_ref):
+def pack_kernel(mask_ref, flag_ref, x0, x1, x2, send_a, send_b, slot_ref, key_ref):
     step = pl.program_id(0)
 
     @pl.when(step == 0)
     def _():
-        flags = mask_ref[...].astype(jnp.float32).astype(jnp.bfloat16)
+        lines = [mask_ref[pl.ds(k, LINES // 5, stride=5), :] for k in range(5)]
+        lines = jnp.concatenate(lines, axis=1).astype(jnp.float32)
         lane = iota((WIDE, 2 * WIDE), 1)
         row = iota((WIDE, 2 * WIDE), 0)
-        before = dot(flags, one_hot(row < lane // 2))
-        kept = dot(flags, one_hot(row == lane // 2))
-        part = (iota((BLOCKS, 2 * WIDE), 1) % 2).astype(jnp.float32)
-        slot_ref[...] = jnp.where(kept > 0.5, before + part * SLOTS, -1.0)
+        ahead_two, here_two = one_hot(row < lane // 2), one_hot(row == lane // 2)
+        part = (iota((LINES // 5, 2 * WIDE), 1) % 2).astype(jnp.float32)
         lane = iota((WIDE, BINS_A), 1)
         row = iota((WIDE, BINS_A), 0)
-        before = dot(flags, one_hot(row < lane))
-        key_ref[...] = jnp.where(dot(flags, one_hot(row == lane)) > 0.5, before, -1.0)
-
-    flag_line = src_ref[0, :1, F:].astype(jnp.float32)
+        ahead, here = one_hot(row < lane), one_hot(row == lane)
+        for m in range(4):
+            flags = lines[:, m * WIDE : (m + 1) * WIDE].astype(jnp.bfloat16)
+            slot_ref[m] = jnp.where(dot(flags, here_two) > 0.5, dot(flags, ahead_two) + part * SLOTS, -1.0)
+            key_ref[m] = jnp.where(dot(flags, here) > 0.5, dot(flags, ahead), -1.0)
+
+    flag_line = flag_ref[:1, :]
     flag_line = jnp.concatenate([flag_line, flag_line], axis=1)
     place = iota((ROWS, 2 * WIDE), 0).astype(jnp.float32).astype(jnp.bfloat16)
     for n in range(PACK):
-        block = step * PACK + n
-        slot = slot_ref[pl.ds(block, 1), :].astype(jnp.bfloat16)
+        four = pl.ds(step * (PACK // 4) + n // 4, 1)
+        slot = slot_ref[n % 4, four, :].astype(jnp.bfloat16)
         pick = jnp.where(place == slot, jnp.ones_like(place), jnp.zeros_like(place))
         at = pl.ds(n * 2 * WIDE, 2 * WIDE)
         band = jnp.concatenate([r.reshape(PACK * 2 * WIDE, 128)[at, :] for r in (x0, x1, x2)], axis=1)
@@ -127,49 +135,52 @@
         factor = lax.rsqrt(energy + 1e-06)
         real = (real * factor).astype(jnp.bfloat16)
         imag = (imag * factor).astype(jnp.bfloat16)
-        for out, lo, hi in ((send_a, 0, BINS_A), (send_b, BINS_A, F)):
-            out[n, :CAP] = real[:, lo:hi]
-            out[n, CAP:SLOTS] = src_ref[0, :SRC, lo:hi]
-            out[n, SLOTS : SLOTS + CAP] = imag[:, lo:hi]
-            out[n, SLOTS + CAP : ROWS] = src_ref[0, SRC:, lo:hi]
+        send_a[n, :CAP] = real[:, :BINS_A]
         line = iota((8, BINS_A), 0)
-        notes = jnp.where(line == 0, key_ref[pl.ds(block, 1), :], flag_line)
-        send_a[n, ROWS:] = notes.astype(jnp.bfloat16)
-
-
-def pack(mask, source, spectra):
+        notes = jnp.where(line == 0, key_ref[n % 4, four, :], flag_line)
+        send_a[n, CAP:SLOTS] = notes.astype(jnp.bfloat16)
+        send_a[n, SLOTS:] = imag[:, :BINS_A]
+        send_b[n, :CAP] = real[:, BINS_A:]
+        send_b[n, CAP:] = imag[:, BINS_A:]
+
+
+def pack(mask, flags, spectra):
     band = lambda k: pl.BlockSpec((PACK * WIDE, 2, 128), lambda b: (b, 0, k))
     return pl.pallas_call(
         pack_kernel,
         grid=(BLOCKS // PACK,),
         in_specs=[
-            pl.BlockSpec((BLOCKS, WIDE), lambda b: (0, 0)),
-            pl.BlockSpec((1, 2 * SRC, F + 128), lambda b: (0, 0, 0)),
+            pl.BlockSpec((LINES, 128), lambda b: (0, 0)),
+            pl.BlockSpec((8, 128), lambda b: (0, 0)),
             *[band(k) for k in range(3)],
         ],
         out_specs=[
-            pl.BlockSpec((PACK, ROWS + 8, BINS_A), lambda b: (b, 0, 0)),
-            pl.BlockSpec((PACK, ROWS, BINS_B), lambda b: (b, 0, 0)),
+            pl.BlockSpec((PACK, SLOTS + CAP, BINS_A), lambda b: (b, 0, 0)),
+            pl.BlockSpec((PACK, 2 * CAP, BINS_B), lambda b: (b, 0, 0)),
         ],
         out_shape=[
-            jax.ShapeDtypeStruct((BLOCKS, ROWS + 8, BINS_A), jnp.bfloat16),
-            jax.ShapeDtypeStruct((BLOCKS, ROWS, BINS_B), jnp.bfloat16),
+            jax.ShapeDtypeStruct((BLOCKS, SLOTS + CAP, BINS_A), jnp.bfloat16),
+            jax.ShapeDtypeStruct((BLOCKS, 2 * CAP, BINS_B), jnp.bfloat16),
         ],
         scratch_shapes=[
-            pltpu.VMEM((BLOCKS, 2 * WIDE), jnp.float32),
-            pltpu.VMEM((BLOCKS, BINS_A), jnp.float32),
+            pltpu.VMEM((4, BLOCKS // 4, 2 * WIDE), jnp.float32),
+            pltpu.VMEM((4, BLOCKS // 4, BINS_A), jnp.float32),
         ],
         cost_estimate=pl.CostEstimate(flops=2 * BLOCKS * ROWS * 2 * WIDE * F, bytes_accessed=30_000_000, transcendentals=0),
         compiler_params=pltpu.CompilerParams(vmem_limit_bytes=GRANT),
         name="whiten_pack",
-    )(mask, source, *[spectra] * 3)
-
-
-def spread_slots(got, pick, held, src, win, bins):
-    rows = jnp.concatenate([got[win, :SLOTS, :], got[win, SLOTS:ROWS, :]], axis=1)
-    held[win] = dot(pick, rows)
-    real = rows[CAP:, :bins].astype(jnp.float32)
-    imag = rows[CAP:, bins:].astype(jnp.float32)
+    )(mask, flags, *[spectra] * 3)
+
+
+def place_of(me, win):
+    apart = jnp.bitwise_xor(me, win)
+    return (apart & 48) + ((apart >> 1) & 3) * 4 + ((apart >> 3) & 1) * 2 + (apart & 1)
+
+
+def spread_slots(real, imag, source, pick, held, src, win, bins):
+    held[win] = dot(pick, jnp.concatenate([real, imag], axis=1))
+    real = source[:SRC].astype(jnp.float32)
+    imag = source[SRC:].astype(jnp.float32)
     for k, rows in enumerate((real, imag, real + imag)):
         for t in range(bins // 128):
             src[win, t, k * SRC : (k + 1) * SRC] = rows[:, t * 128 : (t + 1) * 128]
@@ -206,7 +217,7 @@
     out[q, :, bins:] = (r - p + m).astype(out.dtype)
 
 
-def first_kernel(got, theirs, mine, picks, count, held, src, total):
+def first_kernel(me, got, source, theirs, mine, picks, count, held, src, total):
     step = pl.program_id(0)
 
     @pl.when(step == 0)
@@ -215,12 +226,13 @@
         count[...] = jnp.zeros_like(count)
 
     for win in range(STEP_A):
-        notes = got[win, ROWS:, :].astype(jnp.float32)
+        notes = got[win, CAP:SLOTS, :].astype(jnp.float32)
         key = jnp.transpose(notes)[:WIDE, 0:1]
         pick = one_hot(iota((WIDE, SLOTS), 1) == key.astype(jnp.int32))
         picks[win] = pick
         count[...] += jnp.where(key > -0.5, 1.0, 0.0) * notes[1:2, :128]
-        spread_slots(got, pick, held, src, win, BINS_A)
+        rows = source[place_of(me[0], step * STEP_A + win), :, :BINS_A]
+        spread_slots(got[win, :CAP, :], got[win, SLOTS:, :], rows, pick[:, :CAP], held, src, win, BINS_A)
     correlate(held, src, total, range(SRC), BINS_A, STEP_A)
 
     @pl.when(step == pl.num_programs(0) - 1)
@@ -230,13 +242,17 @@
             store_sums(total, SB + q, mine, q, BINS_A)
 
 
-def first_sums(got):
+def first_sums(me, got, source):
     shape = (SB, WIDE, 2 * BINS_A)
     sums_spec = pl.BlockSpec(shape, lambda g: (0, 0, 0))
     return pl.pallas_call(
         first_kernel,
         grid=(WINS // STEP_A,),
-        in_specs=[pl.BlockSpec((STEP_A, ROWS + 8, BINS_A), lambda g: (g, 0, 0))],
+        in_specs=[
+            pl.BlockSpec(memory_space=pltpu.SMEM),
+            pl.BlockSpec((STEP_A, SLOTS + CAP, BINS_A), lambda g: (g, 0, 0)),
+            pl.BlockSpec((WINS, 2 * SRC, F), lambda g: (0, 0, 0)),
+        ],
         out_specs=[
             sums_spec,
             sums_spec,
@@ -257,10 +273,10 @@
         cost_estimate=pl.CostEstimate(flops=30_000_000_000, bytes_accessed=20_000_000, transcendentals=0),
         compiler_params=pltpu.CompilerParams(vmem_limit_bytes=GRANT),
         name="cross_sums_first",
-    )(got)
-
-
-def second_kernel(first, got, picks, out, held, src, total):
+    )(me, got, source)
+
+
+def second_kernel(first, me, got, source, picks, out, held, src, total):
     step = pl.program_id(0)
 
     @pl.when(step == 0)
@@ -268,7 +284,8 @@
         total[...] = jnp.zeros_like(total)
 
     for win in range(STEP_B):
-        spread_slots(got, picks[win], held, src, win, BINS_B)
+        rows = source[place_of(me[0], step * STEP_B + win), :, BINS_A:]
+        spread_slots(got[win, :CAP, :], got[win, CAP:, :], rows, picks[win, :, :CAP], held, src, win, BINS_B)
     correlate(held, src, total, range(first, first + SB), BINS_B, STEP_B)
 
     @pl.when(step == pl.num_programs(0) - 1)
@@ -277,13 +294,15 @@
             store_sums(total, q, out, q, BINS_B)
 
 
-def second_sums(got, picks, first, dtype):
+def second_sums(me, got, source, picks, first, dtype):
     shape = (SB, WIDE, 2 * BINS_B)
     return pl.pallas_call(
         functools.partial(second_kernel, first),
         grid=(WINS // STEP_B,),
         in_specs=[
-            pl.BlockSpec((STEP_B, ROWS, BINS_B), lambda g: (g, 0, 0)),
+            pl.BlockSpec(memory_space=pltpu.SMEM),
+            pl.BlockSpec((STEP_B, 2 * CAP, BINS_B), lambda g: (g, 0, 0)),
+            pl.BlockSpec((WINS, 2 * SRC, F), lambda g: (0, 0, 0)),
             pl.BlockSpec((STEP_B, WIDE, SLOTS), lambda g: (g, 0, 0)),
         ],
         out_specs=pl.BlockSpec(shape, lambda g: (0, 0, 0)),
@@ -296,7 +315,7 @@
         cost_estimate=pl.CostEstimate(flops=8_000_000_000, bytes_accessed=8_000_000, transcendentals=0),
         compiler_params=pltpu.CompilerParams(vmem_limit_bytes=GRANT),
         name="cross_sums_second",
-    )(got, picks)
+    )(me, got, source, picks)
 
 
 def lags_kernel(mine_a, from_a, mine_b, from_b, table, count, count_from, out, held, scale):
@@ -349,24 +368,38 @@
     return lax.ppermute(x, "tm", [(0, 1), (1, 0)])
 
 
+def gather_sources(rows):
+    def partner(i, bits, r):
+        for n, bit in enumerate(bits):
+            i ^= ((r >> n) & 1) << bit
+        return i
+
+    for bits in ((0, 3), (1, 2), (4, 5)):
+        steps = [[(i, partner(i, bits, r)) for i in range(BLOCKS)] for r in range(1, 4)]
+        rows = jnp.concatenate([rows, *[lax.ppermute(rows, "chan", step) for step in steps]], axis=0)
+    return rows
+
+
 def local(spectra, mask):
+    me = lax.axis_index("chan").astype(jnp.int32)[None]
     tm_index = lax.axis_index("tm").astype(jnp.int32)[None]
-    flags = mask.reshape(BLOCKS, WIDE)
+    mask = mask.reshape(LINES, 128)
     spectra = spectra.reshape(CH, 2, F)
-    source = source_rows(tm_index, flags, spectra)
-    send_a, send_b = pack(flags, source, spectra)
-    send_a, zero = lax.optimization_barrier((send_a, jnp.int32(0)))
+    source, flags = source_rows(tm_index, mask, spectra)
+    send_a, send_b = pack(mask, flags, spectra)
+    send_a, source, zero = lax.optimization_barrier((send_a, source, jnp.int32(0)))
     table = lag_table(zero)
-    send_b, table = lax.optimization_barrier((send_b, table))
+    source = gather_sources(source)
+    send_b, table, source = lax.optimization_barrier((send_b, table, source))
     exchange = lambda x: lax.all_to_all(x, "chan", split_axis=0, concat_axis=0, tiled=True)
     got_a = exchange(send_a)
     got_b = exchange(send_b)
-    theirs_a, mine_a, picks, count = first_sums(got_a)
+    theirs_a, mine_a, picks, count = first_sums(me, got_a, source)
     from_a = swap(theirs_a)
     count_from = swap(count)
-    theirs_b = second_sums(got_b, picks, 0, jnp.bfloat16)
+    theirs_b = second_sums(me, got_b, source, picks, 0, jnp.bfloat16)
     from_b = swap(theirs_b)
-    mine_b = second_sums(got_b, picks, SB, jnp.float32)
+    mine_b = second_sums(me, got_b, source, picks, SB, jnp.float32)
     lagged = to_lags(mine_a, from_a, mine_b, from_b, table, count, count_from)
     return lagged.reshape(SB, WIDE, LAGS)
 

time: 235 us -> 284 us (1.21)
  starting transfers between devices: 24.4 us -> 80.2 us
  waiting for transfers between devices: 90.6 us -> 86.4 us
    all_to_all x2, waiting for transfers between devices: 90.6 us -> 20.5 us  [local(): lax.all_to_all(x, 'chan', split_axis=0, concat_axis=0, tiled=True)]
    ppermute x0 -> x9, starting transfers between devices: none -> 58.5 us  [gather_sources(): lax.ppermute(rows, 'chan', step)]
    ppermute x0 -> x9, waiting for transfers between devices: none -> 54.4 us  [gather_sources(): lax.ppermute(rows, 'chan', step)]
    ppermute x3, waiting for transfers between devices: 0.01 us -> 11.5 us  [swap(): return lax.ppermute(x, 'tm', [(0, 1), (1, 0)])]
  transfers between devices with their start and end apart: 5 -> 14, of which waited for: 2 -> 7; matrix products, arithmetic and copies ran while one was open for 17% -> 14% of each run, Pallas kernels for 20% -> 17%
where the time goes in v5:
time: 284 us
  waiting for transfers between devices  86.4 us (30%)
  starting transfers between devices  80.2 us (28%)
  Pallas kernels  74.8 us (26%)
  other arithmetic  40.9 us (14%)
    ppermute x9, starting transfers between devices, gather_sources(): lax.ppermute(rows, 'chan', step)  58.5 us
    ppermute x9, waiting for transfers between devices, gather_sources(): lax.ppermute(rows, 'chan', step)  54.4 us
    convert_element_type x1, other arithmetic, lag_table(): return table.astype(jnp.bfloat16)  40.8 us
    pallas_call x1, Pallas kernels, first_sums(): pl.pallas_call(first_kernel, grid=(WINS // STEP_A,), in_specs=[pl.BlockSp...  29.2 us
    all_to_all x2, waiting for transfers between devices, local(): lax.all_to_all(x, 'chan', split_axis=0, concat_axis=0, tiled=True)  20.5 us
    pallas_call x2, Pallas kernels, second_sums(): pl.pallas_call(functools.partial(second_kernel, first), grid=(WINS // STE...  19.4 us
    all_to_all x2, starting transfers between devices, local(): lax.all_to_all(x, 'chan', split_axis=0, concat_axis=0, tiled=True)  18.6 us
    pallas_call x1, Pallas kernels, pack(): pl.pallas_call(pack_kernel, grid=(BLOCKS // PACK,), in_specs=[pl.BlockSpe...  18.1 us
  transfers between devices with their start and end apart: 14, of which 7 were waited for; matrix products, arithmetic and copies ran while one was open for 14% of the time, Pallas kernels for 17%

profile of v5, /device:TPU:0, one launch (start us, length us, event | category | flops | bytes accessed | tf_op | source)
XLA Modules:
  0.0 283.8 jit_solution(5632410109608200963)
XLA Ops:
  0.0 1.9 source_rows.1
  1.9 18.1 %whiten_pack.1 = (bf16[64,248,256]{2,1,0:T(8,128)(2,1)}, bf16[64,240,128]{2,1,0:T(8,128)(2,1)}) custom-call(s32[80,128]{1,0:T(8,128)} %bitcast.25, f32[8,128]{1,0:T(8,128)} %get-tuple-element.19.flag_ref, bf16[10240,2,384]{2,1,0:T(2,128)(2,1)} %bitcast.21, bf16[10240,2,384]{2,1,0:T(2,128)(2,1)} %bitcast.22, bf16[10240,2,384]{2,1,0:T(2,128)(2,1)} %bitcast.23), custom_call_target="tpu_custom_call" | custom-call | flops 4026531840 | bytes 30000000 | tf_op jit(solution)/shard_map/whiten_pack/pallas_call | solution.py:149
  19.9 0.0 copy-start.3
  19.9 11.7 %all-to-all-start = ((bf16[64,248,256]{2,1,0:T(8,128)(2,1)}), bf16[64,248,256]{2,1,0:T(8,128)(2,1)}, u32[]{:S(2)}, u32[]{:S(2)}) async-start(bf16[64,248,256]{2,1,0:T(8,128)(2,1)} %get-tuple-element.22), calls=%async_computation | async-start | bytes 16252928 | tf_op jit(solution)/shard_map/all_to_all | solution.py:394
  31.6 0.0 copy-done.3
  31.7 2.8 %collective-permute-start.2 = (bf16[1,16,384]{2,1,0:T(8,128)(2,1)S(1)}, bf16[1,16,384]{2,1,0:T(8,128)(2,1)S(1)}, u32[]{:S(2)}, u32[]{:S(2)}) collective-permute-start(bf16[1,16,384]{2,1,0:T(8,128)(2,1)S(1)} %copy-done.3), channel_id=1, source_target_pairs={{0,18},{2,16},{4,22},{6,20},{8,26},{10,24},{12,30},{14,28},{16,2},... | collective-permute-start | bytes 36872 | tf_op jit(solution)/shard_map/ppermute | solution.py:379
  34.5 0.4 collective-permute-start.1
  34.9 0.2 collective-permute-start
  35.1 0.1 fusion.6
  35.2 0.8 collective-permute-done
  36.1 24.7 %collective-permute-done.1 = bf16[1,16,384]{2,1,0:T(8,128)(2,1)S(1)} collective-permute-done((bf16[1,16,384]{2,1,0:T(8,128)(2,1)S(1)}, bf16[1,16,384]{2,1,0:T(8,128)(2,1)S(1)}, u32[]{:S(2)}, u32[]{:S(2)}) %collective-permute-start.1) | collective-permute-done | bytes 12320 | tf_op jit(solution)/shard_map/ppermute | solution.py:379
  60.8 0.0 collective-permute-done.2
  60.8 12.7 %collective-permute-start.3 = (bf16[4,16,384]{2,1,0:T(8,128)(2,1)S(1)}, bf16[4,16,384]{2,1,0:T(8,128)(2,1)S(1)}, u32[]{:S(2)}, u32[]{:S(2)}) collective-permute-start(bf16[4,16,384]{2,1,0:T(8,128)(2,1)S(1)} %get-tuple-element.41), channel_id=1, source_target_pairs={{0,4},{2,6},{4,0},{6,2},{8,12},{10,14},{12,8},{14,10},{16,20},{18,... | collective-permute-start | bytes 147464 | tf_op jit(solution)/shard_map/ppermute | solution.py:379
  73.5 35.7 %collective-permute-start.5 = (bf16[4,16,384]{2,1,0:T(8,128)(2,1)S(1)}, bf16[4,16,384]{2,1,0:T(8,128)(2,1)S(1)}, u32[]{:S(2)}, u32[]{:S(2)}) collective-permute-start(bf16[4,16,384]{2,1,0:T(8,128)(2,1)S(1)} %get-tuple-element.41), channel_id=1, source_target_pairs={{0,12},{2,14},{4,8},{6,10},{8,4},{10,6},{12,0},{14,2},{16,28},{18,... | collective-permute-start | bytes 147464 | tf_op jit(solution)/shard_map/ppermute | solution.py:379
  109.2 1.4 collective-permute-start.4
  110.7 18.8 %collective-permute-done.3 = bf16[4,16,384]{2,1,0:T(8,128)(2,1)S(1)} collective-permute-done((bf16[4,16,384]{2,1,0:T(8,128)(2,1)S(1)}, bf16[4,16,384]{2,1,0:T(8,128)(2,1)S(1)}, u32[]{:S(2)}, u32[]{:S(2)}) %collective-permute-start.3) | collective-permute-done | bytes 49184 | tf_op jit(solution)/shard_map/ppermute | solution.py:379
  129.5 3.2 %collective-permute-done.4 = bf16[4,16,384]{2,1,0:T(8,128)(2,1)S(1)} collective-permute-done((bf16[4,16,384]{2,1,0:T(8,128)(2,1)S(1)}, bf16[4,16,384]{2,1,0:T(8,128)(2,1)S(1)}, u32[]{:S(2)}, u32[]{:S(2)}) %collective-permute-start.4) | collective-permute-done | bytes 49184 | tf_op jit(solution)/shard_map/ppermute | solution.py:379
  132.8 0.0 collective-permute-done.5
  132.8 1.2 collective-permute-start.7
  134.0 3.4 %collective-permute-start.6 = (bf16[16,16,384]{2,1,0:T(8,128)(2,1)S(1)}, bf16[16,16,384]{2,1,0:T(8,128)(2,1)S(1)}, u32[]{:S(2)}, u32[]{:S(2)}) collective-permute-start(bf16[16,16,384]{2,1,0:T(8,128)(2,1)S(1)} %get-tuple-element.33), channel_id=1, source_target_pairs={{0,32},{2,34},{4,36},{6,38},{8,40},{10,42},{12,44},{14,46},{16,48}... | collective-permute-start | bytes 589832 | tf_op jit(solution)/shard_map/ppermute | solution.py:379
  137.4 40.8 %select_convert_fusion.table = bf16[768,3001]{1,0:T(8,128)(2,1)} fusion(s32[3001]{0:T(1024)S(1)} %iota_add_fusion, s32[768]{0:T(1024)S(1)} %fusion.6, pred[768]{0:T(1024)(128)(4,1)S(1)} %select_compare_fusion), kind=kLoop, calls=%fused_computation.3 | loop fusion | flops 27657216 | bytes 4625380 | tf_op jit(solution)/shard_map/convert_element_type | solution.py:364
  178.2 0.6 collective-permute-start.8
  178.8 0.0 collective-permute-done.6
  178.8 0.0 collective-permute-done.7
  178.9 6.8 %collective-permute-done.8 = bf16[16,16,384]{2,1,0:T(8,128)(2,1)S(1)} collective-permute-done((bf16[16,16,384]{2,1,0:T(8,128)(2,1)S(1)}, bf16[16,16,384]{2,1,0:T(8,128)(2,1)S(1)}, u32[]{:S(2)}, u32[]{:S(2)}) %collective-permute-start.8) | collective-permute-done | bytes 196640 | tf_op jit(solution)/shard_map/ppermute | solution.py:379
  185.7 0.0 copy-start.4
  185.7 0.0 all-to-all-done.got
  185.7 6.9 %all-to-all-start.1 = ((bf16[64,240,128]{2,1,0:T(8,128)(2,1)}), bf16[64,240,128]{2,1,0:T(8,128)(2,1)}, u32[]{:S(2)}, u32[]{:S(2)}) async-start(bf16[64,240,128]{2,1,0:T(8,128)(2,1)} %get-tuple-element.29), calls=%async_computation.1 | async-start | bytes 7864320 | tf_op jit(solution)/shard_map/all_to_all | solution.py:394
  192.6 0.0 copy-done.4
  192.6 29.2 %cross_sums_first.1 = (bf16[4,160,512]{2,1,0:T(8,128)(2,1)}, f32[4,160,512]{2,1,0:T(8,128)}, bf16[64,160,128]{2,1,0:T(8,128)(2,1)}, f32[160,128]{1,0:T(8,128)}) custom-call(s32[1]{0:T(128)} %bitcast.me, bf16[64,248,256]{2,1,0:T(8,128)(2,1)} %all-to-all-done.got, bf16[64,16,384]{2,1,0:T(8,128)(2,1)} %copy-done.4), custom_call_target="tpu_custom_call" | custom-call | flops 30000001024 | bytes 20000000 | tf_op jit(solution)/shard_map/cross_sums_first/pallas_call | solution.py:248
  221.7 1.0 collective-permute-start.11
  222.8 20.5 %all-to-all-done.1.got = bf16[64,240,128]{2,1,0:T(8,128)(2,1)} async-done(((bf16[64,240,128]{2,1,0:T(8,128)(2,1)}), bf16[64,240,128]{2,1,0:T(8,128)(2,1)}, u32[]{:S(2)}, u32[]{:S(2)}) %all-to-all-start.1) | async-done | bytes 3932192 | tf_op jit(solution)/shard_map/all_to_all | solution.py:394
  243.3 0.0 copy-start.5
  243.3 9.4 %cross_sums_second.3 = bf16[4,160,256]{2,1,0:T(8,128)(2,1)} custom-call(s32[1]{0:T(128)} %bitcast.me, bf16[64,240,128]{2,1,0:T(8,128)(2,1)} %all-to-all-done.1.got, bf16[64,16,384]{2,1,0:T(8,128)(2,1)} %copy-done.4, bf16[64,160,128]{2,1,0:T(8,128)(2,1)} %get-tuple-element.30.picks), custom_call_target="tpu_custom_call" | custom-call | flops 8000000000 | bytes 8000000 | tf_op jit(solution)/shard_map/cross_sums_second/pallas_call | solution.py:299
  252.7 1.0 collective-permute-start.10
  253.8 0.0 slice-start
  253.8 0.0 copy-done.5
  253.8 0.0 slice-start.1
  253.8 0.0 copy-start
  253.8 0.0 copy-start.2
  253.8 1.1 collective-permute-start.9
  254.9 10.0 %cross_sums_second.2 = f32[4,160,256]{2,1,0:T(8,128)} custom-call(s32[1]{0:T(128)} %bitcast.me, bf16[64,240,128]{2,1,0:T(8,128)(2,1)} %all-to-all-done.1.got, bf16[64,16,384]{2,1,0:T(8,128)(2,1)} %copy-done.4, bf16[64,160,128]{2,1,0:T(8,128)(2,1)} %get-tuple-element.30.picks), custom_call_target="tpu_custom_call" | custom-call | flops 8000000000 | bytes 8000000 | tf_op jit(solution)/shard_map/cross_sums_second/pallas_call | solution.py:299
  264.9 0.0 collective-permute-done.11.count_from
  264.9 0.0 collective-permute-done.10
  264.9 11.5 %collective-permute-done.9 = bf16[4,160,512]{2,1,0:T(8,128)(2,1)S(1)} collective-permute-done((bf16[4,160,512]{2,1,0:T(8,128)(2,1)S(1)}, bf16[4,160,512]{2,1,0:T(8,128)(2,1)S(1)}, u32[]{:S(2)}, u32[]{:S(2)}) %collective-permute-start.9) | collective-permute-done | bytes 655392 | tf_op jit(solution)/shard_map/ppermute | solution.py:368
  276.4 0.0 slice-done
  276.4 0.0 slice-done.1
  276.4 0.0 copy-done
  276.4 0.0 copy-done.2
  276.4 0.0 copy-start.1
  276.4 1.1 copy-done.1
  277.5 6.3 %to_lags.1 = f32[640,3001]{1,0:T(8,128)} custom-call(f32[640,512]{1,0:T(8,128)S(1)} %bitcast.11, bf16[640,512]{1,0:T(8,128)(2,1)S(1)} %bitcast.12, f32[640,256]{1,0:T(8,128)S(1)} %bitcast.13, bf16[640,256]{1,0:T(8,128)(2,1)S(1)} %bitcast.14, bf16[768,3001]{1,0:T(8,128)(2,1)S(1)} %bitcast.10, f32[160,128]{1,0:T(8,128)S(1)} %copy-done.2, ...), custom_call_target="tpu_custom_call" | custom-call | flops 2950103040 | bytes 15365120 | tf_op jit(solution)/shard_map/to_lags/pallas_call | solution.py:338
  (13 shorter events, 0.2 us)
Async XLA Ops:
  19.9 11.7 %copy-start.3 = (bf16[1,16,384]{2,1,0:T(8,128)(2,1)S(1)}, bf16[1,16,384]{2,1,0:T(8,128)(2,1)}, u32[]{:S(2)}) copy-start(bf16[1,16,384]{2,1,0:T(8,128)(2,1)} %get-tuple-element.25) | copy-start | bytes 36868
  19.9 165.8 %all-to-all-start = ((bf16[64,248,256]{2,1,0:T(8,128)(2,1)}), bf16[64,248,256]{2,1,0:T(8,128)(2,1)}, u32[]{:S(2)}, u32[]{:S(2)}) async-start(bf16[64,248,256]{2,1,0:T(8,128)(2,1)} %get-tuple-element.22), calls=%async_computation | async-start | bytes 16252928 | tf_op jit(solution)/shard_map/all_to_all | solution.py:394
  31.7 29.1 %collective-permute-start.2 = (bf16[1,16,384]{2,1,0:T(8,128)(2,1)S(1)}, bf16[1,16,384]{2,1,0:T(8,128)(2,1)S(1)}, u32[]{:S(2)}, u32[]{:S(2)}) collective-permute-start(bf16[1,16,384]{2,1,0:T(8,128)(2,1)S(1)} %copy-done.3), channel_id=1, source_target_pairs={{0,18},{2,16},{4,22},{6,20},{8,26},{10,24},{12,30},{14,28},{16,2},... | collective-permute-start | bytes 36872 | tf_op jit(solution)/shard_map/ppermute | solution.py:379
  34.5 26.3 %collective-permute-start.1 = (bf16[1,16,384]{2,1,0:T(8,128)(2,1)S(1)}, bf16[1,16,384]{2,1,0:T(8,128)(2,1)S(1)}, u32[]{:S(2)}, u32[]{:S(2)}) collective-permute-start(bf16[1,16,384]{2,1,0:T(8,128)(2,1)S(1)} %copy-done.3), channel_id=1, source_target_pairs={{0,16},{2,18},{4,20},{6,22},{8,24},{10,26},{12,28},{14,30},{16,0},... | collective-permute-start | bytes 36872 | tf_op jit(solution)/shard_map/ppermute | solution.py:379
  34.9 1.2 collective-permute-start
  60.8 68.7 %collective-permute-start.3 = (bf16[4,16,384]{2,1,0:T(8,128)(2,1)S(1)}, bf16[4,16,384]{2,1,0:T(8,128)(2,1)S(1)}, u32[]{:S(2)}, u32[]{:S(2)}) collective-permute-start(bf16[4,16,384]{2,1,0:T(8,128)(2,1)S(1)} %get-tuple-element.41), channel_id=1, source_target_pairs={{0,4},{2,6},{4,0},{6,2},{8,12},{10,14},{12,8},{14,10},{16,20},{18,... | collective-permute-start | bytes 147464 | tf_op jit(solution)/shard_map/ppermute | solution.py:379
  73.5 59.3 %collective-permute-start.5 = (bf16[4,16,384]{2,1,0:T(8,128)(2,1)S(1)}, bf16[4,16,384]{2,1,0:T(8,128)(2,1)S(1)}, u32[]{:S(2)}, u32[]{:S(2)}) collective-permute-start(bf16[4,16,384]{2,1,0:T(8,128)(2,1)S(1)} %get-tuple-element.41), channel_id=1, source_target_pairs={{0,12},{2,14},{4,8},{6,10},{8,4},{10,6},{12,0},{14,2},{16,28},{18,... | collective-permute-start | bytes 147464 | tf_op jit(solution)/shard_map/ppermute | solution.py:379
  109.2 23.5 %collective-permute-start.4 = (bf16[4,16,384]{2,1,0:T(8,128)(2,1)S(1)}, bf16[4,16,384]{2,1,0:T(8,128)(2,1)S(1)}, u32[]{:S(2)}, u32[]{:S(2)}) collective-permute-start(bf16[4,16,384]{2,1,0:T(8,128)(2,1)S(1)} %get-tuple-element.41), channel_id=1, source_target_pairs={{0,8},{2,10},{4,12},{6,14},{8,0},{10,2},{12,4},{14,6},{16,24},{18,... | collective-permute-start | bytes 147464 | tf_op jit(solution)/shard_map/ppermute | solution.py:379
  132.8 46.0 %collective-permute-start.7 = (bf16[16,16,384]{2,1,0:T(8,128)(2,1)S(1)}, bf16[16,16,384]{2,1,0:T(8,128)(2,1)S(1)}, u32[]{:S(2)}, u32[]{:S(2)}) collective-permute-start(bf16[16,16,384]{2,1,0:T(8,128)(2,1)S(1)} %get-tuple-element.33), channel_id=1, source_target_pairs={{0,64},{2,66},{4,68},{6,70},{8,72},{10,74},{12,76},{14,78},{16,80}... | collective-permute-start | bytes 589832 | tf_op jit(solution)/shard_map/ppermute | solution.py:379
  134.0 44.8 %collective-permute-start.6 = (bf16[16,16,384]{2,1,0:T(8,128)(2,1)S(1)}, bf16[16,16,384]{2,1,0:T(8,128)(2,1)S(1)}, u32[]{:S(2)}, u32[]{:S(2)}) collective-permute-start(bf16[16,16,384]{2,1,0:T(8,128)(2,1)S(1)} %get-tuple-element.33), channel_id=1, source_target_pairs={{0,32},{2,34},{4,36},{6,38},{8,40},{10,42},{12,44},{14,46},{16,48}... | collective-permute-start | bytes 589832 | tf_op jit(solution)/shard_map/ppermute | solution.py:379
  178.2 7.5 %collective-permute-start.8 = (bf16[16,16,384]{2,1,0:T(8,128)(2,1)S(1)}, bf16[16,16,384]{2,1,0:T(8,128)(2,1)S(1)}, u32[]{:S(2)}, u32[]{:S(2)}) collective-permute-start(bf16[16,16,384]{2,1,0:T(8,128)(2,1)S(1)} %get-tuple-element.33), channel_id=1, source_target_pairs={{0,96},{2,98},{4,100},{6,102},{8,104},{10,106},{12,108},{14,110},{... | collective-permute-start | bytes 589832 | tf_op jit(solution)/shard_map/ppermute | solution.py:379
  185.7 6.9 %copy-start.4 = (bf16[64,16,384]{2,1,0:T(8,128)(2,1)}, bf16[64,16,384]{2,1,0:T(8,128)(2,1)S(1)}, u32[]{:S(2)}) copy-start(bf16[64,16,384]{2,1,0:T(8,128)(2,1)S(1)} %constant_dynamic-update-slice_fusion.11.source) | copy-start | bytes 2359300
  185.7 57.6 %all-to-all-start.1 = ((bf16[64,240,128]{2,1,0:T(8,128)(2,1)}), bf16[64,240,128]{2,1,0:T(8,128)(2,1)}, u32[]{:S(2)}, u32[]{:S(2)}) async-start(bf16[64,240,128]{2,1,0:T(8,128)(2,1)} %get-tuple-element.29), calls=%async_computation.1 | async-start | bytes 7864320 | tf_op jit(solution)/shard_map/all_to_all | solution.py:394
  221.7 43.1 %collective-permute-start.11 = (f32[160,128]{1,0:T(8,128)}, f32[160,128]{1,0:T(8,128)S(1)}, u32[]{:S(2)}, u32[]{:S(2)}) collective-permute-start(f32[160,128]{1,0:T(8,128)} %get-tuple-element.32.count), channel_id=1, source_target_pairs={{0,1},{1,0},{2,3},{3,2},{4,5},{5,4},{6,7},{7,6},{8,9},{9,8},{10,11... | collective-permute-start | bytes 245768 | tf_op jit(solution)/shard_map/ppermute | solution.py:368
  243.3 10.5 %copy-start.5 = (bf16[4,160,512]{2,1,0:T(8,128)(2,1)S(1)}, bf16[4,160,512]{2,1,0:T(8,128)(2,1)}, u32[]{:S(2)}) copy-start(bf16[4,160,512]{2,1,0:T(8,128)(2,1)} %get-tuple-element.28) | copy-start | bytes 1966084
  252.7 12.1 %collective-permute-start.10 = (bf16[4,160,256]{2,1,0:T(8,128)(2,1)}, bf16[4,160,256]{2,1,0:T(8,128)(2,1)S(1)}, u32[]{:S(2)}, u32[]{:S(2)}) collective-permute-start(bf16[4,160,256]{2,1,0:T(8,128)(2,1)} %cross_sums_second.3), channel_id=1, source_target_pairs={{0,1},{1,0},{2,3},{3,2},{4,5},{5,4},{6,7},{7,6},{8,9},{9,8},{10,11... | collective-permute-start | bytes 983048 | tf_op jit(solution)/shard_map/ppermute | solution.py:368
  253.8 22.6 %slice-start = ((s8[4718592]{0:T(1024)(128)(4,1)}), s8[4194304]{0:T(1024)(128)(4,1)S(1)}, s32[]{:S(2)}) async-start(s8[4718592]{0:T(1024)(128)(4,1)} %bitcast.9), calls=%async_computation.2 | async-start | bytes 8388608
  253.8 22.6 %slice-start.1 = ((s8[4718592]{0:T(1024)(128)(4,1)}), s8[524288]{0:T(1024)(128)(4,1)S(1)}, s32[]{:S(2)}) async-start(s8[4718592]{0:T(1024)(128)(4,1)} %bitcast.9), calls=%async_computation.3 | async-start | bytes 1048576
  253.8 22.6 %copy-start = (f32[4,160,512]{2,1,0:T(8,128)S(1)}, f32[4,160,512]{2,1,0:T(8,128)}, u32[]{:S(2)}) copy-start(f32[4,160,512]{2,1,0:T(8,128)} %get-tuple-element.27) | copy-start | bytes 3932164
  253.8 22.6 %copy-start.2 = (f32[160,128]{1,0:T(8,128)S(1)}, f32[160,128]{1,0:T(8,128)}, u32[]{:S(2)}) copy-start(f32[160,128]{1,0:T(8,128)} %get-tuple-element.32.count) | copy-start | bytes 245764
  253.8 22.6 %collective-permute-start.9 = (bf16[4,160,512]{2,1,0:T(8,128)(2,1)S(1)}, bf16[4,160,512]{2,1,0:T(8,128)(2,1)S(1)}, u32[]{:S(2)}, u32[]{:S(2)}) collective-permute-start(bf16[4,160,512]{2,1,0:T(8,128)(2,1)S(1)} %copy-done.5), channel_id=1, source_target_pairs={{0,1},{1,0},{2,3},{3,2},{4,5},{5,4},{6,7},{7,6},{8,9},{9,8},{10,11... | collective-permute-start | bytes 1966088 | tf_op jit(solution)/shard_map/ppermute | solution.py:368
  276.4 1.1 copy-start.1

commit v6 on v4

--- a/solution.py
+++ b/solution.py
@@ -19,6 +19,7 @@
 BLOCKS = 64
 WIDE = 160
 WINS = 64
+LINES = 80
 SLOTS = 128
 ROWS = 2 * SLOTS
 BINS_A = 256
@@ -45,22 +46,24 @@
     return jnp.dot(a, b, preferred_element_type=jnp.float32)
 
 
-def source_kernel(tm_ref, mask_ref, a0, a1, a2, b0, b1, b2, out):
-    middle = BLOCKS // 2
-    flags = mask_ref[...].astype(jnp.float32).astype(jnp.bfloat16)
+def source_kernel(tm_ref, mask_ref, a0, a1, a2, b0, b1, b2, out, flag_out):
+    middle = LINES // 2
     shift = SB * (1 - tm_ref[0])
-    lane = iota((WIDE, 128), 1)
-    row = iota((WIDE, 128), 0)
+    ones = lambda at: jnp.broadcast_to(mask_ref[at : at + 1, :], (16, 128)).astype(jnp.float32).astype(jnp.bfloat16)
+    flags_a, flags_b = ones(0), ones(middle)
+    lane = iota((128, 128), 1)
+    row = iota((128, 128), 0)
     source = (lane + shift) % SRC
-    first = dot(flags, one_hot((row == source % SB) & (source < SB) & (lane < SRC)))
-    second = dot(flags, one_hot((row == source % SB) & (source >= SB) & (lane < SRC)))
-    kept = dot(flags, one_hot(row == lane // 2))
+    here = (row == source % SB) & (lane < SRC)
+    flag_out[...] = (dot(flags_a, one_hot(here & (source < SB))) + dot(flags_b, one_hot(here & (source >= SB))))[:8]
+    twice = one_hot(row == lane // 2)
+    kept_a, kept_b = dot(flags_a, twice), dot(flags_b, twice)
     take = iota((2 * SRC, 16), 0)
     lane = iota((2 * SRC, 16), 1)
     source = (take % SRC + shift) % SRC
     hit = lane == 2 * (source % SB) + take // SRC
-    pick_a = one_hot(hit & (source < SB) & (kept[0:1, :16] > 0.5))
-    pick_b = one_hot(hit & (source >= SB) & (kept[middle : middle + 1, :16] > 0.5))
+    pick_a = one_hot(hit & (source < SB) & (kept_a[:, :16] > 0.5))
+    pick_b = one_hot(hit & (source >= SB) & (kept_b[:, :16] > 0.5))
     rows = [
         dot(pick_a, ra.reshape(16, 128)[...]) + dot(pick_b, rb.reshape(16, 128)[...])
         for ra, rb in ((a0, b0), (a1, b1), (a2, b2))
@@ -71,9 +74,6 @@
     factor = jnp.concatenate([factor, factor], axis=0)
     for k, r in enumerate(rows):
         out[0, :, k * 128 : (k + 1) * 128] = (r * factor).astype(jnp.bfloat16)
-    line = iota((2 * SRC, 128), 0)
-    flag_line = first[0:1] + second[middle : middle + 1]
-    out[0, :, F:] = jnp.where(line == 0, flag_line, 0.0).astype(jnp.bfloat16)
 
 
 def source_rows(tm_index, mask, spectra):
@@ -84,40 +84,48 @@
         grid=(1,),
         in_specs=[
             pl.BlockSpec(memory_space=pltpu.SMEM),
-            pl.BlockSpec((BLOCKS, WIDE), lambda i: (0, 0)),
+            pl.BlockSpec((LINES, 128), lambda i: (0, 0)),
             *[head(k, 0) for k in range(3)],
             *[head(k, middle) for k in range(3)],
         ],
-        out_specs=pl.BlockSpec((1, 2 * SRC, F + 128), lambda i: (0, 0, 0)),
-        out_shape=jax.ShapeDtypeStruct((1, 2 * SRC, F + 128), jnp.bfloat16),
+        out_specs=[
+            pl.BlockSpec((1, 2 * SRC, F), lambda i: (0, 0, 0)),
+            pl.BlockSpec((8, 128), lambda i: (0, 0)),
+        ],
+        out_shape=[
+            jax.ShapeDtypeStruct((1, 2 * SRC, F), jnp.bfloat16),
+            jax.ShapeDtypeStruct((8, 128), jnp.float32),
+        ],
         cost_estimate=pl.CostEstimate(flops=10_000_000, bytes_accessed=100_000, transcendentals=0),
         name="source_rows",
     )(tm_index, mask, *[spectra] * 6)
 
 
-def pack_kernel(mask_ref, src_ref, x0, x1, x2, send_a, send_b, slot_ref, key_ref):
+def pack_kernel(mask_ref, src_ref, flag_ref, x0, x1, x2, send_a, send_b, slot_ref, key_ref):
     step = pl.program_id(0)
 
     @pl.when(step == 0)
     def _():
-        flags = mask_ref[...].astype(jnp.float32).astype(jnp.bfloat16)
+        lines = [mask_ref[pl.ds(k, LINES // 5, stride=5), :] for k in range(5)]
+        lines = jnp.concatenate(lines, axis=1).astype(jnp.float32)
         lane = iota((WIDE, 2 * WIDE), 1)
         row = iota((WIDE, 2 * WIDE), 0)
-        before = dot(flags, one_hot(row < lane // 2))
-        kept = dot(flags, one_hot(row == lane // 2))
-        part = (iota((BLOCKS, 2 * WIDE), 1) % 2).astype(jnp.float32)
-        slot_ref[...] = jnp.where(kept > 0.5, before + part * SLOTS, -1.0)
+        ahead_two, here_two = one_hot(row < lane // 2), one_hot(row == lane // 2)
+        part = (iota((LINES // 5, 2 * WIDE), 1) % 2).astype(jnp.float32)
         lane = iota((WIDE, BINS_A), 1)
         row = iota((WIDE, BINS_A), 0)
-        before = dot(flags, one_hot(row < lane))
-        key_ref[...] = jnp.where(dot(flags, one_hot(row == lane)) > 0.5, before, -1.0)
-
-    flag_line = src_ref[0, :1, F:].astype(jnp.float32)
+        ahead, here = one_hot(row < lane), one_hot(row == lane)
+        for m in range(4):
+            flags = lines[:, m * WIDE : (m + 1) * WIDE].astype(jnp.bfloat16)
+            slot_ref[m] = jnp.where(dot(flags, here_two) > 0.5, dot(flags, ahead_two) + part * SLOTS, -1.0)
+            key_ref[m] = jnp.where(dot(flags, here) > 0.5, dot(flags, ahead), -1.0)
+
+    flag_line = flag_ref[:1, :]
     flag_line = jnp.concatenate([flag_line, flag_line], axis=1)
     place = iota((ROWS, 2 * WIDE), 0).astype(jnp.float32).astype(jnp.bfloat16)
     for n in range(PACK):
-        block = step * PACK + n
-        slot = slot_ref[pl.ds(block, 1), :].astype(jnp.bfloat16)
+        four = pl.ds(step * (PACK // 4) + n // 4, 1)
+        slot = slot_ref[n % 4, four, :].astype(jnp.bfloat16)
         pick = jnp.where(place == slot, jnp.ones_like(place), jnp.zeros_like(place))
         at = pl.ds(n * 2 * WIDE, 2 * WIDE)
         band = jnp.concatenate([r.reshape(PACK * 2 * WIDE, 128)[at, :] for r in (x0, x1, x2)], axis=1)
@@ -133,18 +141,19 @@
             out[n, SLOTS : SLOTS + CAP] = imag[:, lo:hi]
             out[n, SLOTS + CAP : ROWS] = src_ref[0, SRC:, lo:hi]
         line = iota((8, BINS_A), 0)
-        notes = jnp.where(line == 0, key_ref[pl.ds(block, 1), :], flag_line)
+        notes = jnp.where(line == 0, key_ref[n % 4, four, :], flag_line)
         send_a[n, ROWS:] = notes.astype(jnp.bfloat16)
 
 
-def pack(mask, source, spectra):
+def pack(mask, source, flags, spectra):
     band = lambda k: pl.BlockSpec((PACK * WIDE, 2, 128), lambda b: (b, 0, k))
     return pl.pallas_call(
         pack_kernel,
         grid=(BLOCKS // PACK,),
         in_specs=[
-            pl.BlockSpec((BLOCKS, WIDE), lambda b: (0, 0)),
-            pl.BlockSpec((1, 2 * SRC, F + 128), lambda b: (0, 0, 0)),
+            pl.BlockSpec((LINES, 128), lambda b: (0, 0)),
+            pl.BlockSpec((1, 2 * SRC, F), lambda b: (0, 0, 0)),
+            pl.BlockSpec((8, 128), lambda b: (0, 0)),
             *[band(k) for k in range(3)],
         ],
         out_specs=[
@@ -156,13 +165,13 @@
             jax.ShapeDtypeStruct((BLOCKS, ROWS, BINS_B), jnp.bfloat16),
         ],
         scratch_shapes=[
-            pltpu.VMEM((BLOCKS, 2 * WIDE), jnp.float32),
-            pltpu.VMEM((BLOCKS, BINS_A), jnp.float32),
+            pltpu.VMEM((4, BLOCKS // 4, 2 * WIDE), jnp.float32),
+            pltpu.VMEM((4, BLOCKS // 4, BINS_A), jnp.float32),
         ],
         cost_estimate=pl.CostEstimate(flops=2 * BLOCKS * ROWS * 2 * WIDE * F, bytes_accessed=30_000_000, transcendentals=0),
         compiler_params=pltpu.CompilerParams(vmem_limit_bytes=GRANT),
         name="whiten_pack",
-    )(mask, source, *[spectra] * 3)
+    )(mask, source, flags, *[spectra] * 3)
 
 
 def spread_slots(got, pick, held, src, win, bins):
@@ -277,7 +286,7 @@
             store_sums(total, q, out, q, BINS_B)
 
 
-def second_sums(got, picks, first, dtype):
+def second_sums(got, picks, first, dtype, grant):
     shape = (SB, WIDE, 2 * BINS_B)
     return pl.pallas_call(
         functools.partial(second_kernel, first),
@@ -294,7 +303,7 @@
             pltpu.VMEM((SB, WIDE, 3 * BINS_B), jnp.float32),
         ],
         cost_estimate=pl.CostEstimate(flops=8_000_000_000, bytes_accessed=8_000_000, transcendentals=0),
-        compiler_params=pltpu.CompilerParams(vmem_limit_bytes=GRANT),
+        compiler_params=pltpu.CompilerParams(vmem_limit_bytes=grant),
         name="cross_sums_second",
     )(got, picks)
 
@@ -351,10 +360,10 @@
 
 def local(spectra, mask):
     tm_index = lax.axis_index("tm").astype(jnp.int32)[None]
-    flags = mask.reshape(BLOCKS, WIDE)
+    mask = mask.reshape(LINES, 128)
     spectra = spectra.reshape(CH, 2, F)
-    source = source_rows(tm_index, flags, spectra)
-    send_a, send_b = pack(flags, source, spectra)
+    source, flags = source_rows(tm_index, mask, spectra)
+    send_a, send_b = pack(mask, source, flags, spectra)
     send_a, zero = lax.optimization_barrier((send_a, jnp.int32(0)))
     table = lag_table(zero)
     send_b, table = lax.optimization_barrier((send_b, table))
@@ -364,9 +373,10 @@
     theirs_a, mine_a, picks, count = first_sums(got_a)
     from_a = swap(theirs_a)
     count_from = swap(count)
-    theirs_b = second_sums(got_b, picks, 0, jnp.bfloat16)
+    got_b, count_from = lax.optimization_barrier((got_b, count_from))
+    theirs_b = second_sums(got_b, picks, 0, jnp.bfloat16, GRANT)
     from_b = swap(theirs_b)
-    mine_b = second_sums(got_b, picks, SB, jnp.float32)
+    mine_b = second_sums(got_b, picks, SB, jnp.float32, GRANT // 2)
     lagged = to_lags(mine_a, from_a, mine_b, from_b, table, count, count_from)
     return lagged.reshape(SB, WIDE, LAGS)
 

time: 235 us -> 229 us (0.974)
  transfers between devices with their start and end apart: 5 -> 5, of which waited for: 2 -> 2; matrix products, arithmetic and copies ran while one was open for 17% -> 18% of each run, Pallas kernels for 20% -> 21%
where the time goes in v6:
time: 229 us
  waiting for transfers between devices  89.6 us (39%)
  Pallas kernels  73.5 us (32%)
  other arithmetic  40.9 us (18%)
  starting transfers between devices  24.4 us (11%)
    all_to_all x2, waiting for transfers between devices, local(): lax.all_to_all(x, 'chan', split_axis=0, concat_axis=0, tiled=True)  89.6 us
    convert_element_type x1, other arithmetic, lag_table(): return table.astype(jnp.bfloat16)  40.8 us
    pallas_call x1, Pallas kernels, first_sums(): pl.pallas_call(first_kernel, grid=(WINS // STEP_A,), in_specs=[pl.BlockSp...  29 us
    all_to_all x2, starting transfers between devices, local(): lax.all_to_all(x, 'chan', split_axis=0, concat_axis=0, tiled=True)  21.3 us
    pallas_call x1, Pallas kernels, pack(): pl.pallas_call(pack_kernel, grid=(BLOCKS // PACK,), in_specs=[pl.BlockSpe...  18.2 us
    pallas_call x2, Pallas kernels, second_sums(): pl.pallas_call(functools.partial(second_kernel, first), grid=(WINS // STE...  18 us
    pallas_call x1, Pallas kernels, to_lags(): pl.pallas_call(lags_kernel, grid=(pl.cdiv(LAGS, LAG_TILE),), in_specs=[*s...  6.27 us
  transfers between devices with their start and end apart: 5, of which 2 were waited for; matrix products, arithmetic and copies ran while one was open for 18% of the time, Pallas kernels for 21%

profile of v6, /device:TPU:0, one launch (start us, length us, event | category | flops | bytes accessed | tf_op | source)
XLA Modules:
  0.0 228.5 jit_solution(17455770472233070549)
XLA Ops:
  0.0 1.9 source_rows.1
  1.9 18.2 %whiten_pack.1 = (bf16[64,264,256]{2,1,0:T(8,128)(2,1)}, bf16[64,256,128]{2,1,0:T(8,128)(2,1)}) custom-call(s32[80,128]{1,0:T(8,128)} %bitcast.24, bf16[1,16,384]{2,1,0:T(8,128)(2,1)} %get-tuple-element.19.src_ref, f32[8,128]{1,0:T(8,128)} %get-tuple-element.20.flag_ref, bf16[10240,2,384]{2,1,0:T(2,128)(2,1)} %bitcast.20, bf16[10240,2,384]{2,1,0:T(2,128)(2,1)} %bitcast.21, ...), custom_call_target="tpu_custom_call" | custom-call | flops 4026531840 | bytes 30000000 | tf_op jit(solution)/shard_map/whiten_pack/pallas_call | solution.py:150
  20.1 11.6 %all-to-all-start = ((bf16[64,264,256]{2,1,0:T(8,128)(2,1)}), bf16[64,264,256]{2,1,0:T(8,128)(2,1)}, u32[]{:S(2)}, u32[]{:S(2)}) async-start(bf16[64,264,256]{2,1,0:T(8,128)(2,1)} %get-tuple-element.22), calls=%async_computation | async-start | bytes 17301504 | tf_op jit(solution)/shard_map/all_to_all | solution.py:370
  31.7 0.1 fusion.6
  31.8 40.8 %select_convert_fusion.table = bf16[768,3001]{1,0:T(8,128)(2,1)} fusion(s32[3001]{0:T(1024)S(1)} %iota_add_fusion, s32[768]{0:T(1024)S(1)} %fusion.6, pred[768]{0:T(1024)(128)(4,1)S(1)} %select_compare_fusion), kind=kLoop, calls=%fused_computation.3 | loop fusion | flops 27657216 | bytes 4625380 | tf_op jit(solution)/shard_map/convert_element_type | solution.py:354
  72.6 66.6 %all-to-all-done.got = bf16[64,264,256]{2,1,0:T(8,128)(2,1)} async-done(((bf16[64,264,256]{2,1,0:T(8,128)(2,1)}), bf16[64,264,256]{2,1,0:T(8,128)(2,1)}, u32[]{:S(2)}, u32[]{:S(2)}) %all-to-all-start) | async-done | bytes 8650784 | tf_op jit(solution)/shard_map/all_to_all | solution.py:370
  139.2 9.7 %all-to-all-start.1 = ((bf16[64,256,128]{2,1,0:T(8,128)(2,1)}), bf16[64,256,128]{2,1,0:T(8,128)(2,1)}, u32[]{:S(2)}, u32[]{:S(2)}) async-start(bf16[64,256,128]{2,1,0:T(8,128)(2,1)} %get-tuple-element.27), calls=%async_computation.1 | async-start | bytes 8388608 | tf_op jit(solution)/shard_map/all_to_all | solution.py:370
  148.9 29.0 %cross_sums_first.1 = (bf16[4,160,512]{2,1,0:T(8,128)(2,1)}, f32[4,160,512]{2,1,0:T(8,128)}, bf16[64,160,128]{2,1,0:T(8,128)(2,1)}, f32[160,128]{1,0:T(8,128)}) custom-call(bf16[64,264,256]{2,1,0:T(8,128)(2,1)} %all-to-all-done.got), custom_call_target="tpu_custom_call" | custom-call | flops 30000001024 | bytes 20000000 | tf_op jit(solution)/shard_map/cross_sums_first/pallas_call | solution.py:245
  177.9 1.0 collective-permute-start.1
  178.9 1.0 collective-permute-start
  180.0 23.1 %all-to-all-done.1.got = bf16[64,256,128]{2,1,0:T(8,128)(2,1)} async-done(((bf16[64,256,128]{2,1,0:T(8,128)(2,1)}), bf16[64,256,128]{2,1,0:T(8,128)(2,1)}, u32[]{:S(2)}, u32[]{:S(2)}) %all-to-all-start.1) | async-done | bytes 4194336 | tf_op jit(solution)/shard_map/all_to_all | solution.py:370
  203.0 0.0 collective-permute-done.1.count_from
  203.0 0.0 copy-start.2
  203.0 0.0 slice-start
  203.0 9.3 %cross_sums_second.3 = bf16[4,160,256]{2,1,0:T(8,128)(2,1)} custom-call(bf16[64,256,128]{2,1,0:T(8,128)(2,1)} %all-to-all-done.1.got, bf16[64,160,128]{2,1,0:T(8,128)(2,1)} %get-tuple-element.30.picks), custom_call_target="tpu_custom_call" | custom-call | flops 8000000000 | bytes 8000000 | tf_op jit(solution)/shard_map/cross_sums_second/pallas_call | solution.py:291
  212.3 0.0 slice-start.1
  212.3 0.0 copy-start
  212.3 0.0 copy-start.1
  212.3 1.1 collective-permute-start.2
  213.4 0.0 copy-done.2
  213.4 8.8 %cross_sums_second.2 = f32[4,160,256]{2,1,0:T(8,128)S(1)} custom-call(bf16[64,256,128]{2,1,0:T(8,128)(2,1)} %all-to-all-done.1.got, bf16[64,160,128]{2,1,0:T(8,128)(2,1)S(1)} %copy-done.2), custom_call_target="tpu_custom_call" | custom-call | flops 8000000000 | bytes 8000000 | tf_op jit(solution)/shard_map/cross_sums_second/pallas_call | solution.py:291
  222.2 0.0 collective-permute-done.2
  222.2 0.0 collective-permute-done
  222.2 0.0 slice-done
  222.2 0.0 slice-done.1
  222.2 0.0 copy-done
  222.2 0.0 copy-done.1
  222.3 6.3 %to_lags.1 = f32[640,3001]{1,0:T(8,128)} custom-call(f32[640,512]{1,0:T(8,128)S(1)} %bitcast.10, bf16[640,512]{1,0:T(8,128)(2,1)S(1)} %bitcast.11, f32[640,256]{1,0:T(8,128)S(1)} %bitcast.12, bf16[640,256]{1,0:T(8,128)(2,1)S(1)} %bitcast.13, bf16[768,3001]{1,0:T(8,128)(2,1)S(1)} %bitcast.9, f32[160,128]{1,0:T(8,128)S(1)} %copy-done.1, ...), custom_call_target="tpu_custom_call" | custom-call | flops 2950103040 | bytes 15365120 | tf_op jit(solution)/shard_map/to_lags/pallas_call | solution.py:328
  (3 shorter events, 0.0 us)
Async XLA Ops:
  20.1 119.1 %all-to-all-start = ((bf16[64,264,256]{2,1,0:T(8,128)(2,1)}), bf16[64,264,256]{2,1,0:T(8,128)(2,1)}, u32[]{:S(2)}, u32[]{:S(2)}) async-start(bf16[64,264,256]{2,1,0:T(8,128)(2,1)} %get-tuple-element.22), calls=%async_computation | async-start | bytes 17301504 | tf_op jit(solution)/shard_map/all_to_all | solution.py:370
  139.2 63.8 %all-to-all-start.1 = ((bf16[64,256,128]{2,1,0:T(8,128)(2,1)}), bf16[64,256,128]{2,1,0:T(8,128)(2,1)}, u32[]{:S(2)}, u32[]{:S(2)}) async-start(bf16[64,256,128]{2,1,0:T(8,128)(2,1)} %get-tuple-element.27), calls=%async_computation.1 | async-start | bytes 8388608 | tf_op jit(solution)/shard_map/all_to_all | solution.py:370
  177.9 25.1 %collective-permute-start.1 = (f32[160,128]{1,0:T(8,128)}, f32[160,128]{1,0:T(8,128)S(1)}, u32[]{:S(2)}, u32[]{:S(2)}) collective-permute-start(f32[160,128]{1,0:T(8,128)} %get-tuple-element.28.count), channel_id=1, source_target_pairs={{0,1},{1,0},{2,3},{3,2},{4,5},{5,4},{6,7},{7,6},{8,9},{9,8},{10,11... | collective-permute-start | bytes 245768 | tf_op jit(solution)/shard_map/ppermute | solution.py:358
  178.9 43.3 %collective-permute-start = (bf16[4,160,512]{2,1,0:T(8,128)(2,1)}, bf16[4,160,512]{2,1,0:T(8,128)(2,1)S(1)}, u32[]{:S(2)}, u32[]{:S(2)}) collective-permute-start(bf16[4,160,512]{2,1,0:T(8,128)(2,1)} %get-tuple-element.24), channel_id=1, source_target_pairs={{0,1},{1,0},{2,3},{3,2},{4,5},{5,4},{6,7},{7,6},{8,9},{9,8},{10,11... | collective-permute-start | bytes 1966088 | tf_op jit(solution)/shard_map/ppermute | solution.py:358
  203.0 10.4 %copy-start.2 = (bf16[64,160,128]{2,1,0:T(8,128)(2,1)S(1)}, bf16[64,160,128]{2,1,0:T(8,128)(2,1)}, u32[]{:S(2)}) copy-start(bf16[64,160,128]{2,1,0:T(8,128)(2,1)} %get-tuple-element.30.picks) | copy-start | bytes 7864324
  203.0 19.2 %slice-start = ((s8[4718592]{0:T(1024)(128)(4,1)}), s8[524288]{0:T(1024)(128)(4,1)S(1)}, s32[]{:S(2)}) async-start(s8[4718592]{0:T(1024)(128)(4,1)} %bitcast.8), calls=%async_computation.2 | async-start | bytes 1048576
  212.3 9.9 %slice-start.1 = ((s8[4718592]{0:T(1024)(128)(4,1)}), s8[4194304]{0:T(1024)(128)(4,1)S(1)}, s32[]{:S(2)}) async-start(s8[4718592]{0:T(1024)(128)(4,1)} %bitcast.8), calls=%async_computation.3 | async-start | bytes 8388608
  212.3 9.9 %copy-start = (f32[4,160,512]{2,1,0:T(8,128)S(1)}, f32[4,160,512]{2,1,0:T(8,128)}, u32[]{:S(2)}) copy-start(f32[4,160,512]{2,1,0:T(8,128)} %get-tuple-element.23) | copy-start | bytes 3932164
  212.3 9.9 %copy-start.1 = (f32[160,128]{1,0:T(8,128)S(1)}, f32[160,128]{1,0:T(8,128)}, u32[]{:S(2)}) copy-start(f32[160,128]{1,0:T(8,128)} %get-tuple-element.28.count) | copy-start | bytes 245764
  212.3 9.9 %collective-permute-start.2 = (bf16[4,160,256]{2,1,0:T(8,128)(2,1)}, bf16[4,160,256]{2,1,0:T(8,128)(2,1)S(1)}, u32[]{:S(2)}, u32[]{:S(2)}) collective-permute-start(bf16[4,160,256]{2,1,0:T(8,128)(2,1)} %cross_sums_second.3), channel_id=1, source_target_pairs={{0,1},{1,0},{2,3},{3,2},{4,5},{5,4},{6,7},{7,6},{8,9},{9,8},{10,11... | collective-permute-start | bytes 983048 | tf_op jit(solution)/shard_map/ppermute | solution.py:358

commit v7 on v6

--- a/solution.py
+++ b/solution.py
@@ -76,36 +76,13 @@
         out[0, :, k * 128 : (k + 1) * 128] = (r * factor).astype(jnp.bfloat16)
 
 
-def source_rows(tm_index, mask, spectra):
-    head = lambda k, at: pl.BlockSpec((8, 2, 128), lambda i: (at, 0, k))
-    middle = BLOCKS // 2 * WIDE // 8
-    return pl.pallas_call(
-        source_kernel,
-        grid=(1,),
-        in_specs=[
-            pl.BlockSpec(memory_space=pltpu.SMEM),
-            pl.BlockSpec((LINES, 128), lambda i: (0, 0)),
-            *[head(k, 0) for k in range(3)],
-            *[head(k, middle) for k in range(3)],
-        ],
-        out_specs=[
-            pl.BlockSpec((1, 2 * SRC, F), lambda i: (0, 0, 0)),
-            pl.BlockSpec((8, 128), lambda i: (0, 0)),
-        ],
-        out_shape=[
-            jax.ShapeDtypeStruct((1, 2 * SRC, F), jnp.bfloat16),
-            jax.ShapeDtypeStruct((8, 128), jnp.float32),
-        ],
-        cost_estimate=pl.CostEstimate(flops=10_000_000, bytes_accessed=100_000, transcendentals=0),
-        name="source_rows",
-    )(tm_index, mask, *[spectra] * 6)
-
-
-def pack_kernel(mask_ref, src_ref, flag_ref, x0, x1, x2, send_a, send_b, slot_ref, key_ref):
+def pack_kernel(tm_ref, mask_ref, *refs):
+    heads, (x0, x1, x2, send_a, send_b, slot_ref, key_ref, src_ref, flag_ref) = refs[:6], refs[6:]
     step = pl.program_id(0)
 
     @pl.when(step == 0)
     def _():
+        source_kernel(tm_ref, mask_ref, *heads, src_ref, flag_ref)
         lines = [mask_ref[pl.ds(k, LINES // 5, stride=5), :] for k in range(5)]
         lines = jnp.concatenate(lines, axis=1).astype(jnp.float32)
         lane = iota((WIDE, 2 * WIDE), 1)
@@ -117,12 +94,12 @@
         ahead, here = one_hot(row < lane), one_hot(row == lane)
         for m in range(4):
             flags = lines[:, m * WIDE : (m + 1) * WIDE].astype(jnp.bfloat16)
-            slot_ref[m] = jnp.where(dot(flags, here_two) > 0.5, dot(flags, ahead_two) + part * SLOTS, -1.0)
+            slot_ref[m] = jnp.where(dot(flags, here_two) > 0.5, dot(flags, ahead_two) + part * CAP, -1.0)
             key_ref[m] = jnp.where(dot(flags, here) > 0.5, dot(flags, ahead), -1.0)
 
     flag_line = flag_ref[:1, :]
     flag_line = jnp.concatenate([flag_line, flag_line], axis=1)
-    place = iota((ROWS, 2 * WIDE), 0).astype(jnp.float32).astype(jnp.bfloat16)
+    place = iota((2 * CAP, 2 * WIDE), 0).astype(jnp.float32).astype(jnp.bfloat16)
     for n in range(PACK):
         four = pl.ds(step * (PACK // 4) + n // 4, 1)
         slot = slot_ref[n % 4, four, :].astype(jnp.bfloat16)
@@ -130,7 +107,7 @@
         at = pl.ds(n * 2 * WIDE, 2 * WIDE)
         band = jnp.concatenate([r.reshape(PACK * 2 * WIDE, 128)[at, :] for r in (x0, x1, x2)], axis=1)
         rows = dot(pick, band)
-        real, imag = rows[:CAP], rows[SLOTS : SLOTS + CAP]
+        real, imag = rows[:CAP], rows[CAP:]
         energy = jnp.sum(real * real + imag * imag, axis=1, keepdims=True) / F
         factor = lax.rsqrt(energy + 1e-06)
         real = (real * factor).astype(jnp.bfloat16)
@@ -145,15 +122,18 @@
         send_a[n, ROWS:] = notes.astype(jnp.bfloat16)
 
 
-def pack(mask, source, flags, spectra):
+def pack(tm_index, mask, spectra):
+    head = lambda k, at: pl.BlockSpec((8, 2, 128), lambda b: (at, 0, k))
+    middle = BLOCKS // 2 * WIDE // 8
     band = lambda k: pl.BlockSpec((PACK * WIDE, 2, 128), lambda b: (b, 0, k))
     return pl.pallas_call(
         pack_kernel,
         grid=(BLOCKS // PACK,),
         in_specs=[
+            pl.BlockSpec(memory_space=pltpu.SMEM),
             pl.BlockSpec((LINES, 128), lambda b: (0, 0)),
-            pl.BlockSpec((1, 2 * SRC, F), lambda b: (0, 0, 0)),
-            pl.BlockSpec((8, 128), lambda b: (0, 0)),
+            *[head(k, 0) for k in range(3)],
+            *[head(k, middle) for k in range(3)],
             *[band(k) for k in range(3)],
         ],
         out_specs=[
@@ -167,11 +147,13 @@
         scratch_shapes=[
             pltpu.VMEM((4, BLOCKS // 4, 2 * WIDE), jnp.float32),
             pltpu.VMEM((4, BLOCKS // 4, BINS_A), jnp.float32),
+            pltpu.VMEM((1, 2 * SRC, F), jnp.bfloat16),
+            pltpu.VMEM((8, 128), jnp.float32),
         ],
         cost_estimate=pl.CostEstimate(flops=2 * BLOCKS * ROWS * 2 * WIDE * F, bytes_accessed=30_000_000, transcendentals=0),
         compiler_params=pltpu.CompilerParams(vmem_limit_bytes=GRANT),
         name="whiten_pack",
-    )(mask, source, flags, *[spectra] * 3)
+    )(tm_index, mask, *[spectra] * 9)
 
 
 def spread_slots(got, pick, held, src, win, bins):
@@ -362,8 +344,7 @@
     tm_index = lax.axis_index("tm").astype(jnp.int32)[None]
     mask = mask.reshape(LINES, 128)
     spectra = spectra.reshape(CH, 2, F)
-    source, flags = source_rows(tm_index, mask, spectra)
-    send_a, send_b = pack(mask, source, flags, spectra)
+    send_a, send_b = pack(tm_index, mask, spectra)
     send_a, zero = lax.optimization_barrier((send_a, jnp.int32(0)))
     table = lag_table(zero)
     send_b, table = lax.optimization_barrier((send_b, table))

time: 229 us -> 227 us (level)
  no operation moved by 1% of the time
where the time goes in v7:
time: 227 us
  waiting for transfers between devices  89.6 us (39%)
  Pallas kernels  71.6 us (32%)
  other arithmetic  40.9 us (18%)
  starting transfers between devices  24.4 us (11%)
    all_to_all x2, waiting for transfers between devices, local(): lax.all_to_all(x, 'chan', split_axis=0, concat_axis=0, tiled=True)  89.6 us
    convert_element_type x1, other arithmetic, lag_table(): return table.astype(jnp.bfloat16)  40.8 us
    pallas_call x1, Pallas kernels, first_sums(): pl.pallas_call(first_kernel, grid=(WINS // STEP_A,), in_specs=[pl.BlockSp...  29 us
    all_to_all x2, starting transfers between devices, local(): lax.all_to_all(x, 'chan', split_axis=0, concat_axis=0, tiled=True)  21.3 us
    pallas_call x1, Pallas kernels, pack(): pl.pallas_call(pack_kernel, grid=(BLOCKS // PACK,), in_specs=[pl.BlockSpe...  18.2 us
    pallas_call x2, Pallas kernels, second_sums(): pl.pallas_call(functools.partial(second_kernel, first), grid=(WINS // STE...  18 us
    pallas_call x1, Pallas kernels, to_lags(): pl.pallas_call(lags_kernel, grid=(pl.cdiv(LAGS, LAG_TILE),), in_specs=[*s...  6.27 us
  transfers between devices with their start and end apart: 5, of which 2 were waited for; matrix products, arithmetic and copies ran while one was open for 18% of the time, Pallas kernels for 21%

profile of v7, /device:TPU:0, one launch (start us, length us, event | category | flops | bytes accessed | tf_op | source)
XLA Modules:
  0.0 226.7 jit_solution(1397169442429494706)
XLA Ops:
  0.0 18.2 %whiten_pack.1 = (bf16[64,264,256]{2,1,0:T(8,128)(2,1)}, bf16[64,256,128]{2,1,0:T(8,128)(2,1)}) custom-call(s32[1]{0:T(128)} %bitcast.tm_ref, s32[80,128]{1,0:T(8,128)} %bitcast.23, bf16[10240,2,384]{2,1,0:T(2,128)(2,1)} %bitcast.14, bf16[10240,2,384]{2,1,0:T(2,128)(2,1)} %bitcast.15, bf16[10240,2,384]{2,1,0:T(2,128)(2,1)} %bitcast.16, ...), custom_call_target="tpu_custom_call" | custom-call | flops 4026531840 | bytes 30000000 | tf_op jit(solution)/shard_map/whiten_pack/pallas_call | solution.py:129
  18.2 11.6 %all-to-all-start = ((bf16[64,264,256]{2,1,0:T(8,128)(2,1)}), bf16[64,264,256]{2,1,0:T(8,128)(2,1)}, u32[]{:S(2)}, u32[]{:S(2)}) async-start(bf16[64,264,256]{2,1,0:T(8,128)(2,1)} %get-tuple-element.18), calls=%async_computation | async-start | bytes 17301504 | tf_op jit(solution)/shard_map/all_to_all | solution.py:351
  29.9 0.1 fusion.6
  30.0 40.8 %select_convert_fusion.table = bf16[768,3001]{1,0:T(8,128)(2,1)} fusion(s32[3001]{0:T(1024)S(1)} %iota_add_fusion, s32[768]{0:T(1024)S(1)} %fusion.6, pred[768]{0:T(1024)(128)(4,1)S(1)} %select_compare_fusion), kind=kLoop, calls=%fused_computation.3 | loop fusion | flops 27657216 | bytes 4625380 | tf_op jit(solution)/shard_map/convert_element_type | solution.py:336
  70.8 66.6 %all-to-all-done.got = bf16[64,264,256]{2,1,0:T(8,128)(2,1)} async-done(((bf16[64,264,256]{2,1,0:T(8,128)(2,1)}), bf16[64,264,256]{2,1,0:T(8,128)(2,1)}, u32[]{:S(2)}, u32[]{:S(2)}) %all-to-all-start) | async-done | bytes 8650784 | tf_op jit(solution)/shard_map/all_to_all | solution.py:351
  137.3 9.7 %all-to-all-start.1 = ((bf16[64,256,128]{2,1,0:T(8,128)(2,1)}), bf16[64,256,128]{2,1,0:T(8,128)(2,1)}, u32[]{:S(2)}, u32[]{:S(2)}) async-start(bf16[64,256,128]{2,1,0:T(8,128)(2,1)} %get-tuple-element.23), calls=%async_computation.1 | async-start | bytes 8388608 | tf_op jit(solution)/shard_map/all_to_all | solution.py:351
  147.1 29.0 %cross_sums_first.1 = (bf16[4,160,512]{2,1,0:T(8,128)(2,1)}, f32[4,160,512]{2,1,0:T(8,128)}, bf16[64,160,128]{2,1,0:T(8,128)(2,1)}, f32[160,128]{1,0:T(8,128)}) custom-call(bf16[64,264,256]{2,1,0:T(8,128)(2,1)} %all-to-all-done.got), custom_call_target="tpu_custom_call" | custom-call | flops 30000001024 | bytes 20000000 | tf_op jit(solution)/shard_map/cross_sums_first/pallas_call | solution.py:227
  176.1 1.0 collective-permute-start.1
  177.1 1.0 collective-permute-start
  178.1 23.1 %all-to-all-done.1.got = bf16[64,256,128]{2,1,0:T(8,128)(2,1)} async-done(((bf16[64,256,128]{2,1,0:T(8,128)(2,1)}), bf16[64,256,128]{2,1,0:T(8,128)(2,1)}, u32[]{:S(2)}, u32[]{:S(2)}) %all-to-all-start.1) | async-done | bytes 4194336 | tf_op jit(solution)/shard_map/all_to_all | solution.py:351
  201.2 0.0 collective-permute-done.1.count_from
  201.2 0.0 copy-start.2
  201.2 0.0 slice-start
  201.2 9.3 %cross_sums_second.3 = bf16[4,160,256]{2,1,0:T(8,128)(2,1)} custom-call(bf16[64,256,128]{2,1,0:T(8,128)(2,1)} %all-to-all-done.1.got, bf16[64,160,128]{2,1,0:T(8,128)(2,1)} %get-tuple-element.26.picks), custom_call_target="tpu_custom_call" | custom-call | flops 8000000000 | bytes 8000000 | tf_op jit(solution)/shard_map/cross_sums_second/pallas_call | solution.py:273
  210.5 0.0 slice-start.1
  210.5 0.0 copy-start
  210.5 0.0 copy-start.1
  210.5 1.1 collective-permute-start.2
  211.6 0.0 copy-done.2
  211.6 8.8 %cross_sums_second.2 = f32[4,160,256]{2,1,0:T(8,128)S(1)} custom-call(bf16[64,256,128]{2,1,0:T(8,128)(2,1)} %all-to-all-done.1.got, bf16[64,160,128]{2,1,0:T(8,128)(2,1)S(1)} %copy-done.2), custom_call_target="tpu_custom_call" | custom-call | flops 8000000000 | bytes 8000000 | tf_op jit(solution)/shard_map/cross_sums_second/pallas_call | solution.py:273
  220.4 0.0 collective-permute-done.2
  220.4 0.0 collective-permute-done
  220.4 0.0 slice-done
  220.4 0.0 slice-done.1
  220.4 0.0 copy-done
  220.4 0.0 copy-done.1
  220.4 6.3 %to_lags.1 = f32[640,3001]{1,0:T(8,128)} custom-call(f32[640,512]{1,0:T(8,128)S(1)} %bitcast.10, bf16[640,512]{1,0:T(8,128)(2,1)S(1)} %bitcast.11, f32[640,256]{1,0:T(8,128)S(1)} %bitcast.12, bf16[640,256]{1,0:T(8,128)(2,1)S(1)} %bitcast.13, bf16[768,3001]{1,0:T(8,128)(2,1)S(1)} %bitcast.9, f32[160,128]{1,0:T(8,128)S(1)} %copy-done.1, ...), custom_call_target="tpu_custom_call" | custom-call | flops 2950103040 | bytes 15365120 | tf_op jit(solution)/shard_map/to_lags/pallas_call | solution.py:310
  (3 shorter events, 0.0 us)
Async XLA Ops:
  18.2 119.1 %all-to-all-start = ((bf16[64,264,256]{2,1,0:T(8,128)(2,1)}), bf16[64,264,256]{2,1,0:T(8,128)(2,1)}, u32[]{:S(2)}, u32[]{:S(2)}) async-start(bf16[64,264,256]{2,1,0:T(8,128)(2,1)} %get-tuple-element.18), calls=%async_computation | async-start | bytes 17301504 | tf_op jit(solution)/shard_map/all_to_all | solution.py:351
  137.3 63.8 %all-to-all-start.1 = ((bf16[64,256,128]{2,1,0:T(8,128)(2,1)}), bf16[64,256,128]{2,1,0:T(8,128)(2,1)}, u32[]{:S(2)}, u32[]{:S(2)}) async-start(bf16[64,256,128]{2,1,0:T(8,128)(2,1)} %get-tuple-element.23), calls=%async_computation.1 | async-start | bytes 8388608 | tf_op jit(solution)/shard_map/all_to_all | solution.py:351
  176.1 25.1 %collective-permute-start.1 = (f32[160,128]{1,0:T(8,128)}, f32[160,128]{1,0:T(8,128)S(1)}, u32[]{:S(2)}, u32[]{:S(2)}) collective-permute-start(f32[160,128]{1,0:T(8,128)} %get-tuple-element.24.count), channel_id=1, source_target_pairs={{0,1},{1,0},{2,3},{3,2},{4,5},{5,4},{6,7},{7,6},{8,9},{9,8},{10,11... | collective-permute-start | bytes 245768 | tf_op jit(solution)/shard_map/ppermute | solution.py:340
  177.1 43.2 %collective-permute-start = (bf16[4,160,512]{2,1,0:T(8,128)(2,1)}, bf16[4,160,512]{2,1,0:T(8,128)(2,1)S(1)}, u32[]{:S(2)}, u32[]{:S(2)}) collective-permute-start(bf16[4,160,512]{2,1,0:T(8,128)(2,1)} %get-tuple-element.20), channel_id=1, source_target_pairs={{0,1},{1,0},{2,3},{3,2},{4,5},{5,4},{6,7},{7,6},{8,9},{9,8},{10,11... | collective-permute-start | bytes 1966088 | tf_op jit(solution)/shard_map/ppermute | solution.py:340
  201.2 10.4 %copy-start.2 = (bf16[64,160,128]{2,1,0:T(8,128)(2,1)S(1)}, bf16[64,160,128]{2,1,0:T(8,128)(2,1)}, u32[]{:S(2)}) copy-start(bf16[64,160,128]{2,1,0:T(8,128)(2,1)} %get-tuple-element.26.picks) | copy-start | bytes 7864324
  201.2 19.2 %slice-start = ((s8[4718592]{0:T(1024)(128)(4,1)}), s8[524288]{0:T(1024)(128)(4,1)S(1)}, s32[]{:S(2)}) async-start(s8[4718592]{0:T(1024)(128)(4,1)} %bitcast.8), calls=%async_computation.2 | async-start | bytes 1048576
  210.5 9.9 %slice-start.1 = ((s8[4718592]{0:T(1024)(128)(4,1)}), s8[4194304]{0:T(1024)(128)(4,1)S(1)}, s32[]{:S(2)}) async-start(s8[4718592]{0:T(1024)(128)(4,1)} %bitcast.8), calls=%async_computation.3 | async-start | bytes 8388608
  210.5 9.9 %copy-start = (f32[4,160,512]{2,1,0:T(8,128)S(1)}, f32[4,160,512]{2,1,0:T(8,128)}, u32[]{:S(2)}) copy-start(f32[4,160,512]{2,1,0:T(8,128)} %get-tuple-element.19) | copy-start | bytes 3932164
  210.5 9.9 %copy-start.1 = (f32[160,128]{1,0:T(8,128)S(1)}, f32[160,128]{1,0:T(8,128)}, u32[]{:S(2)}) copy-start(f32[160,128]{1,0:T(8,128)} %get-tuple-element.24.count) | copy-start | bytes 245764
  210.5 9.9 %collective-permute-start.2 = (bf16[4,160,256]{2,1,0:T(8,128)(2,1)}, bf16[4,160,256]{2,1,0:T(8,128)(2,1)S(1)}, u32[]{:S(2)}, u32[]{:S(2)}) collective-permute-start(bf16[4,160,256]{2,1,0:T(8,128)(2,1)} %cross_sums_second.3), channel_id=1, source_target_pairs={{0,1},{1,0},{2,3},{3,2},{4,5},{5,4},{6,7},{7,6},{8,9},{9,8},{10,11... | collective-permute-start | bytes 983048 | tf_op jit(solution)/shard_map/ppermute | solution.py:340

commit v8 on v7

--- a/solution.py
+++ b/solution.py
@@ -77,12 +77,18 @@
 
 
 def pack_kernel(tm_ref, mask_ref, *refs):
-    heads, (x0, x1, x2, send_a, send_b, slot_ref, key_ref, src_ref, flag_ref) = refs[:6], refs[6:]
+    heads, (x0, x1, x2, send_a, send_b, slot_ref, key_ref, src_ref, flag_ref, note_ref) = refs[:6], refs[6:]
     step = pl.program_id(0)
 
     @pl.when(step == 0)
     def _():
         source_kernel(tm_ref, mask_ref, *heads, src_ref, flag_ref)
+        flag_line = flag_ref[:1, :]
+        flag_line = jnp.concatenate([flag_line, flag_line], axis=1)
+        note_ref[...] = jnp.where(iota((8, BINS_A), 0) == 1, flag_line, 0.0)
+        late = src_ref[0, :SRC, BINS_A:].astype(jnp.float32)
+        note_ref[2:6, :BINS_B] = late[:SB]
+        note_ref[2:6, BINS_B:] = late[SB:]
         lines = [mask_ref[pl.ds(k, LINES // 5, stride=5), :] for k in range(5)]
         lines = jnp.concatenate(lines, axis=1).astype(jnp.float32)
         lane = iota((WIDE, 2 * WIDE), 1)
@@ -97,8 +103,6 @@
             slot_ref[m] = jnp.where(dot(flags, here_two) > 0.5, dot(flags, ahead_two) + part * CAP, -1.0)
             key_ref[m] = jnp.where(dot(flags, here) > 0.5, dot(flags, ahead), -1.0)
 
-    flag_line = flag_ref[:1, :]
-    flag_line = jnp.concatenate([flag_line, flag_line], axis=1)
     place = iota((2 * CAP, 2 * WIDE), 0).astype(jnp.float32).astype(jnp.bfloat16)
     for n in range(PACK):
         four = pl.ds(step * (PACK // 4) + n // 4, 1)
@@ -112,14 +116,15 @@
         factor = lax.rsqrt(energy + 1e-06)
         real = (real * factor).astype(jnp.bfloat16)
         imag = (imag * factor).astype(jnp.bfloat16)
-        for out, lo, hi in ((send_a, 0, BINS_A), (send_b, BINS_A, F)):
-            out[n, :CAP] = real[:, lo:hi]
-            out[n, CAP:SLOTS] = src_ref[0, :SRC, lo:hi]
-            out[n, SLOTS : SLOTS + CAP] = imag[:, lo:hi]
-            out[n, SLOTS + CAP : ROWS] = src_ref[0, SRC:, lo:hi]
-        line = iota((8, BINS_A), 0)
-        notes = jnp.where(line == 0, key_ref[n % 4, four, :], flag_line)
+        send_a[n, :CAP] = real[:, :BINS_A]
+        send_a[n, CAP:SLOTS] = src_ref[0, :SRC, :BINS_A]
+        send_a[n, SLOTS : SLOTS + CAP] = imag[:, :BINS_A]
+        send_a[n, SLOTS + CAP : ROWS] = src_ref[0, SRC:, :BINS_A]
+        notes = jnp.where(iota((8, BINS_A), 0) == 0, key_ref[n % 4, four, :], note_ref[...])
         send_a[n, ROWS:] = notes.astype(jnp.bfloat16)
+        send_b[n, :CAP] = real[:, BINS_A:]
+        send_b[n, CAP:SLOTS] = src_ref[0, SRC:, BINS_A:]
+        send_b[n, SLOTS:] = imag[:, BINS_A:]
 
 
 def pack(tm_index, mask, spectra):
@@ -138,17 +143,18 @@
         ],
         out_specs=[
             pl.BlockSpec((PACK, ROWS + 8, BINS_A), lambda b: (b, 0, 0)),
-            pl.BlockSpec((PACK, ROWS, BINS_B), lambda b: (b, 0, 0)),
+            pl.BlockSpec((PACK, SLOTS + CAP, BINS_B), lambda b: (b, 0, 0)),
         ],
         out_shape=[
             jax.ShapeDtypeStruct((BLOCKS, ROWS + 8, BINS_A), jnp.bfloat16),
-            jax.ShapeDtypeStruct((BLOCKS, ROWS, BINS_B), jnp.bfloat16),
+            jax.ShapeDtypeStruct((BLOCKS, SLOTS + CAP, BINS_B), jnp.bfloat16),
         ],
         scratch_shapes=[
             pltpu.VMEM((4, BLOCKS // 4, 2 * WIDE), jnp.float32),
             pltpu.VMEM((4, BLOCKS // 4, BINS_A), jnp.float32),
             pltpu.VMEM((1, 2 * SRC, F), jnp.bfloat16),
             pltpu.VMEM((8, 128), jnp.float32),
+            pltpu.VMEM((8, BINS_A), jnp.float32),
         ],
         cost_estimate=pl.CostEstimate(flops=2 * BLOCKS * ROWS * 2 * WIDE * F, bytes_accessed=30_000_000, transcendentals=0),
         compiler_params=pltpu.CompilerParams(vmem_limit_bytes=GRANT),
@@ -156,11 +162,10 @@
     )(tm_index, mask, *[spectra] * 9)
 
 
-def spread_slots(got, pick, held, src, win, bins):
-    rows = jnp.concatenate([got[win, :SLOTS, :], got[win, SLOTS:ROWS, :]], axis=1)
-    held[win] = dot(pick, rows)
-    real = rows[CAP:, :bins].astype(jnp.float32)
-    imag = rows[CAP:, bins:].astype(jnp.float32)
+def spread_slots(real, imag, src_real, src_imag, pick, held, src, win, bins):
+    held[win] = dot(pick, jnp.concatenate([real, imag], axis=1))
+    real = src_real.astype(jnp.float32)
+    imag = src_imag.astype(jnp.float32)
     for k, rows in enumerate((real, imag, real + imag)):
         for t in range(bins // 128):
             src[win, t, k * SRC : (k + 1) * SRC] = rows[:, t * 128 : (t + 1) * 128]
@@ -197,7 +202,7 @@
     out[q, :, bins:] = (r - p + m).astype(out.dtype)
 
 
-def first_kernel(got, theirs, mine, picks, count, held, src, total):
+def first_kernel(got, theirs, mine, picks, count, late, held, src, total):
     step = pl.program_id(0)
 
     @pl.when(step == 0)
@@ -211,7 +216,10 @@
         pick = one_hot(iota((WIDE, SLOTS), 1) == key.astype(jnp.int32))
         picks[win] = pick
         count[...] += jnp.where(key > -0.5, 1.0, 0.0) * notes[1:2, :128]
-        spread_slots(got, pick, held, src, win, BINS_A)
+        late[win, :SB] = notes[2:6, :BINS_B]
+        late[win, SB:] = notes[2:6, BINS_B:]
+        src_real, src_imag = got[win, CAP:SLOTS, :], got[win, SLOTS + CAP : ROWS, :]
+        spread_slots(got[win, :SLOTS, :], got[win, SLOTS:ROWS, :], src_real, src_imag, pick, held, src, win, BINS_A)
     correlate(held, src, total, range(SRC), BINS_A, STEP_A)
 
     @pl.when(step == pl.num_programs(0) - 1)
@@ -233,12 +241,14 @@
             sums_spec,
             pl.BlockSpec((STEP_A, WIDE, SLOTS), lambda g: (g, 0, 0)),
             pl.BlockSpec((WIDE, 128), lambda g: (0, 0)),
+            pl.BlockSpec((STEP_A, SRC, BINS_B), lambda g: (g, 0, 0)),
         ],
         out_shape=[
             jax.ShapeDtypeStruct(shape, jnp.bfloat16),
             jax.ShapeDtypeStruct(shape, jnp.float32),
             jax.ShapeDtypeStruct((WINS, WIDE, SLOTS), jnp.bfloat16),
             jax.ShapeDtypeStruct((WIDE, 128), jnp.float32),
+            jax.ShapeDtypeStruct((WINS, SRC, BINS_B), jnp.float32),
         ],
         scratch_shapes=[
             pltpu.VMEM((STEP_A, WIDE, 2 * BINS_A), jnp.float32),
@@ -251,7 +261,7 @@
     )(got)
 
 
-def second_kernel(first, got, picks, out, held, src, total):
+def second_kernel(first, got, late, picks, out, held, src, total):
     step = pl.program_id(0)
 
     @pl.when(step == 0)
@@ -259,7 +269,8 @@
         total[...] = jnp.zeros_like(total)
 
     for win in range(STEP_B):
-        spread_slots(got, picks[win], held, src, win, BINS_B)
+        pick = picks[win, :, :CAP]
+        spread_slots(got[win, :CAP, :], got[win, SLOTS:, :], late[win], got[win, CAP:SLOTS, :], pick, held, src, win, BINS_B)
     correlate(held, src, total, range(first, first + SB), BINS_B, STEP_B)
 
     @pl.when(step == pl.num_programs(0) - 1)
@@ -268,13 +279,14 @@
             store_sums(total, q, out, q, BINS_B)
 
 
-def second_sums(got, picks, first, dtype, grant):
+def second_sums(got, late, picks, first, dtype, grant):
     shape = (SB, WIDE, 2 * BINS_B)
     return pl.pallas_call(
         functools.partial(second_kernel, first),
         grid=(WINS // STEP_B,),
         in_specs=[
-            pl.BlockSpec((STEP_B, ROWS, BINS_B), lambda g: (g, 0, 0)),
+            pl.BlockSpec((STEP_B, SLOTS + CAP, BINS_B), lambda g: (g, 0, 0)),
+            pl.BlockSpec((STEP_B, SRC, BINS_B), lambda g: (g, 0, 0)),
             pl.BlockSpec((STEP_B, WIDE, SLOTS), lambda g: (g, 0, 0)),
         ],
         out_specs=pl.BlockSpec(shape, lambda g: (0, 0, 0)),
@@ -287,7 +299,7 @@
         cost_estimate=pl.CostEstimate(flops=8_000_000_000, bytes_accessed=8_000_000, transcendentals=0),
         compiler_params=pltpu.CompilerParams(vmem_limit_bytes=grant),
         name="cross_sums_second",
-    )(got, picks)
+    )(got, late, picks)
 
 
 def lags_kernel(mine_a, from_a, mine_b, from_b, table, count, count_from, out, held, scale):
@@ -351,13 +363,13 @@
     exchange = lambda x: lax.all_to_all(x, "chan", split_axis=0, concat_axis=0, tiled=True)
     got_a = exchange(send_a)
     got_b = exchange(send_b)
-    theirs_a, mine_a, picks, count = first_sums(got_a)
+    theirs_a, mine_a, picks, count, late = first_sums(got_a)
     from_a = swap(theirs_a)
     count_from = swap(count)
     got_b, count_from = lax.optimization_barrier((got_b, count_from))
-    theirs_b = second_sums(got_b, picks, 0, jnp.bfloat16, GRANT)
+    theirs_b = second_sums(got_b, late, picks, 0, jnp.bfloat16, GRANT)
     from_b = swap(theirs_b)
-    mine_b = second_sums(got_b, picks, SB, jnp.float32, GRANT // 2)
+    mine_b = second_sums(got_b, late, picks, SB, jnp.float32, GRANT // 2)
     lagged = to_lags(mine_a, from_a, mine_b, from_b, table, count, count_from)
     return lagged.reshape(SB, WIDE, LAGS)
 

time: 227 us -> 226 us (level)
  no operation moved by 1% of the time
where the time goes in v8:
time: 226 us; the launch traced here: 225 us
  waiting for transfers between devices  88 us (39%)
  Pallas kernels  71.6 us (32%)
  other arithmetic  40.9 us (18%)
  starting transfers between devices  24.4 us (11%)
    all_to_all x2, waiting for transfers between devices, local(): lax.all_to_all(x, 'chan', split_axis=0, concat_axis=0, tiled=True)  88 us
    convert_element_type x1, other arithmetic, lag_table(): return table.astype(jnp.bfloat16)  40.8 us
    pallas_call x1, Pallas kernels, first_sums(): pl.pallas_call(first_kernel, grid=(WINS // STEP_A,), in_specs=[pl.BlockSp...  29 us
    all_to_all x2, starting transfers between devices, local(): lax.all_to_all(x, 'chan', split_axis=0, concat_axis=0, tiled=True)  21.2 us
    pallas_call x1, Pallas kernels, pack(): pl.pallas_call(pack_kernel, grid=(BLOCKS // PACK,), in_specs=[pl.BlockSpe...  18.3 us
    pallas_call x2, Pallas kernels, second_sums(): pl.pallas_call(functools.partial(second_kernel, first), grid=(WINS // STE...  18.1 us
    pallas_call x1, Pallas kernels, to_lags(): pl.pallas_call(lags_kernel, grid=(pl.cdiv(LAGS, LAG_TILE),), in_specs=[*s...  6.27 us
  transfers between devices with their start and end apart: 5, of which 2 were waited for; matrix products, arithmetic and copies ran while one was open for 18% of the time, Pallas kernels for 21%

profile of v8, /device:TPU:0, one launch (start us, length us, event | category | flops | bytes accessed | tf_op | source)
XLA Modules:
  0.0 225.2 jit_solution(3846327409971601975)
XLA Ops:
  0.0 18.3 %whiten_pack.1 = (bf16[64,264,256]{2,1,0:T(8,128)(2,1)}, bf16[64,248,128]{2,1,0:T(8,128)(2,1)}) custom-call(s32[1]{0:T(128)} %bitcast.tm_ref, s32[80,128]{1,0:T(8,128)} %bitcast.23, bf16[10240,2,384]{2,1,0:T(2,128)(2,1)} %bitcast.14, bf16[10240,2,384]{2,1,0:T(2,128)(2,1)} %bitcast.15, bf16[10240,2,384]{2,1,0:T(2,128)(2,1)} %bitcast.16, ...), custom_call_target="tpu_custom_call" | custom-call | flops 4026531840 | bytes 30000000 | tf_op jit(solution)/shard_map/whiten_pack/pallas_call | solution.py:134
  18.3 11.6 %all-to-all-start = ((bf16[64,264,256]{2,1,0:T(8,128)(2,1)}), bf16[64,264,256]{2,1,0:T(8,128)(2,1)}, u32[]{:S(2)}, u32[]{:S(2)}) async-start(bf16[64,264,256]{2,1,0:T(8,128)(2,1)} %get-tuple-element.19), calls=%async_computation | async-start | bytes 17301504 | tf_op jit(solution)/shard_map/all_to_all | solution.py:363
  29.9 0.1 fusion.6
  30.0 40.8 %select_convert_fusion.table = bf16[768,3001]{1,0:T(8,128)(2,1)} fusion(s32[3001]{0:T(1024)S(1)} %iota_add_fusion, s32[768]{0:T(1024)S(1)} %fusion.6, pred[768]{0:T(1024)(128)(4,1)S(1)} %select_compare_fusion), kind=kLoop, calls=%fused_computation.3 | loop fusion | flops 27657216 | bytes 4625380 | tf_op jit(solution)/shard_map/convert_element_type | solution.py:348
  70.8 66.6 %all-to-all-done.got = bf16[64,264,256]{2,1,0:T(8,128)(2,1)} async-done(((bf16[64,264,256]{2,1,0:T(8,128)(2,1)}), bf16[64,264,256]{2,1,0:T(8,128)(2,1)}, u32[]{:S(2)}, u32[]{:S(2)}) %all-to-all-start) | async-done | bytes 8650784 | tf_op jit(solution)/shard_map/all_to_all | solution.py:363
  137.4 9.7 %all-to-all-start.1 = ((bf16[64,248,128]{2,1,0:T(8,128)(2,1)}), bf16[64,248,128]{2,1,0:T(8,128)(2,1)}, u32[]{:S(2)}, u32[]{:S(2)}) async-start(bf16[64,248,128]{2,1,0:T(8,128)(2,1)} %get-tuple-element.24), calls=%async_computation.1 | async-start | bytes 8126464 | tf_op jit(solution)/shard_map/all_to_all | solution.py:363
  147.0 29.0 %cross_sums_first.1 = (bf16[4,160,512]{2,1,0:T(8,128)(2,1)}, f32[4,160,512]{2,1,0:T(8,128)}, bf16[64,160,128]{2,1,0:T(8,128)(2,1)}, f32[160,128]{1,0:T(8,128)}, f32[64,8,128]{2,1,0:T(8,128)}) custom-call(bf16[64,264,256]{2,1,0:T(8,128)(2,1)} %all-to-all-done.got), custom_call_target="tpu_custom_call" | custom-call | flops 30000001024 | bytes 20000000 | tf_op jit(solution)/shard_map/cross_sums_first/pallas_call | solution.py:235
  176.0 1.1 collective-permute-start.1
  177.1 1.0 collective-permute-start
  178.1 21.5 %all-to-all-done.1.got = bf16[64,248,128]{2,1,0:T(8,128)(2,1)} async-done(((bf16[64,248,128]{2,1,0:T(8,128)(2,1)}), bf16[64,248,128]{2,1,0:T(8,128)(2,1)}, u32[]{:S(2)}, u32[]{:S(2)}) %all-to-all-start.1) | async-done | bytes 4063264 | tf_op jit(solution)/shard_map/all_to_all | solution.py:363
  199.6 0.0 collective-permute-done.1.count_from
  199.6 0.0 copy-start.2
  199.6 0.0 copy-start.3
  199.6 0.0 slice-start
  199.6 9.3 %cross_sums_second.3 = bf16[4,160,256]{2,1,0:T(8,128)(2,1)} custom-call(bf16[64,248,128]{2,1,0:T(8,128)(2,1)} %all-to-all-done.1.got, f32[64,8,128]{2,1,0:T(8,128)} %get-tuple-element.27.late, bf16[64,160,128]{2,1,0:T(8,128)(2,1)} %get-tuple-element.28.picks), custom_call_target="tpu_custom_call" | custom-call | flops 8000000000 | bytes 8000000 | tf_op jit(solution)/shard_map/cross_sums_second/pallas_call | solution.py:284
  209.0 0.0 slice-start.1
  209.0 0.0 copy-start
  209.0 0.0 copy-start.1
  209.0 1.1 collective-permute-start.2
  210.1 0.0 copy-done.2
  210.1 0.0 copy-done.3
  210.1 8.7 %cross_sums_second.2 = f32[4,160,256]{2,1,0:T(8,128)S(1)} custom-call(bf16[64,248,128]{2,1,0:T(8,128)(2,1)} %all-to-all-done.1.got, f32[64,8,128]{2,1,0:T(8,128)S(1)} %copy-done.3, bf16[64,160,128]{2,1,0:T(8,128)(2,1)S(1)} %copy-done.2), custom_call_target="tpu_custom_call" | custom-call | flops 8000000000 | bytes 8000000 | tf_op jit(solution)/shard_map/cross_sums_second/pallas_call | solution.py:284
  218.8 0.0 collective-permute-done.2
  218.9 0.0 collective-permute-done
  218.9 0.0 slice-done
  218.9 0.0 slice-done.1
  218.9 0.0 copy-done
  218.9 0.0 copy-done.1
  218.9 6.3 %to_lags.1 = f32[640,3001]{1,0:T(8,128)} custom-call(f32[640,512]{1,0:T(8,128)S(1)} %bitcast.10, bf16[640,512]{1,0:T(8,128)(2,1)S(1)} %bitcast.11, f32[640,256]{1,0:T(8,128)S(1)} %bitcast.12, bf16[640,256]{1,0:T(8,128)(2,1)S(1)} %bitcast.13, bf16[768,3001]{1,0:T(8,128)(2,1)S(1)} %bitcast.9, f32[160,128]{1,0:T(8,128)S(1)} %copy-done.1, ...), custom_call_target="tpu_custom_call" | custom-call | flops 2950103040 | bytes 15365120 | tf_op jit(solution)/shard_map/to_lags/pallas_call | solution.py:322
  (3 shorter events, 0.0 us)
Async XLA Ops:
  18.3 119.1 %all-to-all-start = ((bf16[64,264,256]{2,1,0:T(8,128)(2,1)}), bf16[64,264,256]{2,1,0:T(8,128)(2,1)}, u32[]{:S(2)}, u32[]{:S(2)}) async-start(bf16[64,264,256]{2,1,0:T(8,128)(2,1)} %get-tuple-element.19), calls=%async_computation | async-start | bytes 17301504 | tf_op jit(solution)/shard_map/all_to_all | solution.py:363
  137.4 62.2 %all-to-all-start.1 = ((bf16[64,248,128]{2,1,0:T(8,128)(2,1)}), bf16[64,248,128]{2,1,0:T(8,128)(2,1)}, u32[]{:S(2)}, u32[]{:S(2)}) async-start(bf16[64,248,128]{2,1,0:T(8,128)(2,1)} %get-tuple-element.24), calls=%async_computation.1 | async-start | bytes 8126464 | tf_op jit(solution)/shard_map/all_to_all | solution.py:363
  176.0 23.6 %collective-permute-start.1 = (f32[160,128]{1,0:T(8,128)}, f32[160,128]{1,0:T(8,128)S(1)}, u32[]{:S(2)}, u32[]{:S(2)}) collective-permute-start(f32[160,128]{1,0:T(8,128)} %get-tuple-element.25.count), channel_id=1, source_target_pairs={{0,1},{1,0},{2,3},{3,2},{4,5},{5,4},{6,7},{7,6},{8,9},{9,8},{10,11... | collective-permute-start | bytes 245768 | tf_op jit(solution)/shard_map/ppermute | solution.py:352
  177.1 41.7 %collective-permute-start = (bf16[4,160,512]{2,1,0:T(8,128)(2,1)}, bf16[4,160,512]{2,1,0:T(8,128)(2,1)S(1)}, u32[]{:S(2)}, u32[]{:S(2)}) collective-permute-start(bf16[4,160,512]{2,1,0:T(8,128)(2,1)} %get-tuple-element.21), channel_id=1, source_target_pairs={{0,1},{1,0},{2,3},{3,2},{4,5},{5,4},{6,7},{7,6},{8,9},{9,8},{10,11... | collective-permute-start | bytes 1966088 | tf_op jit(solution)/shard_map/ppermute | solution.py:352
  199.6 10.5 %copy-start.2 = (bf16[64,160,128]{2,1,0:T(8,128)(2,1)S(1)}, bf16[64,160,128]{2,1,0:T(8,128)(2,1)}, u32[]{:S(2)}) copy-start(bf16[64,160,128]{2,1,0:T(8,128)(2,1)} %get-tuple-element.28.picks) | copy-start | bytes 7864324
  199.6 10.5 %copy-start.3 = (f32[64,8,128]{2,1,0:T(8,128)S(1)}, f32[64,8,128]{2,1,0:T(8,128)}, u32[]{:S(2)}) copy-start(f32[64,8,128]{2,1,0:T(8,128)} %get-tuple-element.27.late) | copy-start | bytes 786436
  199.6 19.3 %slice-start = ((s8[4718592]{0:T(1024)(128)(4,1)}), s8[524288]{0:T(1024)(128)(4,1)S(1)}, s32[]{:S(2)}) async-start(s8[4718592]{0:T(1024)(128)(4,1)} %bitcast.8), calls=%async_computation.2 | async-start | bytes 1048576
  209.0 9.9 %slice-start.1 = ((s8[4718592]{0:T(1024)(128)(4,1)}), s8[4194304]{0:T(1024)(128)(4,1)S(1)}, s32[]{:S(2)}) async-start(s8[4718592]{0:T(1024)(128)(4,1)} %bitcast.8), calls=%async_computation.3 | async-start | bytes 8388608
  209.0 9.9 %copy-start = (f32[4,160,512]{2,1,0:T(8,128)S(1)}, f32[4,160,512]{2,1,0:T(8,128)}, u32[]{:S(2)}) copy-start(f32[4,160,512]{2,1,0:T(8,128)} %get-tuple-element.20) | copy-start | bytes 3932164
  209.0 9.9 %copy-start.1 = (f32[160,128]{1,0:T(8,128)S(1)}, f32[160,128]{1,0:T(8,128)}, u32[]{:S(2)}) copy-start(f32[160,128]{1,0:T(8,128)} %get-tuple-element.25.count) | copy-start | bytes 245764
  209.0 9.9 %collective-permute-start.2 = (bf16[4,160,256]{2,1,0:T(8,128)(2,1)}, bf16[4,160,256]{2,1,0:T(8,128)(2,1)S(1)}, u32[]{:S(2)}, u32[]{:S(2)}) collective-permute-start(bf16[4,160,256]{2,1,0:T(8,128)(2,1)} %cross_sums_second.3), channel_id=1, source_target_pairs={{0,1},{1,0},{2,3},{3,2},{4,5},{5,4},{6,7},{7,6},{8,9},{9,8},{10,11... | collective-permute-start | bytes 983048 | tf_op jit(solution)/shard_map/ppermute | solution.py:352
